TPU v7x, 32 devices: a whole 2x2x4 slice. The times are simulated.
32 devices in a mesh: rep: 2 (over y), fsdp: 4 (over z), seq: 4 (over x, core).
Axes of the slice: x: 2, y: 2, z: 4, core: 2. Of those that a mesh axis runs over, the one named last changes fastest.
Arguments:
- latents: bfloat16 [8, 1024, 1152], P(('rep', 'fsdp'), 'seq'), may hold values from -6 to 6
- cond: bfloat16 [8, 1152], P(('rep', 'fsdp')), may hold values from -6 to 6
- w_ada: bfloat16 [1152, 6912], P(('fsdp', 'seq')), may hold values from -0.25 to 0.25
- b_ada: bfloat16 [6912], P(('fsdp', 'seq')), may hold values from -3 to 3
- w_qkv: bfloat16 [1152, 3456], P(('fsdp', 'seq')), may hold values from -0.1875 to 0.1875
- b_qv: bfloat16 [2304], P(('fsdp', 'seq')), may hold values from -3 to 3
- w_out: bfloat16 [1152, 1152], P(('fsdp', 'seq')), may hold values from -1.5 to 1.5
- b_out: bfloat16 [1152], P(('fsdp', 'seq')), may hold values from -3 to 3
- w_one: bfloat16 [1152, 4608], P(('fsdp', 'seq')), may hold values from -0.1875 to 0.1875
- b_one: bfloat16 [4608], P(('fsdp', 'seq')), may hold values from -3 to 3
- w_two: bfloat16 [4608, 1152], P(('fsdp', 'seq')), may hold values from -0.09375 to 0.09375
- b_two: bfloat16 [1152], P(('fsdp', 'seq')), may hold values from -3 to 3
- cotangent: bfloat16 [8, 1024, 1152], P(('rep', 'fsdp'), 'seq'), may hold values from -6 to 6
Outputs:
- block_out: bfloat16 [8, 1024, 1152], P(('rep', 'fsdp'), 'seq')
- grad_latents: float32 [8, 1024, 1152], P(('rep', 'fsdp'), 'seq')
- grad_cond: float32 [8, 1152], P(('rep', 'fsdp'))
- grad_w_ada: float32 [1152, 6912], P(('fsdp', 'seq'))
- grad_b_ada: float32 [6912], P(('fsdp', 'seq'))
- grad_w_qkv: float32 [1152, 3456], P(('fsdp', 'seq'))
- grad_b_qv: float32 [2304], P(('fsdp', 'seq'))
- grad_w_out: float32 [1152, 1152], P(('fsdp', 'seq'))
- grad_b_out: float32 [1152], P(('fsdp', 'seq'))
- grad_w_one: float32 [1152, 4608], P(('fsdp', 'seq'))
- grad_b_one: float32 [4608], P(('fsdp', 'seq'))
- grad_w_two: float32 [4608, 1152], P(('fsdp', 'seq'))
- grad_b_two: float32 [1152], P(('fsdp', 'seq'))
All inputs are finite; a program needn't handle non-finite values.
Results may differ from a plain program's by a relative error of at most 0.014.
The roundings to bfloat16 on the way count: a program that leaves them out, or rounds other values in their place, can miss the bound.
Values may be sent and summed in bfloat16 or wider, within the bound.
A program may use at most 448 MiB of HBM per device.

v0:
```python
import math

import jax
import jax.numpy as jnp
from jax import lax
from jax.sharding import PartitionSpec as P

H = 16


epsilon = 1e-06
gelu_coef = math.sqrt(2.0 / math.pi)


def norm_stats(values):
    center = values - jnp.mean(values, axis=-1, keepdims=True)
    inv_std = lax.rsqrt(jnp.mean(center * center, axis=-1, keepdims=True) + epsilon)
    return (center * inv_std, inv_std)


def norm_back(grad, normed, inv_std):
    return inv_std * (
        grad
        - jnp.mean(grad, axis=-1, keepdims=True)
        - normed * jnp.mean(grad * normed, axis=-1, keepdims=True)
    )


def gelu_tanh(values):
    inner = gelu_coef * (values + 0.044715 * values * values * values)
    return 0.5 * values * (1.0 + jnp.tanh(inner))


def gelu_slope(values):
    inner = gelu_coef * (values + 0.044715 * values * values * values)
    tanh_val = jnp.tanh(inner)
    return 0.5 * (1.0 + tanh_val) + 0.5 * values * (1.0 - tanh_val * tanh_val) * gelu_coef * (
        1.0 + 3.0 * 0.044715 * values * values
    )


def row_dot(left, right):
    return jnp.dot(left, right, preferred_element_type=jnp.float32)


def back_dot(grad, weight):
    return lax.dot_general(
        grad, weight, (((1,), (1,)), ((), ())), preferred_element_type=jnp.float32
    )


def outer_dot(left, grad):
    return lax.dot_general(left, grad, (((0,), (0,)), ((), ())), preferred_element_type=jnp.float32)


def pack_rows(arrays, groups):
    return jnp.concatenate([array.reshape(groups, -1) for array in arrays], axis=1).reshape(-1)


def unpack_rows(flat, layouts, groups):
    pieces = []
    offset = 0
    for layout in layouts:
        amount = math.prod(layout) // groups
        piece = flat[offset : offset + amount].reshape((layout[0] // groups,) + tuple(layout[1:]))
        pieces.append(piece)
        offset = offset + amount
    return pieces


def split_blocks(array, block_len):
    shape = array.shape
    return jnp.moveaxis(
        array.reshape(shape[:2] + (shape[2] // block_len, block_len) + shape[3:]), 2, 0
    )


def join_blocks(array):
    moved = jnp.moveaxis(array, 0, 2)
    shape = moved.shape
    return moved.reshape(shape[:2] + (shape[2] * shape[3],) + shape[4:])


def attention_forward(queries, key_rows, val_rows):
    length = queries.shape[2]
    head_size = queries.shape[3]
    block_len = min(512, length)
    score_scale = head_size ** (-0.5)

    def one_block(query_block):
        scores = (
            jnp.einsum("bhqd,bhkd->bhqk", query_block, key_rows, preferred_element_type=jnp.float32)
            * score_scale
        )
        highest = jnp.max(scores, axis=-1, keepdims=True)
        raised = jnp.exp(scores - highest)
        summed = jnp.sum(raised, axis=-1, keepdims=True)
        probs_low = (raised / summed).astype(jnp.bfloat16)
        result = jnp.einsum(
            "bhqk,bhkd->bhqd", probs_low, val_rows, preferred_element_type=jnp.float32
        )
        return (result.astype(jnp.bfloat16), (highest + jnp.log(summed))[..., 0])

    outputs, log_totals = lax.map(one_block, split_blocks(queries, block_len))
    return (join_blocks(outputs), join_blocks(log_totals))


def attention_backward(queries, key_rows, val_rows, log_totals, grad_out):
    length = queries.shape[2]
    head_size = queries.shape[3]
    block_len = min(512, length)
    score_scale = head_size ** (-0.5)

    def one_block(carried, pieces):
        grad_keys, grad_vals = carried
        query_block, grad_block, lse_block = pieces
        scores = (
            jnp.einsum("bhqd,bhkd->bhqk", query_block, key_rows, preferred_element_type=jnp.float32)
            * score_scale
        )
        attn_probs = jnp.exp(scores - lse_block[..., None])
        grad_probs = jnp.einsum(
            "bhqd,bhkd->bhqk", grad_block, val_rows, preferred_element_type=jnp.float32
        )
        row_inner = jnp.sum(attn_probs * grad_probs, axis=-1, keepdims=True)
        grad_scores = (attn_probs * (grad_probs - row_inner)).astype(jnp.bfloat16)
        grad_query = (
            jnp.einsum("bhqk,bhkd->bhqd", grad_scores, key_rows, preferred_element_type=jnp.float32)
            * score_scale
        )
        grad_keys = (
            grad_keys
            + jnp.einsum(
                "bhqk,bhqd->bhkd", grad_scores, query_block, preferred_element_type=jnp.float32
            )
            * score_scale
        )
        grad_vals = grad_vals + jnp.einsum(
            "bhqk,bhqd->bhkd",
            attn_probs.astype(jnp.bfloat16),
            grad_block,
            preferred_element_type=jnp.float32,
        )
        return ((grad_keys, grad_vals), grad_query)

    zeros_start = jnp.zeros(key_rows.shape, jnp.float32)
    pieces = (
        split_blocks(queries, block_len),
        split_blocks(grad_out, block_len),
        split_blocks(log_totals, block_len),
    )
    (grad_keys, grad_vals), grad_queries = lax.scan(one_block, (zeros_start, zeros_start), pieces)
    return (join_blocks(grad_queries), grad_keys, grad_vals)


def on_device(
    latents, cond, w_ada, b_ada, w_qkv, b_qv, w_out, b_out, w_one, b_one, w_two, b_two, cotangent
):
    latent_count, local_len, width = latents.shape
    token_rows = latent_count * local_len
    head_count = H
    head_size = width // head_count
    seq_count = lax.axis_size("seq")
    group_size = lax.axis_size(("fsdp", "seq"))
    local_heads = head_count // seq_count
    full_len = local_len * seq_count
    owner = lax.axis_index(("fsdp", "seq"))
    own_rows = w_ada.shape[0]
    bias_cols = b_ada.shape[0]
    first_latent = lax.axis_index(("rep", "fsdp")) * latent_count
    cond_float = cond.astype(jnp.float32)
    cond_sigmoid = jax.nn.sigmoid(cond_float)
    silu_cond = (cond_float * cond_sigmoid).astype(jnp.bfloat16)
    silu_every = lax.all_gather(silu_cond, ("rep", "fsdp"), axis=0, tiled=True)
    silu_owned = lax.dynamic_slice_in_dim(silu_every, owner * own_rows, own_rows, 1)
    ada_part = row_dot(silu_owned, w_ada)
    bias_slot = (
        lax.dynamic_slice_in_dim(ada_part, owner * bias_cols, bias_cols, 1)
        + b_ada.astype(jnp.float32)[None, :]
    )
    ada_part = lax.dynamic_update_slice_in_dim(ada_part, bias_slot, owner * bias_cols, 1)
    modulation_every = lax.psum(ada_part, ("fsdp", "seq"))
    modulation = lax.dynamic_slice_in_dim(modulation_every, first_latent, latent_count, 0)
    shift_one, scale_one, gate_one, shift_two, scale_two, gate_two = jnp.split(
        modulation[:, None, :], 6, axis=2
    )
    full_fwd = (
        lax.all_gather(w_qkv, ("fsdp", "seq"), axis=0, tiled=True),
        lax.all_gather(b_qv, ("fsdp", "seq"), axis=0, tiled=True),
        lax.all_gather(w_out, ("fsdp", "seq"), axis=0, tiled=True),
        lax.all_gather(b_out, ("fsdp", "seq"), axis=0, tiled=True),
        lax.all_gather(w_one, ("fsdp", "seq"), axis=0, tiled=True),
        lax.all_gather(b_one, ("fsdp", "seq"), axis=0, tiled=True),
        lax.all_gather(w_two, ("fsdp", "seq"), axis=0, tiled=True),
        lax.all_gather(b_two, ("fsdp", "seq"), axis=0, tiled=True),
    )
    qkv_full, qv_bias, out_full, out_bias, one_full, one_bias, two_full, two_bias = full_fwd
    inputs = latents.astype(jnp.float32)
    normed_one, inv_one = norm_stats(inputs)
    mixed_one = (
        (normed_one * (1.0 + scale_one) + shift_one).astype(jnp.bfloat16).reshape(token_rows, width)
    )
    bias_full = jnp.concatenate(
        [qv_bias[:width], jnp.zeros((width,), jnp.bfloat16), qv_bias[width:]]
    ).astype(jnp.float32)
    projected = (row_dot(mixed_one, qkv_full) + bias_full).astype(jnp.bfloat16)
    token_heads = projected.reshape(latent_count, local_len, 3, head_count, head_size).transpose(
        2, 0, 3, 1, 4
    )
    token_heads = token_heads.reshape(3, latent_count, head_count, local_len * head_size)
    head_tokens = lax.all_to_all(token_heads, "seq", split_axis=2, concat_axis=3, tiled=True)
    head_tokens = head_tokens.reshape(3, latent_count, local_heads, full_len, head_size)
    queries = head_tokens[0]
    key_rows = head_tokens[1]
    val_rows = head_tokens[2]
    attended, log_totals = attention_forward(queries, key_rows, val_rows)
    back_tokens = lax.all_to_all(
        attended.reshape(latent_count, local_heads, full_len * head_size),
        "seq",
        split_axis=2,
        concat_axis=1,
        tiled=True,
    )
    merged = (
        back_tokens.reshape(latent_count, head_count, local_len, head_size)
        .transpose(0, 2, 1, 3)
        .reshape(token_rows, width)
    )
    branch_one = (row_dot(merged, out_full) + out_bias.astype(jnp.float32)).reshape(
        latent_count, local_len, width
    )
    residual = inputs + gate_one * branch_one
    normed_two, inv_two = norm_stats(residual)
    mixed_two = (
        (normed_two * (1.0 + scale_two) + shift_two).astype(jnp.bfloat16).reshape(token_rows, width)
    )
    hidden_pre = row_dot(mixed_two, one_full) + one_bias.astype(jnp.float32)
    hidden_act = gelu_tanh(hidden_pre).astype(jnp.bfloat16)
    branch_two = (row_dot(hidden_act, two_full) + two_bias.astype(jnp.float32)).reshape(
        latent_count, local_len, width
    )
    block_out = (residual + gate_two * branch_two).astype(jnp.bfloat16)
    full_back = (
        lax.all_gather(w_qkv, ("fsdp", "seq"), axis=0, tiled=True),
        lax.all_gather(b_qv, ("fsdp", "seq"), axis=0, tiled=True),
        lax.all_gather(w_out, ("fsdp", "seq"), axis=0, tiled=True),
        lax.all_gather(b_out, ("fsdp", "seq"), axis=0, tiled=True),
        lax.all_gather(w_one, ("fsdp", "seq"), axis=0, tiled=True),
        lax.all_gather(b_one, ("fsdp", "seq"), axis=0, tiled=True),
        lax.all_gather(w_two, ("fsdp", "seq"), axis=0, tiled=True),
        lax.all_gather(b_two, ("fsdp", "seq"), axis=0, tiled=True),
    )
    qkv_back = full_back[0]
    out_back = full_back[2]
    one_back = full_back[4]
    two_back = full_back[6]
    grad_out = cotangent.astype(jnp.float32)
    grad_two = (gate_two * grad_out).astype(jnp.bfloat16).reshape(token_rows, width)
    gate_two_grad = jnp.sum(grad_out * branch_two, axis=1)
    two_w_grad = outer_dot(hidden_act, grad_two)
    two_b_grad = jnp.sum(grad_two, axis=0, dtype=jnp.float32)
    grad_pre = (back_dot(grad_two, two_back) * gelu_slope(hidden_pre)).astype(jnp.bfloat16)
    one_w_grad = outer_dot(mixed_two, grad_pre)
    one_b_grad = jnp.sum(grad_pre, axis=0, dtype=jnp.float32)
    grad_mixed_two = back_dot(grad_pre, one_back).reshape(latent_count, local_len, width)
    shift_two_grad = jnp.sum(grad_mixed_two, axis=1)
    scale_two_grad = jnp.sum(grad_mixed_two * normed_two, axis=1)
    grad_resid = grad_out + norm_back(grad_mixed_two * (1.0 + scale_two), normed_two, inv_two)
    mlp_layouts = (one_w_grad.shape, one_b_grad.shape, two_w_grad.shape, two_b_grad.shape)
    mlp_flat = lax.psum_scatter(
        pack_rows((one_w_grad, one_b_grad, two_w_grad, two_b_grad), group_size),
        ("fsdp", "seq"),
        scatter_dimension=0,
        tiled=True,
    )
    grad_branch = (gate_one * grad_resid).astype(jnp.bfloat16).reshape(token_rows, width)
    gate_one_grad = jnp.sum(grad_resid * branch_one, axis=1)
    out_w_grad = outer_dot(merged, grad_branch)
    out_b_grad = jnp.sum(grad_branch, axis=0, dtype=jnp.float32)
    grad_merged = back_dot(grad_branch, out_back).astype(jnp.bfloat16)
    grad_heads = grad_merged.reshape(latent_count, local_len, head_count, head_size).transpose(
        0, 2, 1, 3
    )
    grad_heads = grad_heads.reshape(latent_count, head_count, local_len * head_size)
    grad_heads = lax.all_to_all(grad_heads, "seq", split_axis=1, concat_axis=2, tiled=True)
    grad_heads = grad_heads.reshape(latent_count, local_heads, full_len, head_size)
    grad_queries, grad_keys, grad_vals = attention_backward(
        queries, key_rows, val_rows, log_totals, grad_heads
    )
    stacked = jnp.stack([grad_queries, grad_keys, grad_vals]).astype(jnp.bfloat16)
    stacked = stacked.reshape(3, latent_count, local_heads, full_len * head_size)
    grad_tokens = lax.all_to_all(stacked, "seq", split_axis=3, concat_axis=2, tiled=True)
    grad_proj = grad_tokens.reshape(3, latent_count, head_count, local_len, head_size).transpose(
        1, 3, 0, 2, 4
    )
    grad_proj = grad_proj.reshape(token_rows, 3 * width)
    qkv_w_grad = outer_dot(mixed_one, grad_proj)
    proj_sums = jnp.sum(grad_proj, axis=0, dtype=jnp.float32)
    qv_b_grad = jnp.concatenate([proj_sums[:width], proj_sums[2 * width :]])
    grad_mixed_one = back_dot(grad_proj, qkv_back).reshape(latent_count, local_len, width)
    shift_one_grad = jnp.sum(grad_mixed_one, axis=1)
    scale_one_grad = jnp.sum(grad_mixed_one * normed_one, axis=1)
    grad_inputs = grad_resid + norm_back(grad_mixed_one * (1.0 + scale_one), normed_one, inv_one)
    partial_mod = jnp.concatenate(
        [
            shift_one_grad,
            scale_one_grad,
            gate_one_grad,
            shift_two_grad,
            scale_two_grad,
            gate_two_grad,
        ],
        axis=1,
    )
    mod_grad = lax.psum(partial_mod, "seq").astype(jnp.bfloat16)
    mod_every = lax.all_gather(mod_grad, ("rep", "fsdp"), axis=0, tiled=True)
    ada_w_grad = outer_dot(silu_owned, mod_every)
    ada_b_grad = jnp.sum(
        lax.dynamic_slice_in_dim(mod_every, owner * bias_cols, bias_cols, 1),
        axis=0,
        dtype=jnp.float32,
    )
    cond_part = back_dot(mod_every, w_ada)
    cond_every = lax.all_gather(cond_part, ("fsdp", "seq"), axis=1, tiled=True)
    cond_lin = lax.dynamic_slice_in_dim(cond_every, first_latent, latent_count, 0)
    cond_grad = cond_lin * cond_sigmoid * (1.0 + cond_float * (1.0 - cond_sigmoid))
    attn_layouts = (qkv_w_grad.shape, qv_b_grad.shape, out_w_grad.shape, out_b_grad.shape)
    attn_flat = lax.psum_scatter(
        pack_rows((qkv_w_grad, qv_b_grad, out_w_grad, out_b_grad), group_size),
        ("fsdp", "seq"),
        scatter_dimension=0,
        tiled=True,
    )
    attn_total, mlp_total = (
        lax.psum(attn_flat.astype(jnp.bfloat16), "rep").astype(jnp.float32),
        lax.psum(mlp_flat.astype(jnp.bfloat16), "rep").astype(jnp.float32),
    )
    attn_parts = unpack_rows(attn_total, attn_layouts, group_size)
    mlp_parts = unpack_rows(mlp_total, mlp_layouts, group_size)
    return (
        block_out,
        grad_inputs,
        cond_grad,
        ada_w_grad,
        ada_b_grad,
        attn_parts[0],
        attn_parts[1],
        attn_parts[2],
        attn_parts[3],
        mlp_parts[0],
        mlp_parts[1],
        mlp_parts[2],
        mlp_parts[3],
    )


def solution(mesh):
    in_specs = (
        P(("rep", "fsdp"), "seq", None),
        P(("rep", "fsdp"), None),
        P(("fsdp", "seq"), None),
        P(("fsdp", "seq")),
        P(("fsdp", "seq"), None),
        P(("fsdp", "seq")),
        P(("fsdp", "seq"), None),
        P(("fsdp", "seq")),
        P(("fsdp", "seq"), None),
        P(("fsdp", "seq")),
        P(("fsdp", "seq"), None),
        P(("fsdp", "seq")),
        P(("rep", "fsdp"), "seq", None),
    )
    out_specs = (
        P(("rep", "fsdp"), "seq", None),
        P(("rep", "fsdp"), "seq", None),
        P(("rep", "fsdp"), None),
        P(("fsdp", "seq"), None),
        P(("fsdp", "seq")),
        P(("fsdp", "seq"), None),
        P(("fsdp", "seq")),
        P(("fsdp", "seq"), None),
        P(("fsdp", "seq")),
        P(("fsdp", "seq"), None),
        P(("fsdp", "seq")),
        P(("fsdp", "seq"), None),
        P(("fsdp", "seq")),
    )
    return jax.shard_map(
        on_device, mesh=mesh, in_specs=in_specs, out_specs=out_specs, check_vma=False
    )
```

profile of v0, /device:TPU:0, one launch (start us, length us, event | category | flops | bytes accessed | tf_op | source)
XLA Modules:
  0.0 3230.9 jit_solution(2037017178745607638)
XLA Ops:
  8.7 32.3 %all-gather = bf16[8,1,1152]{2,1,0:T(2,128)(2,1)S(1)} all-gather(bf16[1,1,1152]{2,1,0:T(2,128)(2,1)S(1)} %get-tuple-element.247), channel_id=1, replica_groups=mesh['rep'=2,'fsdp'=4,'seq'=4] {'rep','fsdp'}, dimensions={0}, use_global_device_ids=true | all-gather | bytes 20736 | tf_op jit(solution)/shard_map/all_gather | solution.py:174
  50.0 57.8 %all-reduce.7 = (bf16[2304]{0:T(1024)(128)(2,1)S(1)}, bf16[1152]{0:T(1024)(128)(2,1)S(1)}, bf16[1152]{0:T(1024)(128)(2,1)S(1)}, bf16[4608]{0:T(1024)(128)(2,1)S(1)}) all-reduce(bf16[2304]{0:T(1024)(128)(2,1)S(1)} %dynamic-update-slice, bf16[1152]{0:T(1024)(128)(2,1)S(1)} %dynamic-update-slice.1, ...), channel_id=1, replica_groups=mesh['rep'=2,'fsdp'=4,'seq'=4] {'fsdp','seq'}, use_global_device_ids=true, to_apply=%add | all-reduce | flops 9216 | bytes 36864
  108.3 25.0 all-reduce.13.cloned.1.call-done
  134.9 73.7 %all-gather.8.cloned.1.call-done = bf16[1152,3456]{1,0:T(8,128)(2,1)} async-done(((bf16[72,3456]{1,0:T(8,128)(2,1)}), bf16[1152,3456]{1,0:T(8,128)(2,1)}) %all-gather.8.cloned.1.call-update) | async-done | bytes 7962640 | tf_op jit(solution)/shard_map/all_gather | solution.py:188
  208.7 7.2 fusion.46
  221.3 8.1 reshape.492
  229.4 3.8 all-to-all-start
  233.2 35.5 %all-to-all-done = bf16[3,1,16,18432]{3,0,1,2:T(4,128)(2,1)S(1)} async-done(((bf16[3,1,16,18432]{3,0,1,2:T(4,128)(2,1)}), bf16[3,1,16,18432]{3,0,1,2:T(4,128)(2,1)S(1)}, u32[]{:S(2)}, u32[]{:S(2)}) %all-to-all-start) | async-done | bytes 1769504 | tf_op jit(solution)/shard_map/all_to_all | solution.py:211
  277.8 4.1 squeeze.14
  283.4 11.3 while.27
  299.2 56.5 %copy.113 = bf16[1,4,73728]{1,0,2:T(2,128)(2,1)} copy(bf16[1,4,73728]{2,1,0:T(4,128)(2,1)S(1)} %reshape_reshape.6) | data formatting | bytes 1179648 | tf_op jit(solution)/shard_map/reshape;reshape | solution.py:218
  356.3 400.0 %reduce.40 = bf16[73728,4]{1,0:T(8,128)(2,1)} reduce(bf16[73728,1,4]{2,1,0:T(2,128)(2,1)} %bitcast.242, bf16[]{:T(256)} %broadcast.232), dimensions={1}, to_apply=%bitcast.165.reduce_sub_computation | reduce | bytes 1179650
  756.3 51.2 %reshape.503 = bf16[4,2,36864]{2,1,0:T(2,128)(2,1)} reshape(bf16[73728,4]{1,0:T(8,128)(2,1)} %reduce.40) | data formatting | bytes 1179648
  807.5 4.3 all-to-all-start.1
  813.2 8.2 all-to-all-done.1
  821.4 61.7 %reshape.504 = bf16[73728,1,4]{2,1,0:T(2,128)(2,1)} reshape(bf16[4,2,36864]{2,1,0:T(2,128)(2,1)} %all-to-all-done.1) | data formatting | bytes 1179648
  883.1 69.2 %copy.114 = bf16[1,4,73728]{2,1,0:T(4,128)(2,1)} copy(bf16[1,4,73728]{1,0,2:T(2,128)(2,1)} %bitcast.243) | data formatting | bytes 1179648 | tf_op jit(solution)/shard_map/all_to_all | solution.py:217
  957.0 4.0 reshape.432
  963.5 4.2 fusion.98
  969.0 9.9 convolution_add_fusion
  978.8 8.2 convert_reduce_fusion.1
  987.1 9.3 fusion.92
  996.4 8.1 fusion.95
  1004.5 9.3 fusion.67
  1023.3 5.3 reshape.493
  1028.6 6.0 reduce.41
  1036.9 4.3 all-to-all-start.2
  1041.3 19.7 reshape.451
  1061.0 15.1 constant_dynamic-update-slice_fusion.7
  1076.1 3.2 fusion.104
  1079.4 4.5 reshape.446
  1085.2 3.5 reshape.506
  1088.7 5.5 bitcast_reduce_fusion
  1098.6 4.0 reshape_reshape.7
  1104.8 38.6 %while.28 = (s32[]{:T(128)}, f32[1,4,1024,72]{2,3,1,0:T(8,128)}, f32[1,4,1024,72]{2,3,1,0:T(8,128)S(1)}, bf16[2,1,4,512,72]{3,4,2,1,0:T(8,128)(2,1)}, bf16[2,1,4...) while((s32[]{:T(128)}, f32[1,4,1024,72]{2,3,1,0:T(8,128)}, ...), condition=%wide.region_13.14_spmd.clone, body=%wide.region_11.13_spmd.clone.sunk | while | flops 1536735232 | bytes 133357912 | solution.py:152
  1109.6 3.3 multiply_convert_fusion.6
  1112.9 4.2 fusion.152
  1117.0 4.6 fusion.153
  1128.6 3.3 multiply_convert_fusion.6
  1131.9 4.5 fusion.152
  1136.4 4.6 fusion.153
  1159.1 70.1 %copy.128 = bf16[3,1,4,73728]{2,0,1,3:T(4,128)(2,1)} copy(bf16[3,1,4,73728]{3,2,1,0:T(4,128)(2,1)S(1)} %pad_maximum_fusion) | data formatting | bytes 3538944 | tf_op jit(solution)/shard_map/stack | solution.py:290
  1229.2 89.7 %reshape.507 = bf16[4,2,110592]{2,1,0:T(2,128)(2,1)} reshape(bf16[73728,1,3,4]{3,2,1,0:T(4,128)(2,1)} %bitcast.169) | data formatting | bytes 3538944
  1318.9 3.7 all-to-all-start.3
  1322.6 13.6 fusion.77
  1336.3 19.7 reshape.453
  1357.5 57.9 %dynamic-update-slice.6 = f32[16,663912]{1,0:T(8,128)} dynamic-update-slice(f32[16,663912]{1,0:T(8,128)} %dynamic-update-slice.5, f32[16,331776]{1,0:T(8,128)} %reshape.453, s32[]{} %constant.143, s32[]{} %constant.145) | dynamic-update-slice | bytes 42467332
  1417.1 56.3 %reshape.455 = f32[10622592]{0:T(1024)} reshape(f32[16,663912]{1,0:T(8,128)} %dynamic-update-slice.7) | data formatting | bytes 84980736 | tf_op jit(solution)/shard_map/reshape | solution.py:57
  1473.5 102.3 %reshape.508 = bf16[73728,1,3,4]{3,2,1,0:T(4,128)(2,1)} reshape(bf16[4,2,110592]{2,1,0:T(2,128)(2,1)S(1)} %all-to-all-done.3) | data formatting | bytes 3538944
  1575.7 101.6 %copy.134 = bf16[3,1,4,4,18432]{4,3,2,0,1:T(4,128)(2,1)} copy(bf16[3,1,4,4,18432]{2,0,4,3,1:T(4,128)(2,1)} %bitcast.33) | data formatting | bytes 3538944 | tf_op jit(solution)/shard_map/all_to_all | solution.py:292
  1680.1 8.3 reshape.439
  1691.0 3.2 copy.131
  1694.3 8.2 fusion.89
  1702.5 6.2 fusion.64
  1709.9 15.0 reshape.445
  1724.8 11.0 constant_dynamic-update-slice_fusion.6
  1737.3 16.0 dynamic-update-slice.10
  1755.1 26.6 reshape.448
  1781.7 1341.9 %all-reduce.16 = (bf16[5311872]{0:T(1024)(128)(2,1)}, bf16[10622592]{0:T(1024)(128)(2,1)}) all-reduce(f32[5311872]{0:T(1024)} %reshape.448, f32[10622592]{0:T(1024)} %reshape.455), channel_id=2, replica_groups=mesh['rep'=2,'fsdp'=4,'seq'=4] {'fsdp','seq'}, use_global_device_ids=true, to_apply=%region_26.27.clone | all-reduce | flops 15934464 | bytes 95606784
  3125.9 3.2 dynamic-slice.16
  3129.2 3.2 fusion.69
  3132.5 22.9 psum.29
  3155.4 31.3 all-gather.1
  3187.1 18.8 all-gather.2
  (268 shorter events, 134.2 us)
Async XLA Ops:
  7.2 35.2 %copy-start = (bf16[72,6912]{1,0:T(8,128)(2,1)S(1)}, bf16[72,6912]{1,0:T(8,128)(2,1)}, u32[]{:S(2)}) copy-start(bf16[72,6912]{1,0:T(8,128)(2,1)} %param.19) | copy-start | bytes 2985988
  7.2 39.2 %copy-start.51 = (u32[32]{0:T(128)S(1)}, u32[32]{0:T(128)}, u32[]{:S(2)}) copy-start(u32[32]{0:T(128)} %constant.104) | copy-start | bytes 388
  7.2 41.8 %copy-start.53 = (bf16[72]{0:T(256)(128)(2,1)S(1)}, bf16[72]{0:T(256)(128)(2,1)}, u32[]{:S(2)}) copy-start(bf16[72]{0:T(256)(128)(2,1)} %param.24) | copy-start | bytes 436
  7.2 42.0 %copy-start.54 = (bf16[72]{0:T(256)(128)(2,1)S(1)}, bf16[72]{0:T(256)(128)(2,1)}, u32[]{:S(2)}) copy-start(bf16[72]{0:T(256)(128)(2,1)} %param.28) | copy-start | bytes 436
  7.2 42.3 %copy-start.55 = (bf16[144]{0:T(256)(128)(2,1)S(1)}, bf16[144]{0:T(256)(128)(2,1)}, u32[]{:S(2)}) copy-start(bf16[144]{0:T(256)(128)(2,1)} %param.22) | copy-start | bytes 868
  7.2 42.5 %copy-start.52 = (bf16[288]{0:T(512)(128)(2,1)S(1)}, bf16[288]{0:T(512)(128)(2,1)}, u32[]{:S(2)}) copy-start(bf16[288]{0:T(512)(128)(2,1)} %param.26) | copy-start | bytes 1732
  7.2 100.5 %copy-start.10 = (bf16[1,256,1152]{2,1,0:T(8,128)(2,1)S(1)}, bf16[1,256,1152]{2,1,0:T(8,128)(2,1)}, u32[]{:S(2)}) copy-start(bf16[1,256,1152]{2,1,0:T(8,128)(2,1)} %param.17) | copy-start | bytes 1769476
  7.3 126.1 %all-reduce.13.cloned.1.call-start = ((), (), s32[]{:S(2)}) async-start(), calls=%async_computation.4 | async-start | bytes 442368 | tf_op jit(solution)/shard_map/psum | solution.py:182
  43.8 164.9 %all-gather.8.cloned.1.call-start = ((), (), s32[]{:S(2)}) async-start(), calls=%async_computation.5 | async-start | bytes 8460288 | tf_op jit(solution)/shard_map/all_gather | solution.py:188
  44.5 918.9 %all-gather.10.cloned.1.call-start = ((), (), s32[]{:S(2)}) async-start(), calls=%async_computation.6 | async-start | bytes 2820096 | tf_op jit(solution)/shard_map/all_gather | solution.py:190
  45.2 923.7 %all-gather.12.cloned.1.call-start = ((), (), s32[]{:S(2)}) async-start(), calls=%async_computation.7 | async-start | bytes 11280384 | tf_op jit(solution)/shard_map/all_gather | solution.py:192
  45.8 933.0 %all-gather.14.cloned.1.call-start = ((), (), s32[]{:S(2)}) async-start(), calls=%async_computation.8 | async-start | bytes 11280384 | tf_op jit(solution)/shard_map/all_gather | solution.py:194
  108.0 100.7 %copy-start.38 = (f32[256]{0:T(256)}, f32[256]{0:T(256)S(1)}, u32[]{:S(2)}) copy-start(f32[256]{0:T(256)S(1)} %broadcast_multiply_fusion.5) | copy-start | bytes 3076
  108.3 100.4 %copy-start.42 = (f32[256]{0:T(256)}, f32[256]{0:T(256)S(1)}, u32[]{:S(2)}) copy-start(f32[256]{0:T(256)S(1)} %add_rsqrt_fusion.1) | copy-start | bytes 3076
  134.9 73.7 %copy-start.27 = (f32[1152]{0:T(1024)}, f32[1152]{0:T(1024)S(1)}, u32[]{:S(2)}) copy-start(f32[1152]{0:T(1024)S(1)} %get-tuple-element.202) | copy-start | bytes 13828
  134.9 73.7 %copy-start.30 = (f32[1152]{0:T(1024)}, f32[1152]{0:T(1024)S(1)}, u32[]{:S(2)}) copy-start(f32[1152]{0:T(1024)S(1)} %get-tuple-element.201) | copy-start | bytes 13828
  229.4 39.4 %all-to-all-start = ((bf16[3,1,16,18432]{3,0,1,2:T(4,128)(2,1)}), bf16[3,1,16,18432]{3,0,1,2:T(4,128)(2,1)S(1)}, u32[]{:S(2)}, u32[]{:S(2)}) async-start(bf16[3,1,16,18432]{3,0,1,2:T(4,128)(2,1)} %reshape.492), calls=%async_computation | async-start | bytes 4718592 | tf_op jit(solution)/shard_map/all_to_all | solution.py:211
  277.8 5.6 copy-start.26
  294.7 61.1 %copy-start.4 = (bf16[1,4,1024,72]{2,3,1,0:T(8,128)(2,1)}, bf16[1,4,1024,72]{2,3,1,0:T(8,128)(2,1)S(1)}, u32[]{:S(2)}) copy-start(bf16[1,4,1024,72]{2,3,1,0:T(8,128)(2,1)S(1)} %get-tuple-element.443) | copy-start | bytes 1769476
  294.7 61.1 %copy-start.33 = (f32[2,1,4,512]{3,2,1,0:T(4,128)}, f32[2,1,4,512]{3,2,1,0:T(4,128)S(1)}, u32[]{:S(2)}) copy-start(f32[2,1,4,512]{3,2,1,0:T(4,128)S(1)} %get-tuple-element.405) | copy-start | bytes 49156
  807.5 13.9 all-to-all-start.1
  963.5 5.5 copy-start.29
  963.5 5.5 copy-start.32
  969.0 9.9 copy-start.36
  978.8 8.2 copy-start.9
  996.4 8.1 copy-start.14
  996.4 8.1 copy-start.18
  1013.8 3.2 copy-start.17
  1036.9 48.2 %all-to-all-start.2 = ((bf16[4,2,36864]{2,1,0:T(2,128)(2,1)}), bf16[4,2,36864]{2,1,0:T(2,128)(2,1)}, u32[]{:S(2)}, u32[]{:S(2)}) async-start(bf16[4,2,36864]{2,1,0:T(2,128)(2,1)} %reshape.505), calls=%async_computation.2 | async-start | bytes 1179648 | tf_op jit(solution)/shard_map/all_to_all | solution.py:285
  1061.0 15.1 copy-start.12
  1061.0 15.1 copy-start.21
  1096.3 8.6 copy-start.34
  1105.0 1.4 copy-start.5
  1105.0 1.4 copy-start.6
  1106.4 3.2 copy-start.1
  1112.9 4.2 copy-start.7
  1117.0 4.6 copy-start.2
  1117.0 4.8 copy-start.24
  1125.4 3.2 copy-start.1
  1131.9 4.5 copy-start.7
  1136.4 4.6 copy-start.2
  1136.4 4.8 copy-start.24
  1143.4 5.1 copy-start.3
  1149.2 6.9 copy-start.22
  1318.9 3.8 copy-start.19
  1318.9 3.8 copy-start.37
  1318.9 154.6 %all-to-all-start.3 = ((bf16[4,2,110592]{2,1,0:T(2,128)(2,1)}), bf16[4,2,110592]{2,1,0:T(2,128)(2,1)S(1)}, u32[]{:S(2)}, u32[]{:S(2)}) async-start(bf16[4,2,110592]{2,1,0:T(2,128)(2,1)} %reshape.507), calls=%async_computation.3 | async-start | bytes 3538944 | tf_op jit(solution)/shard_map/all_to_all | solution.py:292
  1322.6 1886.5 %all-reduce.15.cloned.1.call-start = ((), (), s32[]{:S(2)}) async-start(), calls=%async_computation.9 | async-start | bytes 3989504 | tf_op jit(solution)/shard_map/psum | solution.py:335
  1336.3 19.7 copy-start.40
  1336.3 19.8 copy-start.35
  1691.0 3.3 copy-start.11
  1691.0 3.3 copy-start.28
  1691.0 3.3 copy-start.31
  1691.0 3.3 copy-start.39
  1691.0 3.3 copy-start.43
  1737.3 16.0 copy-start.41
  3125.9 3.3 copy-start.15
  3129.1 3.3 copy-start.49
  3129.1 3.3 copy-start.50
  3129.1 3.3 copy-start.48
  3129.2 77.5 %copy-start.47 = (bf16[8,1,72]{2,1,0:T(2,128)(2,1)S(1)}, bf16[8,1,72]{2,1,0:T(2,128)(2,1)}, u32[]{:S(2)}) copy-start(bf16[8,1,72]{2,1,0:T(2,128)(2,1)} %copy-done.46) | copy-start | bytes 3460
  3132.4 76.0 %copy-start.44 = (bf16[1,1152]{1,0:T(2,128)(2,1)S(1)}, bf16[1,1152]{1,0:T(2,128)(2,1)}, u32[]{:S(2)}) copy-start(bf16[1,1152]{1,0:T(2,128)(2,1)} %param.18) | copy-start | bytes 6916
  3132.4 76.0 %copy-start.45 = (f32[1,1152]{1,0:T(1,128)S(1)}, f32[1,1152]{1,0:T(1,128)}, u32[]{:S(2)}) copy-start(f32[1,1152]{1,0:T(1,128)} %get-tuple-element.248) | copy-start | bytes 13828
  3209.0 5.5 copy-start.13
  (9 other events, 8.5 us)
Sparse Core Ops, SparseCore 0:
  43.9 89.4 all-reduce.12
  135.5 73.1 all-gather.7
  210.8 48.4 all-gather.9
  261.4 87.5 all-gather.11
  351.2 86.8 all-gather.13
  3129.2 68.7 all-reduce.14
where the time goes:
time: 3250 us; the launch traced here: 3230 us
  blocking collectives  1500 us (46%)
  local copies, waits for them, and re-layouts  984 us (30%)
  other arithmetic  434 us (13%)
  waiting for transfers between devices  145 us (4%)
  matrix products  128 us (4%)
    unnamed x2, blocking collectives  1400 us
    unnamed x127, local copies, waits for them, and re-layouts  428 us
    unnamed x5, other arithmetic  407 us
    all_to_all x2, local copies, waits for them, and re-layouts, on_device(): lax.all_to_all(stacked, 'seq', split_axis=3, concat_axis=2, tiled=True)  104 us
    reshape x2, local copies, waits for them, and re-layouts, pack_rows(): jnp.concatenate([array.reshape(groups, -1) for array in arrays], axis=1)  82.9 us
    another operation x4, local copies, waits for them, and re-layouts, on_device(): jnp.stack([grad_queries, grad_keys, grad_vals]).astype(jnp.bfloat16)  78 us
    all_to_all x3, local copies, waits for them, and re-layouts, on_device(): lax.all_to_all(attended.reshape(latent_count, local_heads, full_len * hea...  73.9 us
    all_gather x1, waiting for transfers between devices, on_device(): lax.all_gather(w_qkv, ('fsdp', 'seq'), axis=0, tiled=True)  73.7 us
  transfers between devices with their start and end apart: 10, of which 4 were waited for; matrix products, arithmetic and copies ran while one was open for 28% of the time, Pallas kernels for 0%

commit v1 on v0

v1 whole, which is shorter than its diff:
```python
import math

import jax
import jax.numpy as jnp
from jax import lax
from jax.experimental import pallas as pl
from jax.experimental.pallas import tpu as pltpu
from jax.sharding import PartitionSpec as P

H = 16
epsilon = 1e-06
gelu_coef = math.sqrt(2.0 / math.pi)
log2e = math.log2(math.e)
BF = jnp.bfloat16
F32 = jnp.float32
LANES = 128
VM = pl.BlockSpec(memory_space=pltpu.VMEM)
HB = pl.BlockSpec(memory_space=pl.ANY)
DMA = pltpu.SemaphoreType.DMA


def params(ident, mib):
    return pltpu.CompilerParams(
        collective_id=ident, has_side_effects=True, vmem_limit_bytes=mib * 1024 * 1024
    )


def remote(src, dst, send, recv, device):
    return pltpu.make_async_remote_copy(
        src_ref=src,
        dst_ref=dst,
        send_sem=send,
        recv_sem=recv,
        device_id=device,
        device_id_type=pl.DeviceIdType.MESH,
    )


def local(src, dst, sem):
    return pltpu.make_async_copy(src, dst, sem)


def await_bytes(like, sem):
    pltpu.make_async_copy(like, like, sem).wait()


def each(start, stop, body):
    def step(index, carry):
        body(index)
        return carry

    lax.fori_loop(start, stop, step, 0)


def greet(count, device_of):
    gate = pltpu.get_barrier_semaphore()
    each(
        1,
        count,
        lambda i: pl.semaphore_signal(
            gate, 1, device_id=device_of(i), device_id_type=pl.DeviceIdType.MESH
        ),
    )
    return count - 1


def greet_wait(count):
    pl.semaphore_wait(pltpu.get_barrier_semaphore(), count)


def norm_stats(values):
    center = values - jnp.mean(values, axis=-1, keepdims=True)
    inv_std = lax.rsqrt(jnp.mean(center * center, axis=-1, keepdims=True) + epsilon)
    return (center * inv_std, inv_std)


def norm_back(grad, normed, inv_std):
    return inv_std * (
        grad
        - jnp.mean(grad, axis=-1, keepdims=True)
        - normed * jnp.mean(grad * normed, axis=-1, keepdims=True)
    )


def mm(left, right):
    return jnp.dot(left, right, preferred_element_type=F32)


def mm_nt(left, right):
    return lax.dot_general(left, right, (((1,), (1,)), ((), ())), preferred_element_type=F32)


def mm_tn(left, right):
    return lax.dot_general(left, right, (((0,), (0,)), ((), ())), preferred_element_type=F32)


class Place:
    def __init__(self, sizes):
        self.R, self.F, self.S = sizes
        self.G = self.F * self.S
        self.y = lax.axis_index("rep")
        self.z = lax.axis_index("fsdp")
        self.s = lax.axis_index("seq")
        self.me = self.z * self.S + self.s
        self.mine = lax.rem(self.s, 2) == self.y

    def zs(self, i):
        return lax.rem(self.z + i, self.F)

    def zs_back(self, i):
        return lax.rem(self.z - i + self.F, self.F)

    def ss(self, i):
        return lax.rem(self.s + i, self.S)

    def ss_back(self, i):
        return lax.rem(self.s - i + self.S, self.S)

    def flip(self):
        return {"rep": 1 - self.y}


class ColumnGather:
    sems = (6,)

    def __init__(self, at, src, dst, sem):
        self.at, self.src, self.dst, self.sem = at, src, dst, sem

    @staticmethod
    def scratch(F):
        return DMA((7, F))

    def start(self):
        at, src, dst, sem = self.at, self.src, self.dst, self.sem
        local(src.at[at.s], dst.at[at.me], sem.at[0, 0]).start()

        def near(j):
            t = at.ss(j)
            remote(src.at[t], dst.at[at.me], sem.at[1, 0], sem.at[2, 0], {"seq": t}).start()

        each(1, at.S, near)

        @pl.when(at.mine)
        def _():
            def far(i):
                def one(j):
                    t = at.ss(j)
                    remote(
                        src.at[t],
                        dst.at[at.me],
                        sem.at[3, i],
                        sem.at[4, i],
                        {"fsdp": at.zs(i), "seq": t},
                    ).start()

                each(0, at.S, one)

            each(1, at.F, far)

    def half(self):
        return self.dst.at[pl.ds(0, self.at.S // 2)]

    def forward(self):
        at, dst, sem = self.at, self.dst, self.sem

        def far(i):
            await_bytes(self.half(), sem.at[4, i])

            def one(k):
                slot = at.zs_back(i) * at.S + 2 * k + at.y
                remote(
                    dst.at[slot], dst.at[slot], sem.at[5, i], sem.at[6, i], at.flip()
                ).start()

            each(0, at.S // 2, one)

        each(1, at.F, far)

    def finish(self):
        at, src, dst, sem = self.at, self.src, self.dst, self.sem
        local(src.at[at.s], dst.at[at.me], sem.at[0, 0]).wait()
        near = dst.at[pl.ds(0, at.S - 1)]
        await_bytes(near, sem.at[1, 0])
        await_bytes(near, sem.at[2, 0])

        @pl.when(at.mine)
        def _():
            each(1, at.F, lambda i: await_bytes(src, sem.at[3, i]))

        def far(i):
            await_bytes(self.half(), sem.at[5, i])
            await_bytes(self.half(), sem.at[6, i])

        each(1, at.F, far)


class RowGather:
    def __init__(self, at, src, dst, sem):
        self.at, self.src, self.dst, self.sem = at, src, dst, sem

    @staticmethod
    def scratch(F):
        return DMA((5, F))

    def start(self):
        at, src, dst, sem = self.at, self.src, self.dst, self.sem
        local(src, dst.at[at.z], sem.at[0, 0]).start()

        def far(i):
            remote(
                src.at[at.y], dst.at[at.z, at.y], sem.at[1, i], sem.at[2, i], {"fsdp": at.zs(i)}
            ).start()

        each(1, at.F, far)

    def forward(self):
        at, dst, sem = self.at, self.dst, self.sem

        def far(i):
            block = dst.at[at.zs_back(i), at.y]
            await_bytes(block, sem.at[2, i])
            remote(block, block, sem.at[3, i], sem.at[4, i], at.flip()).start()

        each(1, at.F, far)

    def finish(self):
        at, src, dst, sem = self.at, self.src, self.dst, self.sem
        local(src, dst.at[at.z], sem.at[0, 0]).wait()

        def far(i):
            block = dst.at[0, 0]
            await_bytes(block, sem.at[1, i])
            await_bytes(block, sem.at[3, i])
            await_bytes(block, sem.at[4, i])

        each(1, at.F, far)


class FullGather:
    def __init__(self, at, src, dst, sem):
        self.at, self.src, self.dst, self.sem = at, src, dst, sem

    @staticmethod
    def scratch(F):
        return DMA((5, F))

    def spread(self, i, block):
        at, sem = self.at, self.sem

        def one(j):
            remote(block, block, sem.at[3, i], sem.at[4, i], {"seq": at.ss(j)}).start()

        each(1, at.S, one)

    def start(self):
        at, src, dst, sem = self.at, self.src, self.dst, self.sem
        mine = dst.at[at.z, at.s]
        local(src, mine, sem.at[0, 0]).start()

        def far(i):
            remote(src, mine, sem.at[1, i], sem.at[2, i], {"fsdp": at.zs(i)}).start()

        each(1, at.F, far)

    def forward(self):
        at, src, dst, sem = self.at, self.src, self.dst, self.sem
        local(src, dst.at[at.z, at.s], sem.at[0, 0]).wait()
        self.spread(0, dst.at[at.z, at.s])

        def far(i):
            block = dst.at[at.zs_back(i), at.s]
            await_bytes(block, sem.at[2, i])
            self.spread(i, block)

        each(1, at.F, far)

    def finish(self):
        at, src, dst, sem = self.at, self.src, self.dst, self.sem
        others = dst.at[0, pl.ds(0, at.S - 1)]

        def far(i):
            await_bytes(others, sem.at[3, i])
            await_bytes(others, sem.at[4, i])

        each(0, at.F, far)
        each(1, at.F, lambda i: await_bytes(src, sem.at[1, i]))


def front_kernel(
    sizes,
    cond,
    w_ada,
    bias_slot,
    latents,
    w_qkv,
    w_one,
    w_two,
    w_out,
    bias_pack,
    mixed,
    mod,
    silu_all,
    pack_all,
    g_qkv,
    g_one,
    g_two,
    g_out,
    silu_src,
    part,
    parts_in,
    mod_src,
    mod_in,
    qkv_src,
    one_src,
    silu_sem,
    part_sem,
    mod_sem,
    pack_sem,
    qkv_sem,
    one_sem,
    two_sem,
    out_sem,
):
    at = Place(sizes)
    R, F, S, G = at.R, at.F, at.S, at.G
    D = latents.shape[1]
    C = D // S
    rows = silu_all.shape[2]
    block = one_src.shape[2] // F
    greet(G, lambda i: {"fsdp": lax.rem(at.me + i, G) // S, "seq": lax.rem(at.me + i, S)})
    greet(2 * F, lambda i: {"rep": lax.rem(at.y + i // F, 2), "fsdp": at.zs(i)})
    gate = pltpu.get_barrier_semaphore()
    pl.semaphore_wait(gate, G - 1 + 2 * F - 1)

    value = cond[...].astype(F32)
    silu = (value * jax.nn.sigmoid(value)).astype(BF).astype(F32)
    for g in range(G):
        silu_src[g] = silu[:, g * rows : (g + 1) * rows]
    slot = at.y * F + at.z

    def cond_copy(i):
        z_to = at.zs(i)
        return remote(
            silu_src.at[z_to * S + at.s],
            silu_all.at[slot],
            silu_sem.at[0, i],
            silu_sem.at[1, i],
            {"rep": lax.rem(at.y + i // F, 2), "fsdp": z_to},
        )

    each(1, 2 * F, lambda i: cond_copy(i).start())
    local(silu_src.at[at.me], silu_all.at[slot], silu_sem.at[0, 0]).start()

    def pack_copy(i):
        to = lax.rem(at.me + i, G)
        return remote(
            bias_pack,
            pack_all.at[at.me],
            pack_sem.at[0, 0],
            pack_sem.at[1, 0],
            {"fsdp": to // S, "seq": lax.rem(to, S)},
        )

    local(bias_pack, pack_all.at[at.me], pack_sem.at[2, 0]).start()
    each(1, G, lambda i: pack_copy(i).start())

    for t in range(S):
        for j in range(3):
            qkv_src[t, :, j * C : (j + 1) * C] = w_qkv[:, j * D + t * C : j * D + (t + 1) * C]
    qkv = ColumnGather(at, qkv_src, g_qkv, qkv_sem)
    one = ColumnGather(at, one_src, g_one, one_sem)
    two = RowGather(at, w_two, g_two, two_sem)
    out = FullGather(at, w_out, g_out, out_sem)
    qkv.start()
    out.start()
    for t in range(S):
        for f in range(F):
            col = (f * S + t) * block
            one_src[t, :, f * block : (f + 1) * block] = w_one[:, col : col + block]
    one.start()
    two.start()

    local(silu_src.at[at.me], silu_all.at[slot], silu_sem.at[0, 0]).wait()
    each(1, 2 * F, lambda i: cond_copy(i).wait())
    left = jnp.concatenate([silu_all[at.y * F + f] for f in range(F)], axis=0).astype(BF)
    sums = mm(left, w_ada[...]) + bias_slot[...]
    for f in range(F):
        for v in range(6):
            for t in range(S):
                col = v * D + t * C
                part[f * S + t, v : v + 1, :] = sums[f : f + 1, col : col + C]

    def part_copy(i):
        to = lax.rem(at.me + i, G)
        return remote(
            part.at[to],
            parts_in.at[at.me],
            part_sem.at[0, i],
            part_sem.at[1, i],
            {"fsdp": to // S, "seq": lax.rem(to, S)},
        )

    each(1, G, lambda i: part_copy(i).start())
    local(part.at[at.me], parts_in.at[at.me], part_sem.at[0, 0]).start()
    local(part.at[at.me], parts_in.at[at.me], part_sem.at[0, 0]).wait()
    each(1, G, lambda i: part_copy(i).wait())
    total = parts_in[0]
    for g in range(1, G):
        total = total + parts_in[g]
    mod_src[...] = total

    def mod_copy(i):
        return remote(
            mod_src, mod_in.at[at.s], mod_sem.at[0, i], mod_sem.at[1, i], {"seq": at.ss(i)}
        )

    each(1, S, lambda i: mod_copy(i).start())
    mod_in[at.s] = total
    each(1, S, lambda i: mod_copy(i).wait())
    for t in range(S):
        mod[:, t * C : (t + 1) * C] = mod_in[t]

    shift = mod[0:1, :]
    scale = mod[1:2, :]
    step = min(64, latents.shape[0])

    def norm(i):
        at_rows = pl.ds(i * step, step)
        normed, _ = norm_stats(latents[at_rows, :].astype(F32))
        mixed[at_rows, :] = (normed * (1.0 + scale) + shift).astype(BF)

    each(0, latents.shape[0] // step, norm)

    local(bias_pack, pack_all.at[at.me], pack_sem.at[2, 0]).wait()
    others = pack_all.at[pl.ds(0, G - 1)]
    await_bytes(others, pack_sem.at[0, 0])
    await_bytes(others, pack_sem.at[1, 0])
    qkv.forward()
    out.forward()
    one.forward()
    two.forward()
    qkv.finish()
    out.finish()
    one.finish()
    two.finish()


def front(sizes, cond, w_ada, bias_slot, latents, w_qkv, w_one, w_two, w_out, bias_pack):
    R, F, S = sizes
    G = F * S
    rows, width = w_out.shape
    C = width // S
    hidden = w_one.shape[1] // S
    length = latents.shape[0]
    shape = jax.ShapeDtypeStruct
    return pl.pallas_call(
        lambda *refs: front_kernel(sizes, *refs),
        name="front",
        out_shape=(
            shape((length, width), BF),
            shape((6, width), F32),
            shape((R * F, 1, rows), F32),
            shape((G,) + bias_pack.shape, F32),
            shape((G, rows, 3 * C), BF),
            shape((G, rows, hidden), BF),
            shape((F,) + w_two.shape, BF),
            shape((F, S) + w_out.shape, BF),
        ),
        in_specs=[VM, VM, VM, VM, VM, VM, HB, HB, VM],
        out_specs=(VM, VM, VM, VM, HB, HB, HB, HB),
        scratch_shapes=[
            pltpu.VMEM((G, 1, rows), F32),
            pltpu.VMEM((G, 6, C), F32),
            pltpu.VMEM((G, 6, C), F32),
            pltpu.VMEM((6, C), F32),
            pltpu.VMEM((S, 6, C), F32),
            pltpu.VMEM((S, rows, 3 * C), BF),
            pltpu.VMEM((S, rows, hidden), BF),
            DMA((2, 2 * F)),
            DMA((2, G)),
            DMA((2, S)),
            DMA((3, 1)),
            ColumnGather.scratch(F),
            ColumnGather.scratch(F),
            RowGather.scratch(F),
            FullGather.scratch(F),
        ],
        compiler_params=params(1, 40),
    )(cond, w_ada, bias_slot, latents, w_qkv, w_one, w_two, w_out, bias_pack)
def attend_kernel(
    sizes,
    mixed,
    w_qkv,
    bias,
    mod,
    latents,
    w_out,
    bias_out,
    mixed_all,
    heads,
    log_sums,
    merged,
    branch_one,
    mixed_two,
    val_flip,
    att,
    merged_in,
    mix_sem,
    att_sem,
):
    at = Place(sizes)
    S = at.S
    L, D = mixed.shape
    C = D // S
    T = S * L
    local_heads = H // S
    size = D // H
    greet_wait(greet(S, lambda i: {"seq": at.ss(i)}))

    def mix_copy(j):
        return remote(
            mixed,
            mixed_all.at[at.s],
            mix_sem.at[0, j],
            mix_sem.at[1, j],
            {"seq": lax.bitwise_xor(at.s, j)},
        )

    each(1, S, lambda j: mix_copy(j).start())
    mixed_all[at.s] = mixed[...]

    pad = jnp.zeros((L, LANES - size), BF)

    def project(j):
        t = lax.bitwise_xor(at.s, j)

        @pl.when(j > 0)
        def _():
            mix_copy(j).wait()

        rows = pl.ds(pl.multiple_of(t * L, L), L)
        done = (mm(mixed_all[t], w_qkv[...]) + bias[...]).astype(BF)
        for c in range(3 * local_heads):
            heads[c, rows, :] = jnp.concatenate([done[:, c * size : (c + 1) * size], pad], axis=1)

    each(0, S, project)

    for h in range(local_heads):
        val_flip[h] = heads[2 * local_heads + h].T

    def att_copy(j):
        t = lax.bitwise_xor(at.s, j)
        return remote(
            att.at[t], merged_in.at[at.s], att_sem.at[0, j], att_sem.at[1, j], {"seq": t}
        )

    factor = size ** (-0.5) * log2e

    def attention(index):
        j = S - 1 - index
        t = lax.bitwise_xor(at.s, j)
        rows = pl.ds(pl.multiple_of(t * L, L), L)
        for h in range(local_heads):
            scores = mm_nt(heads[local_heads + h], heads[h, rows, :]) * factor
            highest = jnp.max(scores, axis=0, keepdims=True)
            raised = jnp.exp2(scores - highest)
            summed = jnp.sum(raised, axis=0, keepdims=True)
            result = mm(val_flip[h], raised.astype(BF)) / summed
            log_sums[h, t] = highest + jnp.log2(summed)
            att[t, :, h * size : (h + 1) * size] = result.T[:, :size].astype(BF)

        @pl.when(j > 0)
        def _():
            att_copy(j).start()

    each(0, S, attention)
    merged_in[at.s] = att[at.s]
    each(1, S, lambda j: att_copy(j).wait())
    for t in range(S):
        merged[:, t * C : (t + 1) * C] = merged_in[t]

    gate_one = mod[2:3, :]
    shift = mod[3:4, :]
    scale = mod[4:5, :]
    step = min(64, L)

    def project_out(i):
        rows = pl.ds(pl.multiple_of(i * step, step), step)
        branch = mm(merged[rows, :], w_out[...]) + bias_out[...]
        branch_one[rows, :] = branch
        residual = latents[rows, :].astype(F32) + gate_one * branch
        normed, _ = norm_stats(residual)
        mixed_two[rows, :] = (normed * (1.0 + scale) + shift).astype(BF)

    each(0, L // step, project_out)


def attend(sizes, mixed, w_qkv, bias, mod, latents, w_out, bias_out):
    S = sizes[2]
    L, D = mixed.shape
    C = D // S
    T = S * L
    local_heads = H // S
    shape = jax.ShapeDtypeStruct
    return pl.pallas_call(
        lambda *refs: attend_kernel(sizes, *refs),
        name="attend",
        out_shape=(
            shape((S, L, D), BF),
            shape((3 * local_heads, T, LANES), BF),
            shape((local_heads, S, 1, L), F32),
            shape((L, D), BF),
            shape((L, D), F32),
            shape((L, D), BF),
        ),
        in_specs=[VM] * 7,
        out_specs=(VM,) * 6,
        scratch_shapes=[
            pltpu.VMEM((local_heads, LANES, T), BF),
            pltpu.VMEM((S, L, C), BF),
            pltpu.VMEM((S, L, C), BF),
            DMA((2, S)),
            DMA((2, S)),
        ],
        compiler_params=params(2, 60),
    )(mixed, w_qkv, bias, mod, latents, w_out, bias_out)


def mlp_kernel(
    sizes,
    mixed_two,
    cotangent,
    mod,
    w_one,
    bias_one,
    w_two,
    bias_two,
    branch_one,
    latents,
    w_out,
    merged,
    block_out,
    grad_resid,
    grad_heads,
    grad_w_one,
    grad_w_two,
    grad_w_out,
    grad_b_one,
    grad_b_two,
    grad_b_out,
    mod_sums,
    mix_all,
    grad_all,
    act_all,
    pre_all,
    branch_src,
    mix_src,
    branch_in,
    mix_in,
    grad_branch,
    in_sem,
    branch_sem,
    mix_sem,
):
    at = Place(sizes)
    S = at.S
    L, D = mixed_two.shape
    C = D // S
    hidden = w_one.shape[1]
    greet_wait(greet(S, lambda i: {"seq": at.ss(i)}))
    gate_one = mod[2:3, :]
    scale = mod[4:5, :]
    gate_two = mod[5:6, :]

    def peer(j):
        return lax.bitwise_xor(at.s, j)

    def mixed_copy(j):
        return remote(
            mixed_two, mix_all.at[at.s], in_sem.at[0, j], in_sem.at[1, j], {"seq": peer(j)}
        )

    def grad_copy(j):
        return remote(
            grad_all.at[at.s],
            grad_all.at[at.s],
            in_sem.at[2, j],
            in_sem.at[3, j],
            {"seq": peer(j)},
        )

    each(1, S, lambda j: mixed_copy(j).start())
    grad_all[at.s] = (gate_two * cotangent[...].astype(F32)).astype(BF)
    each(1, S, lambda j: grad_copy(j).start())
    mix_all[at.s] = mixed_two[...]

    def branch_copy(j):
        return remote(
            branch_src.at[peer(j)],
            branch_in.at[j],
            branch_sem.at[0, j],
            branch_sem.at[1, j],
            {"seq": peer(j)},
        )

    def mix_copy(j):
        return remote(
            mix_src.at[peer(j)],
            mix_in.at[j],
            mix_sem.at[0, j],
            mix_sem.at[1, j],
            {"seq": peer(j)},
        )

    def block(j):
        t = peer(j)

        @pl.when(j > 0)
        def _():
            mixed_copy(j).wait()
            grad_copy(j).wait()

        step = min(128, L)

        def part(i):
            rows = pl.ds(pl.multiple_of(i * step, step), step)
            pre = mm(mix_all[t, rows, :], w_one[...]) + bias_one[...]
            square = pre * pre
            inner = gelu_coef * (pre + 0.044715 * square * pre)
            tanh_val = jnp.tanh(inner)
            half = 0.5 * (1.0 + tanh_val)
            act = (pre * half).astype(BF)
            act_all[t, rows, :] = act
            slope = half + 0.5 * pre * (1.0 - tanh_val * tanh_val) * gelu_coef * (
                1.0 + 3.0 * 0.044715 * square
            )
            grad_pre = (mm_nt(grad_all[t, rows, :], w_two[...]) * slope).astype(BF)
            pre_all[t, rows, :] = grad_pre
            mix_src[t, rows, :] = mm_nt(grad_pre, w_one[...]).astype(BF)
            branch_src[t, rows, :] = mm(act, w_two[...]).astype(BF)

        each(0, L // step, part)

        @pl.when(j > 0)
        def _():
            mix_copy(j).start()
            branch_copy(j).start()

    each(0, S, block)

    def flat(ref, cols):
        return ref[:, :, cols].reshape(S * L, -1)

    step = 128 if hidden % 128 == 0 else hidden
    for i in range(hidden // step):
        cols = slice(i * step, (i + 1) * step)
        grads = pre_all[:, :, cols].reshape(S * L, step)
        grad_b_one[:, cols] = jnp.sum(grads.astype(F32), axis=0, keepdims=True)
    wide = 384 if hidden % 384 == 0 else hidden
    for i in range(hidden // wide):
        cols = slice(i * wide, (i + 1) * wide)
        grad_w_one[:, cols] = mm_tn(
            mix_all[...].reshape(S * L, D), pre_all[:, :, cols].reshape(S * L, wide)
        ).astype(BF)
        grad_w_two[cols, :] = mm_tn(
            act_all[:, :, cols].reshape(S * L, wide), grad_all[...].reshape(S * L, D)
        ).astype(BF)
    grad_b_two[...] = jnp.sum(grad_all[at.s].astype(F32), axis=0, keepdims=True)

    each(1, S, lambda j: mix_copy(j).wait())
    step = min(32, L)
    mod_sums[...] = jnp.zeros_like(mod_sums)
    grad_b_out[...] = jnp.zeros_like(grad_b_out)

    def gather(src, incoming, rows):
        total = src[at.s, rows, :].astype(F32)
        for j in range(1, S):
            total = total + incoming[j, rows, :].astype(F32)
        return total

    def back(i):
        rows = pl.ds(pl.multiple_of(i * step, step), step)
        grad_mixed = gather(mix_src, mix_in, rows)
        branch = branch_one[rows, :]
        residual = latents[rows, :].astype(F32) + gate_one * branch
        normed, inv_std = norm_stats(residual)
        grad_out = cotangent[rows, :].astype(F32)
        grad = grad_out + norm_back(grad_mixed * (1.0 + scale), normed, inv_std)
        grad_resid[rows, :] = grad
        low = (gate_one * grad).astype(BF)
        grad_branch[rows, :] = low
        mod_sums[2:3, :] += jnp.sum(grad * branch, axis=0, keepdims=True)
        mod_sums[3:4, :] += jnp.sum(grad_mixed, axis=0, keepdims=True)
        mod_sums[4:5, :] += jnp.sum(grad_mixed * normed, axis=0, keepdims=True)
        grad_b_out[...] += jnp.sum(low.astype(F32), axis=0, keepdims=True)

    each(0, L // step, back)
    grad_merged = mm_nt(grad_branch[...], w_out[...]).astype(BF)
    for t in range(S):
        grad_heads[t] = grad_merged[:, t * C : (t + 1) * C]
    wide = 384
    for i in range(D // wide):
        cols = slice(i * wide, (i + 1) * wide)
        grad_w_out[:, cols] = mm_tn(merged[...], grad_branch[:, cols]).astype(BF)

    each(1, S, lambda j: branch_copy(j).wait())

    def finish(i):
        rows = pl.ds(pl.multiple_of(i * step, step), step)
        branch_two = gather(branch_src, branch_in, rows) + bias_two[...]
        residual = latents[rows, :].astype(F32) + gate_one * branch_one[rows, :]
        block_out[rows, :] = (residual + gate_two * branch_two).astype(BF)
        grad_out = cotangent[rows, :].astype(F32)
        mod_sums[5:6, :] += jnp.sum(grad_out * branch_two, axis=0, keepdims=True)

    each(0, L // step, finish)


def mlp(sizes, mixed_two, cotangent, mod, w_one, b_one, w_two, b_two, branch, latents, w_out, merged):
    S = sizes[2]
    L, D = mixed_two.shape
    C = D // S
    hidden = w_one.shape[1]
    shape = jax.ShapeDtypeStruct
    tokens = (S, L, D)
    return pl.pallas_call(
        lambda *refs: mlp_kernel(sizes, *refs),
        name="mlp",
        out_shape=(
            shape((L, D), BF),
            shape((L, D), F32),
            shape((S, L, C), BF),
            shape((D, hidden), BF),
            shape((hidden, D), BF),
            shape((D, D), BF),
            shape((1, hidden), F32),
            shape((1, D), F32),
            shape((1, D), F32),
            shape((6, D), F32),
        ),
        in_specs=[VM] * 11,
        out_specs=(VM,) * 10,
        scratch_shapes=[
            pltpu.VMEM(tokens, BF),
            pltpu.VMEM(tokens, BF),
            pltpu.VMEM((S, L, hidden), BF),
            pltpu.VMEM((S, L, hidden), BF),
            pltpu.VMEM(tokens, BF),
            pltpu.VMEM(tokens, BF),
            pltpu.VMEM(tokens, BF),
            pltpu.VMEM(tokens, BF),
            pltpu.VMEM((L, D), BF),
            DMA((4, S)),
            DMA((2, S)),
            DMA((2, S)),
        ],
        compiler_params=params(3, 60),
    )(mixed_two, cotangent, mod, w_one, b_one, w_two, b_two, branch, latents, w_out, merged)


def attend_back_kernel(
    sizes,
    grad_heads,
    heads,
    log_sums,
    mixed_all,
    w_qkv,
    latents,
    mod,
    grad_resid,
    sums_in,
    grad_latents,
    grad_w_qkv,
    grad_b_qkv,
    mod_sums,
    grad_in,
    key_flip,
    key_grad,
    val_grad,
    grad_proj,
    mix_src,
    mix_in,
    in_sem,
    mix_sem,
):
    at = Place(sizes)
    S = at.S
    _, L, C = grad_heads.shape
    D = latents.shape[1]
    local_heads = H // S
    size = D // H
    greet_wait(greet(S, lambda i: {"seq": at.ss(i)}))

    def peer(j):
        return lax.bitwise_xor(at.s, j)

    def in_copy(j):
        return remote(
            grad_heads.at[peer(j)],
            grad_in.at[at.s],
            in_sem.at[0, j],
            in_sem.at[1, j],
            {"seq": peer(j)},
        )

    each(1, S, lambda j: in_copy(j).start())
    grad_in[at.s] = grad_heads[at.s]
    for h in range(local_heads):
        key_flip[h] = heads[local_heads + h].T
    key_grad[...] = jnp.zeros_like(key_grad)
    val_grad[...] = jnp.zeros_like(val_grad)
    factor = size ** (-0.5) * log2e
    score_scale = size ** (-0.5)
    pad = jnp.zeros((L, LANES - size), BF)

    def block(j):
        t = peer(j)

        @pl.when(j > 0)
        def _():
            in_copy(j).wait()

        rows = pl.ds(pl.multiple_of(t * L, L), L)
        for h in range(local_heads):
            query = heads[h, rows, :]
            grad = jnp.concatenate([grad_in[t, :, h * size : (h + 1) * size], pad], axis=1)
            scores = mm_nt(heads[local_heads + h], query) * factor
            probs = jnp.exp2(scores - log_sums[h, t])
            grad_probs = mm_nt(heads[2 * local_heads + h], grad)
            inner = jnp.sum(probs * grad_probs, axis=0, keepdims=True)
            grad_scores = (probs * (grad_probs - inner)).astype(BF)
            query_grad = mm(key_flip[h], grad_scores) * score_scale
            grad_proj[t, :, h * size : (h + 1) * size] = query_grad.T[:, :size].astype(BF)
            key_grad[h] += mm(grad_scores, query)
            val_grad[h] += mm(probs.astype(BF), grad)

    each(0, S, block)
    for h in range(local_heads):
        low = (key_grad[h] * score_scale)[:, :size].astype(BF)
        grad_proj[:, :, C + h * size : C + (h + 1) * size] = low.reshape(S, L, size)
        low = val_grad[h][:, :size].astype(BF)
        grad_proj[:, :, 2 * C + h * size : 2 * C + (h + 1) * size] = low.reshape(S, L, size)

    def mix_copy(j):
        return remote(
            mix_src.at[peer(j)],
            mix_in.at[j],
            mix_sem.at[0, j],
            mix_sem.at[1, j],
            {"seq": peer(j)},
        )

    def spread(index):
        j = S - 1 - index
        t = peer(j)
        mix_src[t] = mm_nt(grad_proj[t], w_qkv[...]).astype(BF)

        @pl.when(j > 0)
        def _():
            mix_copy(j).start()

    each(0, S, spread)
    wide = 288 if C % 288 == 0 else C
    tokens = mixed_all[...].reshape(S * L, D)
    grads = grad_proj[...].reshape(S * L, 3 * C)
    grad_w_qkv[...] = mm_tn(tokens, grads).astype(BF)
    grad_b_qkv[...] = jnp.sum(grads.astype(F32), axis=0, keepdims=True)

    each(1, S, lambda j: mix_copy(j).wait())
    step = min(32, L)
    mod_sums[...] = sums_in[...]
    scale = mod[1:2, :]

    def back(i):
        rows = pl.ds(pl.multiple_of(i * step, step), step)
        grad_mixed = mix_src[at.s, rows, :].astype(F32)
        for j in range(1, S):
            grad_mixed = grad_mixed + mix_in[j, rows, :].astype(F32)
        normed, inv_std = norm_stats(latents[rows, :].astype(F32))
        grad_latents[rows, :] = grad_resid[rows, :] + norm_back(
            grad_mixed * (1.0 + scale), normed, inv_std
        )
        mod_sums[0:1, :] += jnp.sum(grad_mixed, axis=0, keepdims=True)
        mod_sums[1:2, :] += jnp.sum(grad_mixed * normed, axis=0, keepdims=True)

    each(0, L // step, back)


def attend_back(sizes, grad_heads, heads, log_sums, mixed_all, w_qkv, latents, mod, grad_resid, sums):
    S, L, C = grad_heads.shape
    D = latents.shape[1]
    T = S * L
    local_heads = H // S
    shape = jax.ShapeDtypeStruct
    return pl.pallas_call(
        lambda *refs: attend_back_kernel(sizes, *refs),
        name="attend_back",
        out_shape=(
            shape((L, D), F32),
            shape((D, 3 * C), BF),
            shape((1, 3 * C), F32),
            shape((6, D), F32),
        ),
        in_specs=[VM] * 9,
        out_specs=(VM,) * 4,
        scratch_shapes=[
            pltpu.VMEM((S, L, C), BF),
            pltpu.VMEM((local_heads, LANES, T), BF),
            pltpu.VMEM((local_heads, T, LANES), F32),
            pltpu.VMEM((local_heads, T, LANES), F32),
            pltpu.VMEM((S, L, 3 * C), BF),
            pltpu.VMEM((S, L, D), BF),
            pltpu.VMEM((S, L, D), BF),
            DMA((2, S)),
            DMA((2, S)),
        ],
        compiler_params=params(4, 60),
    )(grad_heads, heads, log_sums, mixed_all, w_qkv, latents, mod, grad_resid, sums)
class ColumnScatter:
    def __init__(self, at, src, got, stage, inn, done, sem):
        self.at, self.src, self.got, self.stage = at, src, got, stage
        self.inn, self.done, self.sem = inn, done, sem

    @staticmethod
    def scratch(sizes, rows, cols):
        R, F, S = sizes
        return [
            pltpu.VMEM((F, S // 2, rows, cols), BF),
            pltpu.VMEM((F, S // 2, rows, cols), BF),
            pltpu.VMEM((F * S, rows, cols), BF),
            pltpu.VMEM((S, rows, cols), BF),
            DMA((6, F)),
        ]

    def start(self):
        at = self.at

        def far(i):
            z_to = at.zs(i)

            def one(k):
                remote(
                    self.src.at[z_to * at.S + 2 * k + 1 - at.y],
                    self.got.at[z_to, k],
                    self.sem.at[0, i],
                    self.sem.at[1, i],
                    at.flip(),
                ).start()

            each(0, at.S // 2, one)

        each(0, at.F, far)

    def scatter(self):
        at = self.at

        def far(index):
            i = lax.rem(index + 1, at.F)
            z_to = at.zs(i)
            await_bytes(self.got.at[0], self.sem.at[1, i])

            def one(k):
                s_to = 2 * k + at.y
                total = self.src[z_to * at.S + s_to].astype(F32) + self.got[z_to, k].astype(F32)
                low = total.astype(BF)
                home = (i == 0) & (s_to == at.s)
                self.stage[z_to, k] = low

                @pl.when(home)
                def _():
                    self.inn[at.me] = low

                @pl.when(jnp.logical_not(home))
                def _():
                    remote(
                        self.stage.at[z_to, k],
                        self.inn.at[at.me],
                        self.sem.at[2, i],
                        self.sem.at[3, 0],
                        {"fsdp": z_to, "seq": s_to},
                    ).start()

            each(0, at.S // 2, one)

        each(0, at.F, far)

    def total(self):
        at = self.at

        @pl.when(at.mine)
        def _():
            await_bytes(self.inn.at[pl.ds(0, at.G - 1)], self.sem.at[3, 0])

            def one(t):
                total = self.inn[t].astype(F32)
                for f in range(1, at.F):
                    total = total + self.inn[f * at.S + t].astype(F32)
                self.done[t] = total.astype(BF)

            each(0, at.S, one)
            remote(
                self.done, self.done, self.sem.at[4, 0], self.sem.at[5, 0], at.flip()
            ).start()

    def finish(self):
        at = self.at
        half = self.got.at[0]
        each(0, at.F, lambda i: await_bytes(half, self.sem.at[0, i]))
        each(1, at.F, lambda i: await_bytes(half, self.sem.at[2, i]))

        @pl.when(at.mine)
        def _():
            if at.S > 2:
                await_bytes(self.got.at[0, pl.ds(0, at.S // 2 - 1)], self.sem.at[2, 0])
            await_bytes(self.done, self.sem.at[4, 0])

        @pl.when(jnp.logical_not(at.mine))
        def _():
            await_bytes(half, self.sem.at[2, 0])
            await_bytes(self.done, self.sem.at[5, 0])


class RowScatter:
    def __init__(self, at, src, got, stage, inn, done, sem):
        self.at, self.src, self.got, self.stage = at, src, got, stage
        self.inn, self.done, self.sem = inn, done, sem

    @staticmethod
    def scratch(sizes, rows, cols):
        R, F, S = sizes
        return [
            pltpu.VMEM((F, rows, cols), BF),
            pltpu.VMEM((F, rows, cols), BF),
            pltpu.VMEM((F, rows, cols), BF),
            pltpu.VMEM((2, rows, cols), BF),
            DMA((6, F)),
        ]

    def start(self):
        at = self.at

        def far(i):
            z_to = at.zs(i)
            remote(
                self.src.at[z_to, 1 - at.y],
                self.got.at[z_to],
                self.sem.at[0, i],
                self.sem.at[1, i],
                at.flip(),
            ).start()

        each(0, at.F, far)

    def out_copy(self, i):
        at = self.at
        return remote(
            self.stage.at[at.zs(i)],
            self.inn.at[at.z],
            self.sem.at[2, i],
            self.sem.at[3, i],
            {"fsdp": at.zs(i)},
        )

    def scatter(self):
        at = self.at

        def far(index):
            i = lax.rem(index + 1, at.F)
            z_to = at.zs(i)
            await_bytes(self.got.at[0], self.sem.at[1, i])
            total = self.src[z_to, at.y].astype(F32) + self.got[z_to].astype(F32)
            self.stage[z_to] = total.astype(BF)

            @pl.when(i > 0)
            def _():
                self.out_copy(i).start()

        each(0, at.F, far)

    def total(self):
        at = self.at
        self.inn[at.z] = self.stage[at.z]
        each(1, at.F, lambda i: self.out_copy(i).wait())
        total = self.inn[0].astype(F32)
        for f in range(1, at.F):
            total = total + self.inn[f].astype(F32)
        self.done[at.y] = total.astype(BF)
        half = self.done.at[at.y]
        remote(half, half, self.sem.at[4, 0], self.sem.at[5, 0], at.flip()).start()

    def finish(self):
        at = self.at
        each(0, at.F, lambda i: await_bytes(self.got.at[0], self.sem.at[0, i]))
        await_bytes(self.done.at[0], self.sem.at[4, 0])
        await_bytes(self.done.at[0], self.sem.at[5, 0])


class FullScatter:
    def __init__(self, at, src, got, stage, inn, swap, sem):
        self.at, self.src, self.got, self.stage = at, src, got, stage
        self.inn, self.swap, self.sem = inn, swap, sem

    @staticmethod
    def scratch(sizes, rows, cols):
        R, F, S = sizes
        return [
            pltpu.VMEM((S, F, rows, cols), BF),
            pltpu.VMEM((F, rows, cols), BF),
            pltpu.VMEM((F, rows, cols), BF),
            pltpu.VMEM((2, rows, cols), BF),
            DMA((6, max(F, S))),
        ]

    def start(self):
        at = self.at

        def near(j):
            def one(f):
                remote(
                    self.src.at[f, at.ss(j)],
                    self.got.at[j, f],
                    self.sem.at[0, j],
                    self.sem.at[1, j],
                    {"seq": at.ss(j)},
                ).start()

            each(0, at.F, one)

        each(1, at.S, near)

    def out_copy(self, i):
        at = self.at
        return remote(
            self.stage.at[at.zs(i)],
            self.inn.at[at.z],
            self.sem.at[2, i],
            self.sem.at[3, i],
            {"fsdp": at.zs(i)},
        )

    def scatter(self):
        at = self.at

        def arrived(j):
            await_bytes(self.got.at[0], self.sem.at[0, j])
            await_bytes(self.got.at[0], self.sem.at[1, j])

        each(1, at.S, arrived)

        def far(i):
            z_to = at.zs(i)
            total = self.src[z_to, at.s].astype(F32)
            for j in range(1, at.S):
                total = total + self.got[j, z_to].astype(F32)
            self.stage[z_to] = total.astype(BF)

            @pl.when(i > 0)
            def _():
                self.out_copy(i).start()

        each(0, at.F, far)

    def total(self):
        at = self.at
        self.inn[at.z] = self.stage[at.z]
        each(1, at.F, lambda i: self.out_copy(i).wait())
        total = self.inn[0].astype(F32)
        for f in range(1, at.F):
            total = total + self.inn[f].astype(F32)
        self.swap[at.y] = total.astype(BF)
        mine = self.swap.at[at.y]
        remote(mine, mine, self.sem.at[4, 0], self.sem.at[5, 0], at.flip()).start()

    def finish(self):
        await_bytes(self.swap.at[0], self.sem.at[4, 0])
        await_bytes(self.swap.at[0], self.sem.at[5, 0])


class Tail:
    def __init__(self, at, sums, first_in, mod_src, mod_all, small_src, small_in, cond_src, cond_in, pieces, sem):
        self.at, self.sums, self.first_in = at, sums, first_in
        self.mod_src, self.mod_all = mod_src, mod_all
        self.small_src, self.small_in = small_src, small_in
        self.cond_src, self.cond_in, self.pieces, self.sem = cond_src, cond_in, pieces, sem

    @staticmethod
    def scratch(sizes, D, hidden, rows):
        R, F, S = sizes
        G = F * S
        C = D // S
        pack = 2 * D // G + 2 * rows + hidden // F
        wide = max(D, hidden, 3 * C)
        return [
            pltpu.VMEM((10, wide), F32),
            pltpu.VMEM((S, 10, wide), F32),
            pltpu.VMEM((6, D), BF),
            pltpu.VMEM((R * F, 6, D), BF),
            pltpu.VMEM((F, 1, pack), F32),
            pltpu.VMEM((R * F, 1, pack), F32),
            pltpu.VMEM((R * F, 1, rows), F32),
            pltpu.VMEM((G, 1, rows), F32),
            pltpu.VMEM((G, 1, pack), F32),
            DMA((8, max(S, 2 * F, G))),
        ]

    def first_copy(self, j):
        at = self.at
        return remote(
            self.sums, self.first_in.at[at.s], self.sem.at[0, j], self.sem.at[1, j], {"seq": at.ss(j)}
        )

    def start(self, mod_sums, b_one, b_two, b_out, b_qkv):
        sums = self.sums
        D = mod_sums.shape[1]
        hidden = b_one.shape[1]
        sums[...] = jnp.zeros_like(sums)
        sums[0:6, 0:D] = mod_sums[...]
        sums[6:7, 0:hidden] = b_one[...]
        sums[7:8, 0:D] = b_two[...]
        sums[8:9, 0:D] = b_out[...]
        sums[9:10, 0 : b_qkv.shape[1]] = b_qkv[...]
        each(1, self.at.S, lambda j: self.first_copy(j).start())
        self.first_in[self.at.s] = sums[...]

    def wide_copies(self, i):
        at = self.at
        slot = at.y * at.F + at.z
        device = {"rep": lax.rem(at.y + i // at.F, 2), "fsdp": at.zs(i)}
        return (
            remote(self.mod_src, self.mod_all.at[slot], self.sem.at[2, i], self.sem.at[3, i], device),
            remote(
                self.small_src.at[at.zs(i)],
                self.small_in.at[slot],
                self.sem.at[4, i],
                self.sem.at[5, i],
                device,
            ),
        )

    def middle(self, D, hidden, rows):
        at = self.at
        F, S, G = at.F, at.S, at.G
        C = D // S
        qv = 2 * D // G
        each(1, S, lambda j: self.first_copy(j).wait())
        total = self.first_in[0]
        for t in range(1, S):
            total = total + self.first_in[t]
        self.mod_src[...] = total[0:6, 0:D].astype(BF)
        for g in range(G):
            g_half = g % (G // 2)
            t = g_half // (F // 2)
            col = (g_half % (F // 2)) * qv + (2 * C if g >= G // 2 else 0)
            self.pieces[g, :, 0:qv] = self.first_in[t, 9:10, col : col + qv]
            self.pieces[g, :, qv : qv + rows] = total[8:9, g * rows : (g + 1) * rows]
            self.pieces[g, :, qv + rows : qv + 2 * rows] = total[7:8, g * rows : (g + 1) * rows]
        block = hidden // F
        for f in range(F):
            self.small_src[f, :, 0 : qv + 2 * rows] = self.pieces[f * S + at.s][:, 0 : qv + 2 * rows]
            self.small_src[f, :, qv + 2 * rows :] = self.sums[6:7, f * block : (f + 1) * block]

        def send(i):
            first, second = self.wide_copies(i)
            first.start()
            second.start()

        each(1, 2 * F, send)
        slot = at.y * F + at.z
        self.mod_all[slot] = self.mod_src[...]
        self.small_in[slot] = self.small_src[at.z]

    def cond_copy(self, i):
        at = self.at
        to = lax.rem(at.me + i, at.G)
        return remote(
            self.cond_src.at[at.y * at.F + to // at.S],
            self.cond_in.at[at.me],
            self.sem.at[6, i],
            self.sem.at[7, i],
            {"fsdp": to // at.S, "seq": lax.rem(to, at.S)},
        )

    def owners(self, silu_all, w_ada, grad_w_ada, grad_b_ada, flat_sum, b_pieces, small_out):
        at = self.at
        F, G = at.F, at.G
        D = self.mod_src.shape[1]
        width = grad_b_ada.shape[1]

        def arrive(i):
            first, second = self.wide_copies(i)
            first.wait()
            second.wait()

        each(1, 2 * F, arrive)
        cond = None
        for v in range(6):
            rows = self.mod_all[:, v, :]
            part = mm_nt(rows, w_ada[:, v * D : (v + 1) * D])
            cond = part if cond is None else cond + part
        for i in range(2 * F):
            self.cond_src[i] = cond[i : i + 1, :]
        each(1, G, lambda i: self.cond_copy(i).start())
        self.cond_in[at.me] = self.cond_src[at.y * F + at.z]
        silu = silu_all[:, 0, :].astype(BF)
        for v in range(6):
            rows = self.mod_all[:, v, :]
            grad_w_ada[:, v * D : (v + 1) * D] = mm_tn(silu, rows)
            flat_sum[:, v * D : (v + 1) * D] = jnp.sum(rows.astype(F32), axis=0, keepdims=True)
        for g in range(G):
            b_pieces[g] = flat_sum[:, g * width : (g + 1) * width]
        grad_b_ada[...] = b_pieces[at.me]
        total = self.small_in[0]
        for i in range(1, 2 * F):
            total = total + self.small_in[i]
        small_out[...] = total

    def finish(self, cond, grad_cond):
        at = self.at
        rows = self.cond_in.shape[2]
        each(1, at.G, lambda i: self.cond_copy(i).wait())
        for g in range(at.G):
            cols = slice(g * rows, (g + 1) * rows)
            value = cond[:, cols].astype(F32)
            gate = jax.nn.sigmoid(value)
            grad_cond[:, cols] = self.cond_in[g] * gate * (1.0 + value * (1.0 - gate))


def sums_kernel(sizes, *refs):
    at = Place(sizes)
    R, F, S, G = at.R, at.F, at.S, at.G
    qkv_g, one_g, two_g, out_g, mod_sums, b_one, b_two, b_out, b_qkv, silu_all, w_ada, cond = refs[:12]
    o_qkv, o_one, o_two, o_out, o_ada, o_b_ada, o_small, o_cond = refs[12:20]
    rest = list(refs[20:])
    qkv = ColumnScatter(at, qkv_g, *rest[0:5])
    one = ColumnScatter(at, one_g, *rest[5:10])
    two = RowScatter(at, two_g, *rest[10:15])
    out = FullScatter(at, out_g, *rest[15:20])
    tail = Tail(at, *rest[20:30])
    flat_sum, b_pieces = rest[30:32]
    rows, D = o_out.shape
    C = D // S
    hidden = one_g.shape[2]
    greet(G, lambda i: {"fsdp": lax.rem(at.me + i, G) // S, "seq": lax.rem(at.me + i, S)})
    greet(2 * F, lambda i: {"rep": lax.rem(at.y + i // F, 2), "fsdp": at.zs(i)})
    greet_wait(G - 1 + 2 * F - 1)
    tail.start(mod_sums, b_one, b_two, b_out, b_qkv)
    out.start()
    two.start()
    one.start()
    qkv.start()
    tail.middle(D, hidden, rows)
    out.scatter()
    tail.owners(silu_all, w_ada, o_ada, o_b_ada, flat_sum, b_pieces, o_small)
    two.scatter()
    one.scatter()
    qkv.scatter()
    tail.finish(cond, o_cond)
    out.total()
    two.total()
    one.total()
    qkv.total()
    out.finish()
    o_out[...] = out.swap[0].astype(F32) + out.swap[1].astype(F32)
    two.finish()
    for p in range(2):
        o_two[p] = two.done[p].astype(F32)
    one.finish()
    block = hidden // F
    for t in range(S):
        for f in range(F):
            col = (f * S + t) * block
            o_one[:, col : col + block] = one.done[t, :, f * block : (f + 1) * block].astype(F32)
    qkv.finish()
    for t in range(S):
        for j in range(3):
            o_qkv[:, j * D + t * C : j * D + (t + 1) * C] = qkv.done[
                t, :, j * C : (j + 1) * C
            ].astype(F32)


def sums(sizes, qkv_g, one_g, two_g, out_g, mod_sums, b_one, b_two, b_out, b_qkv, silu_all, w_ada, cond):
    R, F, S = sizes
    G = F * S
    D = cond.shape[1]
    rows = w_ada.shape[0]
    hidden = one_g.shape[2]
    width = w_ada.shape[1] // G
    shape = jax.ShapeDtypeStruct
    pack = 2 * D // G + 2 * rows + hidden // F
    return pl.pallas_call(
        lambda *refs: sums_kernel(sizes, *refs),
        name="sums",
        out_shape=(
            shape((rows, 3 * D), F32),
            shape((rows, hidden * S), F32),
            shape(two_g.shape[1:], F32),
            shape((rows, D), F32),
            shape(w_ada.shape, F32),
            shape((1, width), F32),
            shape((1, pack), F32),
            shape((1, D), F32),
        ),
        in_specs=[VM] * 12,
        out_specs=(VM,) * 8,
        scratch_shapes=ColumnScatter.scratch(sizes, rows, qkv_g.shape[2])
        + ColumnScatter.scratch(sizes, rows, hidden)
        + RowScatter.scratch(sizes, two_g.shape[2], D)
        + FullScatter.scratch(sizes, rows, D)
        + Tail.scratch(sizes, D, hidden, rows)
        + [pltpu.VMEM((1, w_ada.shape[1]), F32), pltpu.VMEM((G, 1, width), F32)],
        compiler_params=params(5, 62),
    )(qkv_g, one_g, two_g, out_g, mod_sums, b_one, b_two, b_out, b_qkv, silu_all, w_ada, cond)


def on_device(
    latents, cond, w_ada, b_ada, w_qkv, b_qv, w_out, b_out, w_one, b_one, w_two, b_two, cotangent
):
    sizes = R, F, S = tuple(lax.axis_size(name) for name in ("rep", "fsdp", "seq"))
    G = F * S
    _, L, D = latents.shape
    C = D // S
    hidden = w_one.shape[1] // S
    rows = w_ada.shape[0]
    qv = b_qv.shape[0]
    owner = lax.axis_index(("fsdp", "seq"))
    s = lax.axis_index("seq")
    width = b_ada.shape[0]
    bias_slot = lax.dynamic_update_slice(
        jnp.zeros((w_ada.shape[1],), F32), b_ada.astype(F32), (owner * width,)
    )[None]
    bias_pack = jnp.concatenate([b_qv, b_out, b_two, b_one]).astype(F32)[None]
    tokens = latents[0]
    two_rows = w_two.shape[0]
    mixed, mod, silu_all, packs, g_qkv, g_one, g_two, g_out = front(
        sizes,
        cond,
        w_ada,
        bias_slot,
        tokens,
        w_qkv,
        w_one,
        w_two.reshape(2, two_rows // 2, D),
        w_out,
        bias_pack,
    )
    packs = packs[:, 0]
    half = G // 2
    own = F // 2
    q_bias = lax.dynamic_slice_in_dim(packs[:half, :qv], s * own, own, 0).reshape(1, C)
    v_bias = lax.dynamic_slice_in_dim(packs[half:, :qv], s * own, own, 0).reshape(1, C)
    qkv_bias = jnp.concatenate([q_bias, jnp.zeros((1, C), F32), v_bias], axis=1)
    bias_out = packs[:, qv : qv + rows].reshape(1, D)
    bias_two = packs[:, qv + rows : qv + 2 * rows].reshape(1, D)
    bias_one = lax.dynamic_index_in_dim(
        packs[:, qv + 2 * rows :].reshape(F, S, -1), s, 1, False
    ).reshape(1, hidden)
    full_qkv = g_qkv.reshape(D, 3 * C)
    full_one = g_one.reshape(D, hidden)
    full_two = g_two.reshape(hidden, D)
    full_out = g_out.reshape(D, D)
    mixed_all, heads, log_sums, merged, branch_one, mixed_two = attend(
        sizes, mixed, full_qkv, qkv_bias, mod, tokens, full_out, bias_out
    )
    (
        block_out,
        grad_resid,
        grad_heads,
        one_g,
        two_g,
        out_g,
        grad_b_one,
        grad_b_two,
        grad_b_out,
        mod_sums,
    ) = mlp(
        sizes,
        mixed_two,
        cotangent[0],
        mod,
        full_one,
        bias_one,
        full_two,
        bias_two,
        branch_one,
        tokens,
        full_out,
        merged,
    )
    grad_latents, qkv_g, grad_b_qkv, mod_sums = attend_back(
        sizes, grad_heads, heads, log_sums, mixed_all, full_qkv, tokens, mod, grad_resid, mod_sums
    )
    o_qkv, o_one, o_two, o_out, o_ada, o_b_ada, o_small, o_cond = sums(
        sizes,
        qkv_g.reshape(G, rows, 3 * C),
        one_g.reshape(G, rows, hidden),
        two_g.reshape(F, 2, two_rows // 2, D),
        out_g.reshape(F, S, rows, D),
        mod_sums,
        grad_b_one,
        grad_b_two,
        grad_b_out,
        grad_b_qkv,
        silu_all,
        w_ada,
        cond,
    )
    small = o_small[0]
    return (
        block_out[None],
        grad_latents[None],
        o_cond,
        o_ada,
        o_b_ada[0],
        o_qkv,
        small[:qv],
        o_out,
        small[qv : qv + rows],
        o_one,
        small[qv + 2 * rows :],
        o_two.reshape(two_rows, D),
        small[qv + rows : qv + 2 * rows],
    )


def solution(mesh):
    owned = P(("fsdp", "seq"), None)
    owned_bias = P(("fsdp", "seq"))
    token_spec = P(("rep", "fsdp"), "seq", None)
    cond_spec = P(("rep", "fsdp"), None)
    weights = (owned, owned_bias) * 5
    in_specs = (token_spec, cond_spec) + weights + (token_spec,)
    out_specs = (token_spec, token_spec, cond_spec) + weights
    return jax.shard_map(
        on_device, mesh=mesh, in_specs=in_specs, out_specs=out_specs, check_vma=False
    )
```

time: 3250 us -> 610 us (0.19)
  blocking collectives: 1500 us -> 0 us
  local copies, waits for them, and re-layouts: 984 us -> 31.1 us
  Pallas kernels: 0 us -> 569 us
  other arithmetic: 434 us -> 2.08 us
  waiting for transfers between devices: 145 us -> 0 us
  matrix products: 128 us -> 0 us
    unnamed x2 -> x0, blocking collectives: 1400 us -> none
    pallas_call x0 -> x5, Pallas kernels: none -> 569 us  [the longest x1 177 us: sums(): pl.pallas_call(lambda *refs: sums_kernel(sizes, *refs), name='sums', out_...]
    unnamed x5 -> x0, other arithmetic: 407 us -> none
    unnamed x127 -> x56, local copies, waits for them, and re-layouts: 428 us -> 23.2 us
    all_to_all x9 -> x0, local copies, waits for them, and re-layouts: 190 us -> none  [the longest x2 104 us: on_device(): lax.all_to_all(stacked, 'seq', split_axis=3, concat_axis=2, tiled=True)]
    reshape x18 -> x6, local copies, waits for them, and re-layouts: 178 us -> 2.24 us  [the longest x1 0.69 us: on_device(): bias_two = packs[:, qv + rows:qv + 2 * rows].reshape(1, D)]
    another operation x10 -> x0, local copies, waits for them, and re-layouts: 146 us -> none  [the longest x4 78 us: on_device(): jnp.stack([grad_queries, grad_keys, grad_vals]).astype(jnp.bfloat16)]
    dot_general x29 -> x0, matrix products: 128 us -> none  [the longest x5 36.1 us: outer_dot(): lax.dot_general(left, grad, (((0,), (0,)), ((), ())), preferred_element_t...]
  transfers between devices with their start and end apart: 10 -> 0, of which waited for: 4 -> 0; matrix products, arithmetic and copies ran while one was open for 28% -> 0% of each run, Pallas kernels for 0% -> 0%
where the time goes in v1:
time: 610 us; the launch traced here: 603 us
  Pallas kernels  569 us (93%)
  local copies, waits for them, and re-layouts  31.1 us (5%)
    pallas_call x1, Pallas kernels, sums(): pl.pallas_call(lambda *refs: sums_kernel(sizes, *refs), name='sums', out_...  177 us
    pallas_call x1, Pallas kernels, front(): pl.pallas_call(lambda *refs: front_kernel(sizes, *refs), name='front', ou...  173 us
    pallas_call x1, Pallas kernels, mlp(): pl.pallas_call(lambda *refs: mlp_kernel(sizes, *refs), name='mlp', out_sh...  113 us
    pallas_call x1, Pallas kernels, attend_back(): pl.pallas_call(lambda *refs: attend_back_kernel(sizes, *refs), name='atte...  54.9 us
    pallas_call x1, Pallas kernels, attend(): pl.pallas_call(lambda *refs: attend_kernel(sizes, *refs), name='attend',...  50.8 us
    unnamed x56, local copies, waits for them, and re-layouts  23.2 us

profile of v1, /device:TPU:0, one launch (start us, length us, event | category | flops | bytes accessed | tf_op | source)
XLA Modules:
  0.0 602.5 jit_solution(17054570808710994218)
XLA Ops:
  0.7 0.7 concatenate.21
  1.3 0.7 concatenate.24
  2.0 0.7 maximum_convert_fusion.refs_8_
  2.7 0.7 broadcast_in_dim.24
  3.4 0.1 pad.1.clone
  3.5 0.2 dynamic_update_slice.4.refs_2_
  3.7 0.0 copy-start.1
  3.7 1.1 copy-done.1
  4.8 1.2 copy-done.3
  6.0 0.0 copy-start.6
  6.0 1.1 copy-done.6
  7.1 0.0 copy-start.7
  7.1 1.1 copy-done.7
  8.2 0.0 copy-start.9
  8.2 1.0 copy-done.9
  9.2 0.9 copy-done.11
  10.1 0.0 copy-start.12
  10.1 0.7 copy-done.12
  10.8 173.1 %front.1 = (bf16[256,1152]{1,0:T(8,128)(2,1)S(1)}, f32[6,1152]{1,0:T(8,128)S(1)}, f32[8,1,72]{2,1,0:T(1,128)S(1)}, f32[16,1,576]{2,1,0:T(1,128)S(1)}, bf16[16,72...) custom-call(bf16[1,1152]{1,0:T(2,128)(2,1)S(1)} %copy-done.12, ...), custom_call_target="tpu_custom_call" | custom-call | tf_op jit(solution)/shard_map/front/pallas_call | solution.py:456
  183.9 0.0 copy-start
  183.9 1.6 copy-done
  185.5 1.3 copy-done.2
  186.8 1.5 copy-done.4
  188.3 1.5 copy-done.5
  189.8 0.8 copy-done.8
  190.7 0.6 copy-done.10
  191.3 0.6 copy-done.13
  191.9 0.1 fusion.1
  191.9 0.7 reshape.147.refs_6_
  192.6 0.7 reshape.142.refs_6_
  193.3 0.1 slice.55
  193.4 0.7 reshape.145.refs_4_
  194.1 0.1 reshape.140
  194.2 0.1 reshape.139
  194.3 0.7 fusion.refs_2_
  195.0 50.8 %attend.1 = (bf16[4,256,1152]{2,1,0:T(8,128)(2,1)}, bf16[12,1024,128]{2,1,0:T(8,128)(2,1)}, f32[4,4,1,256]{3,2,1,0:T(1,128)}, bf16[256,1152]{1,0:T(8,128)(2,1)},...) custom-call(bf16[256,1152]{1,0:T(8,128)(2,1)} %copy-done.8, bf16[1152,864]{1,0:T(8,128)(2,1)} %bitcast.32, ...), custom_call_target="tpu_custom_call" | custom-call | tf_op jit(solution)/shard_map/attend/pallas_call | solution.py:605
  245.7 113.1 %mlp.1 = (bf16[256,1152]{1,0:T(8,128)(2,1)}, f32[256,1152]{1,0:T(8,128)}, bf16[4,256,288]{2,1,0:T(8,128)(2,1)}, bf16[1152,1152]{1,0:T(8,128)(2,1)}, bf16[1152,11...) custom-call(bf16[256,1152]{1,0:T(8,128)(2,1)} %get-tuple-element.54., ...), custom_call_target="tpu_custom_call" | custom-call | tf_op jit(solution)/shard_map/mlp/pallas_call | solution.py:826
  358.8 54.9 %attend_back.1 = (f32[256,1152]{1,0:T(8,128)}, bf16[1152,864]{1,0:T(8,128)(2,1)}, f32[1,864]{1,0:T(1,128)}, f32[6,1152]{1,0:T(8,128)}) custom-call(bf16[4,256,288]{2,1,0:T(8,128)(2,1)} %get-tuple-element.60.refs_0_, bf16[12,1024,128]{2,1,0:T(8,128)(2,1)} %get-tuple-element.61.refs_1_, f32[4,4,1,256]{3,2,1,0:T(1,128)} %get-tuple-element.62.refs_2_, ...), custom_call_target="tpu_custom_call" | custom-call | tf_op jit(solution)/shard_map/attend_back/pallas_call | solution.py:995
  413.7 0.0 copy-start.19
  413.7 0.0 copy-start.17
  413.7 176.7 %sums.1 = (f32[72,3456]{1,0:T(8,128)}, f32[72,4608]{1,0:T(8,128)}, f32[2,144,1152]{2,1,0:T(8,128)}, f32[72,1152]{1,0:T(8,128)}, f32[72,6912]{1,0:T(8,128)}, /*in...) custom-call(bf16[16,72,864]{2,1,0:T(8,128)(2,1)} %bitcast.40, bf16[16,72,1152]{2,1,0:T(8,128)(2,1)} %bitcast.37, ...), custom_call_target="tpu_custom_call" | custom-call | tf_op jit(solution)/shard_map/sums/pallas_call | solution.py:1490
  590.5 0.0 copy-start.21
  590.5 0.0 copy-start.14
  590.5 1.4 slice.44
  591.8 1.2 slice_bitcast_fusion
  593.1 1.3 slice_reduce_fusion
  594.4 0.0 copy-done.19
  594.4 0.8 copy.41
  595.2 0.0 copy-done.17
  595.2 1.0 copy.42
  596.3 0.0 copy-done.21
  596.3 0.6 copy.43
  596.9 0.0 copy-done.14
  596.9 1.3 copy.44
  598.1 0.0 copy-done.22
  598.1 0.6 copy.45
  598.7 0.0 copy-done.18
  598.7 0.9 copy.46
  599.7 0.0 copy-done.20
  599.7 0.7 copy.47
  600.4 0.0 copy-done.16
  600.4 1.1 copy.48
  601.5 0.0 copy-done.15
  601.5 1.1 copy.49
  (20 shorter events, 0.1 us)
Async XLA Ops:
  3.7 1.1 copy-start.1
  4.8 1.2 copy-start.3
  6.0 1.1 copy-start.6
  7.1 1.1 copy-start.7
  8.2 1.0 copy-start.9
  9.2 0.9 copy-start.11
  10.1 0.7 copy-start.12
  183.9 1.6 copy-start
  185.5 1.4 copy-start.2
  186.8 1.5 copy-start.4
  188.3 1.5 copy-start.5
  189.8 0.8 copy-start.8
  190.7 0.6 copy-start.10
  191.3 0.6 copy-start.13
  413.7 180.7 %copy-start.19 = (bf16[256,1152]{1,0:T(8,128)(2,1)S(1)}, bf16[256,1152]{1,0:T(8,128)(2,1)}, u32[]{:S(2)}) copy-start(bf16[256,1152]{1,0:T(8,128)(2,1)} %get-tuple-element.59) | copy-start | bytes 1769476
  413.7 181.5 %copy-start.17 = (f32[256,1152]{1,0:T(8,128)S(1)}, f32[256,1152]{1,0:T(8,128)}, u32[]{:S(2)}) copy-start(f32[256,1152]{1,0:T(8,128)} %get-tuple-element.66) | copy-start | bytes 3538948
  590.5 5.8 copy-start.21
  590.5 6.4 %copy-start.14 = (f32[72,6912]{1,0:T(8,128)S(1)}, f32[72,6912]{1,0:T(8,128)}, u32[]{:S(2)}) copy-start(f32[72,6912]{1,0:T(8,128)} %get-tuple-element.109) | copy-start | bytes 5971972
  596.3 1.9 copy-start.22
  596.3 2.5 copy-start.18
  596.9 2.8 copy-start.20
  598.1 2.3 copy-start.16
  599.7 1.8 copy-start.15

commit v2 on v1

--- a/solution.py
+++ b/solution.py
@@ -118,6 +118,119 @@
 
     def flip(self):
         return {"rep": 1 - self.y}
+
+    def peer(self, j):
+        return lax.bitwise_xor(self.s, j)
+
+
+class SeqGather:
+    def __init__(self, at, dst, sem):
+        self.at, self.dst, self.sem = at, dst, sem
+
+    @staticmethod
+    def scratch(S):
+        return DMA((4, S))
+
+    def direct(self, j):
+        at, block = self.at, self.dst.at[self.at.s]
+        return remote(block, block, self.sem.at[0, j], self.sem.at[1, j], {"seq": at.peer(j)})
+
+    def handed(self, j):
+        at = self.at
+        block = self.dst.at[at.peer(j)]
+        return remote(block, block, self.sem.at[2, j], self.sem.at[3, j], {"seq": at.peer(1)})
+
+    def start(self):
+        for j in range(3, self.at.S, 2):
+            self.direct(j).start()
+        self.direct(1).start()
+
+    def arrive(self, index):
+        @pl.when(index == 1)
+        def _():
+            self.direct(1).wait()
+
+        if self.at.S > 2:
+
+            @pl.when((index >= 2) & (lax.rem(index, 2) == 0))
+            def _():
+                self.direct(index + 1).wait()
+                self.handed(index + 1).start()
+
+            @pl.when((index >= 2) & (lax.rem(index, 2) == 1))
+            def _():
+                self.handed(index).wait()
+
+
+def arrival(index):
+    return jnp.where(index < 2, index, lax.bitwise_xor(index, 1))
+
+
+class SeqSum:
+    def __init__(self, at, src, near, inn, sem):
+        self.at, self.src, self.near, self.inn, self.sem = at, src, near, inn, sem
+
+    @staticmethod
+    def scratch(S, rows, cols):
+        return [
+            pltpu.VMEM((S, rows, cols), BF),
+            pltpu.VMEM((S // 2, rows, cols), BF),
+            pltpu.VMEM((S // 2, rows, cols), BF),
+            DMA((4, S)),
+        ]
+
+    def sibling(self, j):
+        at = self.at
+        return remote(
+            self.src.at[at.peer(j)],
+            self.near.at[j // 2],
+            self.sem.at[0, j],
+            self.sem.at[1, j],
+            {"seq": at.peer(1)},
+        )
+
+    def direct(self, j):
+        at = self.at
+        return remote(
+            self.src.at[at.peer(j)],
+            self.inn.at[j // 2],
+            self.sem.at[2, j],
+            self.sem.at[3, j],
+            {"seq": at.peer(j)},
+        )
+
+    def send(self, index):
+        @pl.when((index == 1) | ((index >= 2) & (lax.rem(index, 2) == 0)))
+        def _():
+            self.sibling(lax.bitwise_or(index, 1)).start()
+
+        if self.at.S > 2:
+
+            @pl.when((index >= 2) & (lax.rem(index, 2) == 1))
+            def _():
+                j = index - 1
+                self.sibling(index).wait()
+                t = self.at.peer(j)
+                step = min(64, self.src.shape[1])
+
+                def add(i):
+                    rows = pl.ds(pl.multiple_of(i * step, step), step)
+                    both = self.src[t, rows, :].astype(F32) + self.near[j // 2, rows, :].astype(F32)
+                    self.src[t, rows, :] = both.astype(BF)
+
+                each(0, self.src.shape[1] // step, add)
+                self.direct(j).start()
+
+    def wait(self):
+        self.sibling(1).wait()
+        for j in range(2, self.at.S, 2):
+            self.direct(j).wait()
+
+    def total(self, rows):
+        value = self.src[self.at.s, rows, :].astype(F32) + self.near[0, rows, :].astype(F32)
+        for k in range(1, self.at.S // 2):
+            value = value + self.inn[k, rows, :].astype(F32)
+        return value
 
 
 class ColumnGather:
@@ -286,56 +399,32 @@
         each(1, at.F, lambda i: await_bytes(src, sem.at[1, i]))
 
 
-def front_kernel(
-    sizes,
-    cond,
-    w_ada,
-    bias_slot,
-    latents,
-    w_qkv,
-    w_one,
-    w_two,
-    w_out,
-    bias_pack,
-    mixed,
-    mod,
-    silu_all,
-    pack_all,
-    g_qkv,
-    g_one,
-    g_two,
-    g_out,
-    silu_src,
-    part,
-    parts_in,
-    mod_src,
-    mod_in,
-    qkv_src,
-    one_src,
-    silu_sem,
-    part_sem,
-    mod_sem,
-    pack_sem,
-    qkv_sem,
-    one_sem,
-    two_sem,
-    out_sem,
-):
+def forward_kernel(sizes, *refs):
     at = Place(sizes)
     R, F, S, G = at.R, at.F, at.S, at.G
-    D = latents.shape[1]
+    cond, w_ada, bias_slot, latents, cotangent, w_qkv, w_one, bias_pack, w_two, w_out = refs[:10]
+    mixed_all, heads, log_sums, merged, branch_one, mixed_two = refs[10:16]
+    mod, silu_all, grad_all, full_qkv, full_out, bias_one, bias_two, g_one, g_two = refs[16:25]
+    silu_src, part, parts_in, mod_src, mod_in, qkv_src, one_src, pack_all = refs[25:33]
+    g_qkv, g_out, wide, bias_qkv, bias_out, val_flip, att, merged_in = refs[33:41]
+    silu_sem, part_sem, mod_sem, pack_sem, qkv_sem, one_sem, two_sem, out_sem = refs[41:49]
+    mixed_sem, grad_sem, att_sem = refs[49:52]
+    L, D = latents.shape
     C = D // S
-    rows = silu_all.shape[2]
-    block = one_src.shape[2] // F
+    T = S * L
+    local_heads = H // S
+    size = D // H
+    rows_own = silu_all.shape[2]
+    hidden = one_src.shape[2]
+    block = hidden // F
     greet(G, lambda i: {"fsdp": lax.rem(at.me + i, G) // S, "seq": lax.rem(at.me + i, S)})
     greet(2 * F, lambda i: {"rep": lax.rem(at.y + i // F, 2), "fsdp": at.zs(i)})
-    gate = pltpu.get_barrier_semaphore()
-    pl.semaphore_wait(gate, G - 1 + 2 * F - 1)
+    greet_wait(G - 1 + 2 * F - 1)
 
     value = cond[...].astype(F32)
     silu = (value * jax.nn.sigmoid(value)).astype(BF).astype(F32)
     for g in range(G):
-        silu_src[g] = silu[:, g * rows : (g + 1) * rows]
+        silu_src[g] = silu[:, g * rows_own : (g + 1) * rows_own]
     slot = at.y * F + at.z
 
     def cond_copy(i):
@@ -349,7 +438,7 @@
         )
 
     each(1, 2 * F, lambda i: cond_copy(i).start())
-    local(silu_src.at[at.me], silu_all.at[slot], silu_sem.at[0, 0]).start()
+    silu_all[slot] = silu_src[at.me]
 
     def pack_copy(i):
         to = lax.rem(at.me + i, G)
@@ -361,26 +450,22 @@
             {"fsdp": to // S, "seq": lax.rem(to, S)},
         )
 
-    local(bias_pack, pack_all.at[at.me], pack_sem.at[2, 0]).start()
     each(1, G, lambda i: pack_copy(i).start())
-
-    for t in range(S):
-        for j in range(3):
-            qkv_src[t, :, j * C : (j + 1) * C] = w_qkv[:, j * D + t * C : j * D + (t + 1) * C]
+    pack_all[at.me] = bias_pack[...]
+
     qkv = ColumnGather(at, qkv_src, g_qkv, qkv_sem)
     one = ColumnGather(at, one_src, g_one, one_sem)
     two = RowGather(at, w_two, g_two, two_sem)
     out = FullGather(at, w_out, g_out, out_sem)
+    for t in range(S):
+        for j in range(3):
+            qkv_src[t, :, j * C : (j + 1) * C] = w_qkv[:, j * D + t * C : j * D + (t + 1) * C]
     qkv.start()
-    out.start()
     for t in range(S):
         for f in range(F):
             col = (f * S + t) * block
             one_src[t, :, f * block : (f + 1) * block] = w_one[:, col : col + block]
-    one.start()
-    two.start()
-
-    local(silu_src.at[at.me], silu_all.at[slot], silu_sem.at[0, 0]).wait()
+
     each(1, 2 * F, lambda i: cond_copy(i).wait())
     left = jnp.concatenate([silu_all[at.y * F + f] for f in range(F)], axis=0).astype(BF)
     sums = mm(left, w_ada[...]) + bias_slot[...]
@@ -401,8 +486,7 @@
         )
 
     each(1, G, lambda i: part_copy(i).start())
-    local(part.at[at.me], parts_in.at[at.me], part_sem.at[0, 0]).start()
-    local(part.at[at.me], parts_in.at[at.me], part_sem.at[0, 0]).wait()
+    parts_in[at.me] = part[at.me]
     each(1, G, lambda i: part_copy(i).wait())
     total = parts_in[0]
     for g in range(1, G):
@@ -420,54 +504,156 @@
     for t in range(S):
         mod[:, t * C : (t + 1) * C] = mod_in[t]
 
-    shift = mod[0:1, :]
-    scale = mod[1:2, :]
-    step = min(64, latents.shape[0])
+    step = min(64, L)
 
     def norm(i):
-        at_rows = pl.ds(i * step, step)
+        at_rows = pl.ds(pl.multiple_of(i * step, step), step)
         normed, _ = norm_stats(latents[at_rows, :].astype(F32))
-        mixed[at_rows, :] = (normed * (1.0 + scale) + shift).astype(BF)
-
-    each(0, latents.shape[0] // step, norm)
-
-    local(bias_pack, pack_all.at[at.me], pack_sem.at[2, 0]).wait()
+        mixed_all[at.s, at_rows, :] = (normed * (1.0 + mod[1:2, :]) + mod[0:1, :]).astype(BF)
+
+    each(0, L // step, norm)
+    gather = SeqGather(at, mixed_all, mixed_sem)
+    gather.start()
+    out.start()
+
     others = pack_all.at[pl.ds(0, G - 1)]
     await_bytes(others, pack_sem.at[0, 0])
     await_bytes(others, pack_sem.at[1, 0])
+    qv = 2 * D // G
+    own = F // 2
+    bias_qkv[...] = jnp.zeros_like(bias_qkv)
+    for i in range(own):
+        bias_qkv[:, i * qv : (i + 1) * qv] = pack_all[at.s * own + i][:, 0:qv]
+        bias_qkv[:, 2 * C + i * qv : 2 * C + (i + 1) * qv] = pack_all[G // 2 + at.s * own + i][
+            :, 0:qv
+        ]
+    for g in range(G):
+        cols = slice(g * rows_own, (g + 1) * rows_own)
+        bias_out[:, cols] = pack_all[g][:, qv : qv + rows_own]
+        bias_two[:, cols] = pack_all[g][:, qv + rows_own : qv + 2 * rows_own]
+    for f in range(F):
+        bias_one[:, f * block : (f + 1) * block] = pack_all[f * S + at.s][:, qv + 2 * rows_own :]
+
     qkv.forward()
+    one.start()
+    two.start()
+    grad_all[at.s] = (mod[5:6, :] * cotangent[...].astype(F32)).astype(BF)
+    grad_gather = SeqGather(at, grad_all, grad_sem)
+    grad_gather.start()
+    qkv.finish()
+
+    def join(slabs, whole):
+        cols = whole.shape[1]
+        for g in range(G):
+            wide[g * rows_own : (g + 1) * rows_own, 0:cols] = slabs(g).astype(F32)
+        tall = 128 if D % 128 == 0 else D
+
+        def cast(i):
+            at_rows = pl.ds(pl.multiple_of(i * tall, tall), tall)
+            whole[at_rows, :] = wide[at_rows, 0:cols].astype(BF)
+
+        each(0, D // tall, cast)
+
+    join(lambda g: g_qkv[g], full_qkv)
+
+    pad = jnp.zeros((L, LANES - size), BF)
+
+    def project(index):
+        gather.arrive(index)
+        t = at.peer(arrival(index))
+        at_rows = pl.ds(pl.multiple_of(t * L, L), L)
+        done = (mm(mixed_all[t], full_qkv[...]) + bias_qkv[...]).astype(BF)
+        for c in range(3 * local_heads):
+            heads[c, at_rows, :] = jnp.concatenate(
+                [done[:, c * size : (c + 1) * size], pad], axis=1
+            )
+
+    each(0, S, project)
     out.forward()
+    for h in range(local_heads):
+        val_flip[h] = heads[2 * local_heads + h].T
+
+    def att_copy(j):
+        t = at.peer(j)
+        return remote(
+            att.at[t], merged_in.at[at.s], att_sem.at[0, j], att_sem.at[1, j], {"seq": t}
+        )
+
+    factor = size ** (-0.5) * log2e
+
+    def attention(index):
+        j = S - 1 - index
+        t = at.peer(j)
+        at_rows = pl.ds(pl.multiple_of(t * L, L), L)
+        for h in range(local_heads):
+            scores = mm_nt(heads[local_heads + h], heads[h, at_rows, :]) * factor
+            highest = jnp.max(scores, axis=0, keepdims=True)
+            raised = jnp.exp2(scores - highest)
+            summed = jnp.sum(raised, axis=0, keepdims=True)
+            result = mm(val_flip[h], raised.astype(BF)) / summed
+            log_sums[h, t] = highest + jnp.log2(summed)
+            att[t, :, h * size : (h + 1) * size] = result.T[:, :size].astype(BF)
+
+        @pl.when(j > 0)
+        def _():
+            att_copy(j).start()
+
+    each(0, S, attention)
+    merged_in[at.s] = att[at.s]
+    out.finish()
+    join(lambda g: g_out[g // S, g % S], full_out)
     one.forward()
+    each(1, S, lambda j: att_copy(j).wait())
+    for t in range(S):
+        merged[:, t * C : (t + 1) * C] = merged_in[t]
+
+    def project_out(i):
+        at_rows = pl.ds(pl.multiple_of(i * step, step), step)
+        branch = mm(merged[at_rows, :], full_out[...]) + bias_out[...]
+        branch_one[at_rows, :] = branch
+        residual = latents[at_rows, :].astype(F32) + mod[2:3, :] * branch
+        normed, _ = norm_stats(residual)
+        mixed_two[at_rows, :] = (normed * (1.0 + mod[4:5, :]) + mod[3:4, :]).astype(BF)
+
+    each(0, L // step, project_out)
+    each(1, S, grad_gather.arrive)
     two.forward()
-    qkv.finish()
-    out.finish()
     one.finish()
     two.finish()
 
 
-def front(sizes, cond, w_ada, bias_slot, latents, w_qkv, w_one, w_two, w_out, bias_pack):
+def forward(sizes, cond, w_ada, bias_slot, latents, cotangent, w_qkv, w_one, bias_pack, w_two, w_out):
     R, F, S = sizes
     G = F * S
-    rows, width = w_out.shape
-    C = width // S
+    rows, D = w_out.shape
+    L = latents.shape[0]
+    T = S * L
+    C = D // S
+    local_heads = H // S
     hidden = w_one.shape[1] // S
-    length = latents.shape[0]
     shape = jax.ShapeDtypeStruct
     return pl.pallas_call(
-        lambda *refs: front_kernel(sizes, *refs),
-        name="front",
+        lambda *refs: forward_kernel(sizes, *refs),
+        name="forward",
         out_shape=(
-            shape((length, width), BF),
-            shape((6, width), F32),
+            shape((S, L, D), BF),
+            shape((3 * local_heads, T, LANES), BF),
+            shape((local_heads, S, 1, L), F32),
+            shape((L, D), BF),
+            shape((L, D), F32),
+            shape((L, D), BF),
+            shape((6, D), F32),
             shape((R * F, 1, rows), F32),
-            shape((G,) + bias_pack.shape, F32),
-            shape((G, rows, 3 * C), BF),
+            shape((S, L, D), BF),
+            shape((D, 3 * C), BF),
+            shape((D, D), BF),
+            shape((1, hidden), F32),
+            shape((1, D), F32),
             shape((G, rows, hidden), BF),
             shape((F,) + w_two.shape, BF),
-            shape((F, S) + w_out.shape, BF),
         ),
-        in_specs=[VM, VM, VM, VM, VM, VM, HB, HB, VM],
-        out_specs=(VM, VM, VM, VM, HB, HB, HB, HB),
+        in_specs=[VM] * 8 + [HB] * 2,
+        out_specs=(VM,) * 13 + (HB,) * 2,
         scratch_shapes=[
             pltpu.VMEM((G, 1, rows), F32),
             pltpu.VMEM((G, 6, C), F32),
@@ -476,159 +662,35 @@
             pltpu.VMEM((S, 6, C), F32),
             pltpu.VMEM((S, rows, 3 * C), BF),
             pltpu.VMEM((S, rows, hidden), BF),
+            pltpu.VMEM((G,) + bias_pack.shape, F32),
+            pltpu.VMEM((G, rows, 3 * C), BF),
+            pltpu.VMEM((F, S, rows, D), BF),
+            pltpu.VMEM((D, max(D, 3 * C)), F32),
+            pltpu.VMEM((1, 3 * C), F32),
+            pltpu.VMEM((1, D), F32),
+            pltpu.VMEM((local_heads, LANES, T), BF),
+            pltpu.VMEM((S, L, C), BF),
+            pltpu.VMEM((S, L, C), BF),
             DMA((2, 2 * F)),
             DMA((2, G)),
             DMA((2, S)),
-            DMA((3, 1)),
+            DMA((2, 1)),
             ColumnGather.scratch(F),
             ColumnGather.scratch(F),
             RowGather.scratch(F),
             FullGather.scratch(F),
-        ],
-        compiler_params=params(1, 40),
-    )(cond, w_ada, bias_slot, latents, w_qkv, w_one, w_two, w_out, bias_pack)
-def attend_kernel(
-    sizes,
-    mixed,
-    w_qkv,
-    bias,
-    mod,
-    latents,
-    w_out,
-    bias_out,
-    mixed_all,
-    heads,
-    log_sums,
-    merged,
-    branch_one,
-    mixed_two,
-    val_flip,
-    att,
-    merged_in,
-    mix_sem,
-    att_sem,
-):
-    at = Place(sizes)
-    S = at.S
-    L, D = mixed.shape
-    C = D // S
-    T = S * L
-    local_heads = H // S
-    size = D // H
-    greet_wait(greet(S, lambda i: {"seq": at.ss(i)}))
-
-    def mix_copy(j):
-        return remote(
-            mixed,
-            mixed_all.at[at.s],
-            mix_sem.at[0, j],
-            mix_sem.at[1, j],
-            {"seq": lax.bitwise_xor(at.s, j)},
-        )
-
-    each(1, S, lambda j: mix_copy(j).start())
-    mixed_all[at.s] = mixed[...]
-
-    pad = jnp.zeros((L, LANES - size), BF)
-
-    def project(j):
-        t = lax.bitwise_xor(at.s, j)
-
-        @pl.when(j > 0)
-        def _():
-            mix_copy(j).wait()
-
-        rows = pl.ds(pl.multiple_of(t * L, L), L)
-        done = (mm(mixed_all[t], w_qkv[...]) + bias[...]).astype(BF)
-        for c in range(3 * local_heads):
-            heads[c, rows, :] = jnp.concatenate([done[:, c * size : (c + 1) * size], pad], axis=1)
-
-    each(0, S, project)
-
-    for h in range(local_heads):
-        val_flip[h] = heads[2 * local_heads + h].T
-
-    def att_copy(j):
-        t = lax.bitwise_xor(at.s, j)
-        return remote(
-            att.at[t], merged_in.at[at.s], att_sem.at[0, j], att_sem.at[1, j], {"seq": t}
-        )
-
-    factor = size ** (-0.5) * log2e
-
-    def attention(index):
-        j = S - 1 - index
-        t = lax.bitwise_xor(at.s, j)
-        rows = pl.ds(pl.multiple_of(t * L, L), L)
-        for h in range(local_heads):
-            scores = mm_nt(heads[local_heads + h], heads[h, rows, :]) * factor
-            highest = jnp.max(scores, axis=0, keepdims=True)
-            raised = jnp.exp2(scores - highest)
-            summed = jnp.sum(raised, axis=0, keepdims=True)
-            result = mm(val_flip[h], raised.astype(BF)) / summed
-            log_sums[h, t] = highest + jnp.log2(summed)
-            att[t, :, h * size : (h + 1) * size] = result.T[:, :size].astype(BF)
-
-        @pl.when(j > 0)
-        def _():
-            att_copy(j).start()
-
-    each(0, S, attention)
-    merged_in[at.s] = att[at.s]
-    each(1, S, lambda j: att_copy(j).wait())
-    for t in range(S):
-        merged[:, t * C : (t + 1) * C] = merged_in[t]
-
-    gate_one = mod[2:3, :]
-    shift = mod[3:4, :]
-    scale = mod[4:5, :]
-    step = min(64, L)
-
-    def project_out(i):
-        rows = pl.ds(pl.multiple_of(i * step, step), step)
-        branch = mm(merged[rows, :], w_out[...]) + bias_out[...]
-        branch_one[rows, :] = branch
-        residual = latents[rows, :].astype(F32) + gate_one * branch
-        normed, _ = norm_stats(residual)
-        mixed_two[rows, :] = (normed * (1.0 + scale) + shift).astype(BF)
-
-    each(0, L // step, project_out)
-
-
-def attend(sizes, mixed, w_qkv, bias, mod, latents, w_out, bias_out):
-    S = sizes[2]
-    L, D = mixed.shape
-    C = D // S
-    T = S * L
-    local_heads = H // S
-    shape = jax.ShapeDtypeStruct
-    return pl.pallas_call(
-        lambda *refs: attend_kernel(sizes, *refs),
-        name="attend",
-        out_shape=(
-            shape((S, L, D), BF),
-            shape((3 * local_heads, T, LANES), BF),
-            shape((local_heads, S, 1, L), F32),
-            shape((L, D), BF),
-            shape((L, D), F32),
-            shape((L, D), BF),
-        ),
-        in_specs=[VM] * 7,
-        out_specs=(VM,) * 6,
-        scratch_shapes=[
-            pltpu.VMEM((local_heads, LANES, T), BF),
-            pltpu.VMEM((S, L, C), BF),
-            pltpu.VMEM((S, L, C), BF),
-            DMA((2, S)),
+            SeqGather.scratch(S),
+            SeqGather.scratch(S),
             DMA((2, S)),
         ],
-        compiler_params=params(2, 60),
-    )(mixed, w_qkv, bias, mod, latents, w_out, bias_out)
+        compiler_params=params(1, 60),
+    )(cond, w_ada, bias_slot, latents, cotangent, w_qkv, w_one, bias_pack, w_two, w_out)
 
 
 def mlp_kernel(
     sizes,
     mixed_two,
+    grad_all,
     cotangent,
     mod,
     w_one,
@@ -650,18 +712,13 @@
     grad_b_out,
     mod_sums,
     mix_all,
-    grad_all,
     act_all,
     pre_all,
-    branch_src,
-    mix_src,
-    branch_in,
-    mix_in,
     grad_branch,
-    in_sem,
-    branch_sem,
-    mix_sem,
+    mixed_sem,
+    *rest,
 ):
+    branch_refs, mix_refs = rest[:4], rest[4:]
     at = Place(sizes)
     S = at.S
     L, D = mixed_two.shape
@@ -672,54 +729,17 @@
     scale = mod[4:5, :]
     gate_two = mod[5:6, :]
 
-    def peer(j):
-        return lax.bitwise_xor(at.s, j)
-
-    def mixed_copy(j):
-        return remote(
-            mixed_two, mix_all.at[at.s], in_sem.at[0, j], in_sem.at[1, j], {"seq": peer(j)}
-        )
-
-    def grad_copy(j):
-        return remote(
-            grad_all.at[at.s],
-            grad_all.at[at.s],
-            in_sem.at[2, j],
-            in_sem.at[3, j],
-            {"seq": peer(j)},
-        )
-
-    each(1, S, lambda j: mixed_copy(j).start())
-    grad_all[at.s] = (gate_two * cotangent[...].astype(F32)).astype(BF)
-    each(1, S, lambda j: grad_copy(j).start())
+    mixed_gather = SeqGather(at, mix_all, mixed_sem)
+    branch_sum = SeqSum(at, *branch_refs)
+    mix_sum = SeqSum(at, *mix_refs)
+    branch_src = branch_refs[0]
+    mix_src = mix_refs[0]
     mix_all[at.s] = mixed_two[...]
-
-    def branch_copy(j):
-        return remote(
-            branch_src.at[peer(j)],
-            branch_in.at[j],
-            branch_sem.at[0, j],
-            branch_sem.at[1, j],
-            {"seq": peer(j)},
-        )
-
-    def mix_copy(j):
-        return remote(
-            mix_src.at[peer(j)],
-            mix_in.at[j],
-            mix_sem.at[0, j],
-            mix_sem.at[1, j],
-            {"seq": peer(j)},
-        )
-
-    def block(j):
-        t = peer(j)
-
-        @pl.when(j > 0)
-        def _():
-            mixed_copy(j).wait()
-            grad_copy(j).wait()
-
+    mixed_gather.start()
+
+    def block(index):
+        mixed_gather.arrive(index)
+        t = at.peer(arrival(index))
         step = min(128, L)
 
         def part(i):
@@ -741,15 +761,10 @@
 
         each(0, L // step, part)
 
-        @pl.when(j > 0)
-        def _():
-            mix_copy(j).start()
-            branch_copy(j).start()
+        mix_sum.send(index)
+        branch_sum.send(index)
 
     each(0, S, block)
-
-    def flat(ref, cols):
-        return ref[:, :, cols].reshape(S * L, -1)
 
     step = 128 if hidden % 128 == 0 else hidden
     for i in range(hidden // step):
@@ -767,20 +782,14 @@
         ).astype(BF)
     grad_b_two[...] = jnp.sum(grad_all[at.s].astype(F32), axis=0, keepdims=True)
 
-    each(1, S, lambda j: mix_copy(j).wait())
+    mix_sum.wait()
     step = min(32, L)
     mod_sums[...] = jnp.zeros_like(mod_sums)
     grad_b_out[...] = jnp.zeros_like(grad_b_out)
 
-    def gather(src, incoming, rows):
-        total = src[at.s, rows, :].astype(F32)
-        for j in range(1, S):
-            total = total + incoming[j, rows, :].astype(F32)
-        return total
-
     def back(i):
         rows = pl.ds(pl.multiple_of(i * step, step), step)
-        grad_mixed = gather(mix_src, mix_in, rows)
+        grad_mixed = mix_sum.total(rows)
         branch = branch_one[rows, :]
         residual = latents[rows, :].astype(F32) + gate_one * branch
         normed, inv_std = norm_stats(residual)
@@ -803,11 +812,11 @@
         cols = slice(i * wide, (i + 1) * wide)
         grad_w_out[:, cols] = mm_tn(merged[...], grad_branch[:, cols]).astype(BF)
 
-    each(1, S, lambda j: branch_copy(j).wait())
+    branch_sum.wait()
 
     def finish(i):
         rows = pl.ds(pl.multiple_of(i * step, step), step)
-        branch_two = gather(branch_src, branch_in, rows) + bias_two[...]
+        branch_two = branch_sum.total(rows) + bias_two[...]
         residual = latents[rows, :].astype(F32) + gate_one * branch_one[rows, :]
         block_out[rows, :] = (residual + gate_two * branch_two).astype(BF)
         grad_out = cotangent[rows, :].astype(F32)
@@ -816,11 +825,11 @@
     each(0, L // step, finish)
 
 
-def mlp(sizes, mixed_two, cotangent, mod, w_one, b_one, w_two, b_two, branch, latents, w_out, merged):
+def mlp(sizes, mixed_two, *args):
     S = sizes[2]
     L, D = mixed_two.shape
     C = D // S
-    hidden = w_one.shape[1]
+    hidden = args[3].shape[1]
     shape = jax.ShapeDtypeStruct
     tokens = (S, L, D)
     return pl.pallas_call(
@@ -838,184 +847,21 @@
             shape((1, D), F32),
             shape((6, D), F32),
         ),
-        in_specs=[VM] * 11,
+        in_specs=[VM] * 12,
         out_specs=(VM,) * 10,
         scratch_shapes=[
             pltpu.VMEM(tokens, BF),
-            pltpu.VMEM(tokens, BF),
             pltpu.VMEM((S, L, hidden), BF),
             pltpu.VMEM((S, L, hidden), BF),
-            pltpu.VMEM(tokens, BF),
-            pltpu.VMEM(tokens, BF),
-            pltpu.VMEM(tokens, BF),
-            pltpu.VMEM(tokens, BF),
             pltpu.VMEM((L, D), BF),
-            DMA((4, S)),
-            DMA((2, S)),
-            DMA((2, S)),
-        ],
+            SeqGather.scratch(S),
+        ]
+        + SeqSum.scratch(S, L, D)
+        + SeqSum.scratch(S, L, D),
         compiler_params=params(3, 60),
-    )(mixed_two, cotangent, mod, w_one, b_one, w_two, b_two, branch, latents, w_out, merged)
-
-
-def attend_back_kernel(
-    sizes,
-    grad_heads,
-    heads,
-    log_sums,
-    mixed_all,
-    w_qkv,
-    latents,
-    mod,
-    grad_resid,
-    sums_in,
-    grad_latents,
-    grad_w_qkv,
-    grad_b_qkv,
-    mod_sums,
-    grad_in,
-    key_flip,
-    key_grad,
-    val_grad,
-    grad_proj,
-    mix_src,
-    mix_in,
-    in_sem,
-    mix_sem,
-):
-    at = Place(sizes)
-    S = at.S
-    _, L, C = grad_heads.shape
-    D = latents.shape[1]
-    local_heads = H // S
-    size = D // H
-    greet_wait(greet(S, lambda i: {"seq": at.ss(i)}))
-
-    def peer(j):
-        return lax.bitwise_xor(at.s, j)
-
-    def in_copy(j):
-        return remote(
-            grad_heads.at[peer(j)],
-            grad_in.at[at.s],
-            in_sem.at[0, j],
-            in_sem.at[1, j],
-            {"seq": peer(j)},
-        )
-
-    each(1, S, lambda j: in_copy(j).start())
-    grad_in[at.s] = grad_heads[at.s]
-    for h in range(local_heads):
-        key_flip[h] = heads[local_heads + h].T
-    key_grad[...] = jnp.zeros_like(key_grad)
-    val_grad[...] = jnp.zeros_like(val_grad)
-    factor = size ** (-0.5) * log2e
-    score_scale = size ** (-0.5)
-    pad = jnp.zeros((L, LANES - size), BF)
-
-    def block(j):
-        t = peer(j)
-
-        @pl.when(j > 0)
-        def _():
-            in_copy(j).wait()
-
-        rows = pl.ds(pl.multiple_of(t * L, L), L)
-        for h in range(local_heads):
-            query = heads[h, rows, :]
-            grad = jnp.concatenate([grad_in[t, :, h * size : (h + 1) * size], pad], axis=1)
-            scores = mm_nt(heads[local_heads + h], query) * factor
-            probs = jnp.exp2(scores - log_sums[h, t])
-            grad_probs = mm_nt(heads[2 * local_heads + h], grad)
-            inner = jnp.sum(probs * grad_probs, axis=0, keepdims=True)
-            grad_scores = (probs * (grad_probs - inner)).astype(BF)
-            query_grad = mm(key_flip[h], grad_scores) * score_scale
-            grad_proj[t, :, h * size : (h + 1) * size] = query_grad.T[:, :size].astype(BF)
-            key_grad[h] += mm(grad_scores, query)
-            val_grad[h] += mm(probs.astype(BF), grad)
-
-    each(0, S, block)
-    for h in range(local_heads):
-        low = (key_grad[h] * score_scale)[:, :size].astype(BF)
-        grad_proj[:, :, C + h * size : C + (h + 1) * size] = low.reshape(S, L, size)
-        low = val_grad[h][:, :size].astype(BF)
-        grad_proj[:, :, 2 * C + h * size : 2 * C + (h + 1) * size] = low.reshape(S, L, size)
-
-    def mix_copy(j):
-        return remote(
-            mix_src.at[peer(j)],
-            mix_in.at[j],
-            mix_sem.at[0, j],
-            mix_sem.at[1, j],
-            {"seq": peer(j)},
-        )
-
-    def spread(index):
-        j = S - 1 - index
-        t = peer(j)
-        mix_src[t] = mm_nt(grad_proj[t], w_qkv[...]).astype(BF)
-
-        @pl.when(j > 0)
-        def _():
-            mix_copy(j).start()
-
-    each(0, S, spread)
-    wide = 288 if C % 288 == 0 else C
-    tokens = mixed_all[...].reshape(S * L, D)
-    grads = grad_proj[...].reshape(S * L, 3 * C)
-    grad_w_qkv[...] = mm_tn(tokens, grads).astype(BF)
-    grad_b_qkv[...] = jnp.sum(grads.astype(F32), axis=0, keepdims=True)
-
-    each(1, S, lambda j: mix_copy(j).wait())
-    step = min(32, L)
-    mod_sums[...] = sums_in[...]
-    scale = mod[1:2, :]
-
-    def back(i):
-        rows = pl.ds(pl.multiple_of(i * step, step), step)
-        grad_mixed = mix_src[at.s, rows, :].astype(F32)
-        for j in range(1, S):
-            grad_mixed = grad_mixed + mix_in[j, rows, :].astype(F32)
-        normed, inv_std = norm_stats(latents[rows, :].astype(F32))
-        grad_latents[rows, :] = grad_resid[rows, :] + norm_back(
-            grad_mixed * (1.0 + scale), normed, inv_std
-        )
-        mod_sums[0:1, :] += jnp.sum(grad_mixed, axis=0, keepdims=True)
-        mod_sums[1:2, :] += jnp.sum(grad_mixed * normed, axis=0, keepdims=True)
-
-    each(0, L // step, back)
-
-
-def attend_back(sizes, grad_heads, heads, log_sums, mixed_all, w_qkv, latents, mod, grad_resid, sums):
-    S, L, C = grad_heads.shape
-    D = latents.shape[1]
-    T = S * L
-    local_heads = H // S
-    shape = jax.ShapeDtypeStruct
-    return pl.pallas_call(
-        lambda *refs: attend_back_kernel(sizes, *refs),
-        name="attend_back",
-        out_shape=(
-            shape((L, D), F32),
-            shape((D, 3 * C), BF),
-            shape((1, 3 * C), F32),
-            shape((6, D), F32),
-        ),
-        in_specs=[VM] * 9,
-        out_specs=(VM,) * 4,
-        scratch_shapes=[
-            pltpu.VMEM((S, L, C), BF),
-            pltpu.VMEM((local_heads, LANES, T), BF),
-            pltpu.VMEM((local_heads, T, LANES), F32),
-            pltpu.VMEM((local_heads, T, LANES), F32),
-            pltpu.VMEM((S, L, 3 * C), BF),
-            pltpu.VMEM((S, L, D), BF),
-            pltpu.VMEM((S, L, D), BF),
-            DMA((2, S)),
-            DMA((2, S)),
-        ],
-        compiler_params=params(4, 60),
-    )(grad_heads, heads, log_sums, mixed_all, w_qkv, latents, mod, grad_resid, sums)
+    )(mixed_two, *args)
+
+
 class ColumnScatter:
     def __init__(self, at, src, got, stage, inn, done, sem):
         self.at, self.src, self.got, self.stage = at, src, got, stage
@@ -1028,8 +874,7 @@
             pltpu.VMEM((F, S // 2, rows, cols), BF),
             pltpu.VMEM((F, S // 2, rows, cols), BF),
             pltpu.VMEM((F * S, rows, cols), BF),
-            pltpu.VMEM((S, rows, cols), BF),
-            DMA((6, F)),
+            DMA((7, F)),
         ]
 
     def start(self):
@@ -1039,6 +884,8 @@
             z_to = at.zs(i)
 
             def one(k):
+                slot = z_to * at.S + 2 * k + at.y
+                local(self.src.at[slot], self.stage.at[z_to, k], self.sem.at[6, i]).start()
                 remote(
                     self.src.at[z_to * at.S + 2 * k + 1 - at.y],
                     self.got.at[z_to, k],
@@ -1058,10 +905,11 @@
             i = lax.rem(index + 1, at.F)
             z_to = at.zs(i)
             await_bytes(self.got.at[0], self.sem.at[1, i])
+            await_bytes(self.got.at[0], self.sem.at[6, i])
 
             def one(k):
                 s_to = 2 * k + at.y
-                total = self.src[z_to * at.S + s_to].astype(F32) + self.got[z_to, k].astype(F32)
+                total = self.stage[z_to, k].astype(F32) + self.got[z_to, k].astype(F32)
                 low = total.astype(BF)
                 home = (i == 0) & (s_to == at.s)
                 self.stage[z_to, k] = low
@@ -1132,8 +980,7 @@
             pltpu.VMEM((F, rows, cols), BF),
             pltpu.VMEM((F, rows, cols), BF),
             pltpu.VMEM((F, rows, cols), BF),
-            pltpu.VMEM((2, rows, cols), BF),
-            DMA((6, F)),
+            DMA((7, F)),
         ]
 
     def start(self):
@@ -1141,6 +988,7 @@
 
         def far(i):
             z_to = at.zs(i)
+            local(self.src.at[z_to, at.y], self.stage.at[z_to], self.sem.at[6, i]).start()
             remote(
                 self.src.at[z_to, 1 - at.y],
                 self.got.at[z_to],
@@ -1168,7 +1016,8 @@
             i = lax.rem(index + 1, at.F)
             z_to = at.zs(i)
             await_bytes(self.got.at[0], self.sem.at[1, i])
-            total = self.src[z_to, at.y].astype(F32) + self.got[z_to].astype(F32)
+            await_bytes(self.got.at[0], self.sem.at[6, i])
+            total = self.stage[z_to].astype(F32) + self.got[z_to].astype(F32)
             self.stage[z_to] = total.astype(BF)
 
             @pl.when(i > 0)
@@ -1207,7 +1056,6 @@
             pltpu.VMEM((S, F, rows, cols), BF),
             pltpu.VMEM((F, rows, cols), BF),
             pltpu.VMEM((F, rows, cols), BF),
-            pltpu.VMEM((2, rows, cols), BF),
             DMA((6, max(F, S))),
         ]
 
@@ -1227,6 +1075,7 @@
             each(0, at.F, one)
 
         each(1, at.S, near)
+        local(self.src.at[:, at.s], self.stage, self.sem.at[0, 0]).start()
 
     def out_copy(self, i):
         at = self.at
@@ -1246,10 +1095,11 @@
             await_bytes(self.got.at[0], self.sem.at[1, j])
 
         each(1, at.S, arrived)
+        local(self.src.at[:, at.s], self.stage, self.sem.at[0, 0]).wait()
 
         def far(i):
             z_to = at.zs(i)
-            total = self.src[z_to, at.s].astype(F32)
+            total = self.stage[z_to].astype(F32)
             for j in range(1, at.S):
                 total = total + self.got[j, z_to].astype(F32)
             self.stage[z_to] = total.astype(BF)
@@ -1277,7 +1127,7 @@
 
 
 class Tail:
-    def __init__(self, at, sums, first_in, mod_src, mod_all, small_src, small_in, cond_src, cond_in, pieces, sem):
+    def __init__(self, at, mod_all, sums, first_in, mod_src, small_src, small_in, cond_src, cond_in, pieces, sem):
         self.at, self.sums, self.first_in = at, sums, first_in
         self.mod_src, self.mod_all = mod_src, mod_all
         self.small_src, self.small_in = small_src, small_in
@@ -1294,7 +1144,6 @@
             pltpu.VMEM((10, wide), F32),
             pltpu.VMEM((S, 10, wide), F32),
             pltpu.VMEM((6, D), BF),
-            pltpu.VMEM((R * F, 6, D), BF),
             pltpu.VMEM((F, 1, pack), F32),
             pltpu.VMEM((R * F, 1, pack), F32),
             pltpu.VMEM((R * F, 1, rows), F32),
@@ -1380,11 +1229,10 @@
             {"fsdp": to // at.S, "seq": lax.rem(to, at.S)},
         )
 
-    def owners(self, silu_all, w_ada, grad_w_ada, grad_b_ada, flat_sum, b_pieces, small_out):
+    def owners(self, w_ada, small_out):
         at = self.at
         F, G = at.F, at.G
         D = self.mod_src.shape[1]
-        width = grad_b_ada.shape[1]
 
         def arrive(i):
             first, second = self.wide_copies(i)
@@ -1401,14 +1249,6 @@
             self.cond_src[i] = cond[i : i + 1, :]
         each(1, G, lambda i: self.cond_copy(i).start())
         self.cond_in[at.me] = self.cond_src[at.y * F + at.z]
-        silu = silu_all[:, 0, :].astype(BF)
-        for v in range(6):
-            rows = self.mod_all[:, v, :]
-            grad_w_ada[:, v * D : (v + 1) * D] = mm_tn(silu, rows)
-            flat_sum[:, v * D : (v + 1) * D] = jnp.sum(rows.astype(F32), axis=0, keepdims=True)
-        for g in range(G):
-            b_pieces[g] = flat_sum[:, g * width : (g + 1) * width]
-        grad_b_ada[...] = b_pieces[at.me]
         total = self.small_in[0]
         for i in range(1, 2 * F):
             total = total + self.small_in[i]
@@ -1425,91 +1265,225 @@
             grad_cond[:, cols] = self.cond_in[g] * gate * (1.0 + value * (1.0 - gate))
 
 
-def sums_kernel(sizes, *refs):
+def backward_kernel(sizes, *refs):
     at = Place(sizes)
     R, F, S, G = at.R, at.F, at.S, at.G
-    qkv_g, one_g, two_g, out_g, mod_sums, b_one, b_two, b_out, b_qkv, silu_all, w_ada, cond = refs[:12]
-    o_qkv, o_one, o_two, o_out, o_ada, o_b_ada, o_small, o_cond = refs[12:20]
-    rest = list(refs[20:])
-    qkv = ColumnScatter(at, qkv_g, *rest[0:5])
-    one = ColumnScatter(at, one_g, *rest[5:10])
-    two = RowScatter(at, two_g, *rest[10:15])
-    out = FullScatter(at, out_g, *rest[15:20])
-    tail = Tail(at, *rest[20:30])
-    flat_sum, b_pieces = rest[30:32]
-    rows, D = o_out.shape
-    C = D // S
+    grad_heads, heads, log_sums, mixed_all, w_qkv, latents, mod, grad_resid, sums_in = refs[:9]
+    one_g, two_g, out_g, b_one, b_two, b_out, w_ada, cond = refs[9:17]
+    grad_latents, o_qkv, o_one, o_two, o_out, o_mod, o_small, o_cond = refs[17:25]
+    grad_in, key_flip, key_grad, val_grad, grad_proj, qkv_wide, qkv_g, mod_sums, b_qkv, in_sem = refs[25:35]
+    rest = list(refs[35:])
+    mix_sum = SeqSum(at, *rest[0:4])
+    mix_src = rest[0]
+    qkv = ColumnScatter(at, qkv_g, *rest[4:7], o_qkv, rest[7])
+    one = ColumnScatter(at, one_g, *rest[8:11], o_one, rest[11])
+    two = RowScatter(at, two_g, *rest[12:15], o_two, rest[15])
+    out = FullScatter(at, out_g, *rest[16:19], o_out, rest[19])
+    tail = Tail(at, o_mod, *rest[20:29])
+    _, L, C = grad_heads.shape
+    rows_own, D = o_out.shape[1:]
     hidden = one_g.shape[2]
+    local_heads = H // S
+    size = D // H
     greet(G, lambda i: {"fsdp": lax.rem(at.me + i, G) // S, "seq": lax.rem(at.me + i, S)})
     greet(2 * F, lambda i: {"rep": lax.rem(at.y + i // F, 2), "fsdp": at.zs(i)})
     greet_wait(G - 1 + 2 * F - 1)
+
+    def in_copy(j):
+        return remote(
+            grad_heads.at[at.peer(j)],
+            grad_in.at[at.s],
+            in_sem.at[0, j],
+            in_sem.at[1, j],
+            {"seq": at.peer(j)},
+        )
+
+    each(1, S, lambda j: in_copy(j).start())
+    two.start()
+    out.start()
+    one.start()
+    grad_in[at.s] = grad_heads[at.s]
+    for h in range(local_heads):
+        key_flip[h] = heads[local_heads + h].T
+    key_grad[...] = jnp.zeros_like(key_grad)
+    val_grad[...] = jnp.zeros_like(val_grad)
+    factor = size ** (-0.5) * log2e
+    score_scale = size ** (-0.5)
+    pad = jnp.zeros((L, LANES - size), BF)
+
+    def block(j):
+        t = at.peer(j)
+
+        @pl.when(j > 0)
+        def _():
+            in_copy(j).wait()
+
+        rows = pl.ds(pl.multiple_of(t * L, L), L)
+        for h in range(local_heads):
+            query = heads[h, rows, :]
+            grad = jnp.concatenate([grad_in[t, :, h * size : (h + 1) * size], pad], axis=1)
+            scores = mm_nt(heads[local_heads + h], query) * factor
+            probs = jnp.exp2(scores - log_sums[h, t])
+            grad_probs = mm_nt(heads[2 * local_heads + h], grad)
+            inner = jnp.sum(probs * grad_probs, axis=0, keepdims=True)
+            grad_scores = (probs * (grad_probs - inner)).astype(BF)
+            query_grad = mm(key_flip[h], grad_scores) * score_scale
+            grad_proj[t, :, h * size : (h + 1) * size] = query_grad.T[:, :size].astype(BF)
+            key_grad[h] += mm(grad_scores, query)
+            val_grad[h] += mm(probs.astype(BF), grad)
+
+    each(0, S, block)
+    for h in range(local_heads):
+        low = (key_grad[h] * score_scale)[:, :size].astype(BF)
+        grad_proj[:, :, C + h * size : C + (h + 1) * size] = low.reshape(S, L, size)
+        low = val_grad[h][:, :size].astype(BF)
+        grad_proj[:, :, 2 * C + h * size : 2 * C + (h + 1) * size] = low.reshape(S, L, size)
+
+    def spread(index):
+        t = at.peer(arrival(index))
+        mix_src[t] = mm_nt(grad_proj[t], w_qkv[...]).astype(BF)
+        mix_sum.send(index)
+
+    each(0, S, lambda index: spread(lax.rem(index + 2, S)))
+    grads = grad_proj[...].reshape(S * L, 3 * C)
+    qkv_wide[...] = mm_tn(mixed_all[...].reshape(S * L, D), grads)
+    for g in range(G):
+        qkv_g[g] = qkv_wide[g * rows_own : (g + 1) * rows_own, :].astype(BF)
+    qkv.start()
+    b_qkv[...] = jnp.sum(grads.astype(F32), axis=0, keepdims=True)
+
+    two.scatter()
+    out.scatter()
+    mix_sum.wait()
+    step = min(32, L)
+    mod_sums[...] = sums_in[...]
+    scale = mod[1:2, :]
+
+    def back(i):
+        rows = pl.ds(pl.multiple_of(i * step, step), step)
+        grad_mixed = mix_sum.total(rows)
+        normed, inv_std = norm_stats(latents[rows, :].astype(F32))
+        grad_latents[rows, :] = grad_resid[rows, :] + norm_back(
+            grad_mixed * (1.0 + scale), normed, inv_std
+        )
+        mod_sums[0:1, :] += jnp.sum(grad_mixed, axis=0, keepdims=True)
+        mod_sums[1:2, :] += jnp.sum(grad_mixed * normed, axis=0, keepdims=True)
+
+    each(0, L // step, back)
     tail.start(mod_sums, b_one, b_two, b_out, b_qkv)
-    out.start()
-    two.start()
-    one.start()
-    qkv.start()
-    tail.middle(D, hidden, rows)
-    out.scatter()
-    tail.owners(silu_all, w_ada, o_ada, o_b_ada, flat_sum, b_pieces, o_small)
-    two.scatter()
     one.scatter()
-    qkv.scatter()
-    tail.finish(cond, o_cond)
+    tail.middle(D, hidden, rows_own)
     out.total()
     two.total()
+    tail.owners(w_ada, o_small)
+    qkv.scatter()
     one.total()
+    tail.finish(cond, o_cond)
     qkv.total()
     out.finish()
-    o_out[...] = out.swap[0].astype(F32) + out.swap[1].astype(F32)
     two.finish()
+    one.finish()
+    qkv.finish()
+
+
+def backward(sizes, *args):
+    R, F, S = sizes
+    G = F * S
+    grad_heads, latents = args[0], args[5]
+    one_g, two_g, w_ada = args[9], args[10], args[15]
+    _, L, C = grad_heads.shape
+    D = latents.shape[1]
+    T = S * L
+    local_heads = H // S
+    rows = w_ada.shape[0]
+    hidden = one_g.shape[2]
+    pack = 2 * D // G + 2 * rows + hidden // F
+    shape = jax.ShapeDtypeStruct
+    return pl.pallas_call(
+        lambda *refs: backward_kernel(sizes, *refs),
+        name="backward",
+        out_shape=(
+            shape((L, D), F32),
+            shape((S, rows, 3 * C), BF),
+            shape((S, rows, hidden), BF),
+            shape(two_g.shape[1:], BF),
+            shape((2, rows, D), BF),
+            shape((R * F, 6, D), BF),
+            shape((1, pack), F32),
+            shape((1, D), F32),
+        ),
+        in_specs=[VM] * 9 + [HB] * 3 + [VM] * 5,
+        out_specs=(VM,) * 8,
+        scratch_shapes=[
+            pltpu.VMEM((S, L, C), BF),
+            pltpu.VMEM((local_heads, LANES, T), BF),
+            pltpu.VMEM((local_heads, T, LANES), F32),
+            pltpu.VMEM((local_heads, T, LANES), F32),
+            pltpu.VMEM((S, L, 3 * C), BF),
+            pltpu.VMEM((D, 3 * C), F32),
+            pltpu.VMEM((G, rows, 3 * C), BF),
+            pltpu.VMEM((6, D), F32),
+            pltpu.VMEM((1, 3 * C), F32),
+            DMA((2, S)),
+        ]
+        + SeqSum.scratch(S, L, D)
+        + ColumnScatter.scratch(sizes, rows, 3 * C)
+        + ColumnScatter.scratch(sizes, rows, hidden)
+        + RowScatter.scratch(sizes, two_g.shape[2], D)
+        + FullScatter.scratch(sizes, rows, D)
+        + Tail.scratch(sizes, D, hidden, rows),
+        compiler_params=params(4, 60),
+    )(*args)
+
+
+def assemble_kernel(sizes, qkv, one, two, out, mod_all, silu_all, o_qkv, o_one, o_two, o_out, o_ada, o_b_ada, flat, pieces):
+    R, F, S = sizes
+    G = F * S
+    D = o_out.shape[1]
+    C = D // S
+    hidden = one.shape[2]
+    o_out[...] = out[0].astype(F32) + out[1].astype(F32)
     for p in range(2):
-        o_two[p] = two.done[p].astype(F32)
-    one.finish()
+        o_two[p] = two[p].astype(F32)
     block = hidden // F
     for t in range(S):
         for f in range(F):
             col = (f * S + t) * block
-            o_one[:, col : col + block] = one.done[t, :, f * block : (f + 1) * block].astype(F32)
-    qkv.finish()
-    for t in range(S):
+            o_one[:, col : col + block] = one[t, :, f * block : (f + 1) * block].astype(F32)
         for j in range(3):
-            o_qkv[:, j * D + t * C : j * D + (t + 1) * C] = qkv.done[
-                t, :, j * C : (j + 1) * C
-            ].astype(F32)
-
-
-def sums(sizes, qkv_g, one_g, two_g, out_g, mod_sums, b_one, b_two, b_out, b_qkv, silu_all, w_ada, cond):
+            o_qkv[:, j * D + t * C : j * D + (t + 1) * C] = qkv[t, :, j * C : (j + 1) * C].astype(F32)
+    silu = silu_all[:, 0, :].astype(BF)
+    width = o_b_ada.shape[1]
+    for v in range(6):
+        rows = mod_all[:, v, :]
+        o_ada[:, v * D : (v + 1) * D] = mm_tn(silu, rows)
+        flat[:, v * D : (v + 1) * D] = jnp.sum(rows.astype(F32), axis=0, keepdims=True)
+    for g in range(G):
+        pieces[g] = flat[:, g * width : (g + 1) * width]
+    o_b_ada[...] = pieces[lax.axis_index("fsdp") * S + lax.axis_index("seq")]
+
+
+def assemble(sizes, qkv, one, two, out, mod_all, silu_all):
     R, F, S = sizes
     G = F * S
-    D = cond.shape[1]
-    rows = w_ada.shape[0]
-    hidden = one_g.shape[2]
-    width = w_ada.shape[1] // G
+    rows, D = out.shape[1:]
     shape = jax.ShapeDtypeStruct
-    pack = 2 * D // G + 2 * rows + hidden // F
     return pl.pallas_call(
-        lambda *refs: sums_kernel(sizes, *refs),
-        name="sums",
+        lambda *refs: assemble_kernel(sizes, *refs),
+        name="assemble",
         out_shape=(
             shape((rows, 3 * D), F32),
-            shape((rows, hidden * S), F32),
-            shape(two_g.shape[1:], F32),
+            shape((rows, one.shape[2] * S), F32),
+            shape(two.shape, F32),
             shape((rows, D), F32),
-            shape(w_ada.shape, F32),
-            shape((1, width), F32),
-            shape((1, pack), F32),
-            shape((1, D), F32),
+            shape((rows, 6 * D), F32),
+            shape((1, 6 * D // G), F32),
         ),
-        in_specs=[VM] * 12,
-        out_specs=(VM,) * 8,
-        scratch_shapes=ColumnScatter.scratch(sizes, rows, qkv_g.shape[2])
-        + ColumnScatter.scratch(sizes, rows, hidden)
-        + RowScatter.scratch(sizes, two_g.shape[2], D)
-        + FullScatter.scratch(sizes, rows, D)
-        + Tail.scratch(sizes, D, hidden, rows)
-        + [pltpu.VMEM((1, w_ada.shape[1]), F32), pltpu.VMEM((G, 1, width), F32)],
-        compiler_params=params(5, 62),
-    )(qkv_g, one_g, two_g, out_g, mod_sums, b_one, b_two, b_out, b_qkv, silu_all, w_ada, cond)
+        in_specs=[VM] * 6,
+        out_specs=(VM,) * 6,
+        scratch_shapes=[pltpu.VMEM((1, 6 * D), F32), pltpu.VMEM((G, 1, 6 * D // G), F32)],
+        compiler_params=pltpu.CompilerParams(vmem_limit_bytes=40 * 1024 * 1024),
+    )(qkv, one, two, out, mod_all, silu_all)
 
 
 def on_device(
@@ -1518,12 +1492,10 @@
     sizes = R, F, S = tuple(lax.axis_size(name) for name in ("rep", "fsdp", "seq"))
     G = F * S
     _, L, D = latents.shape
-    C = D // S
     hidden = w_one.shape[1] // S
     rows = w_ada.shape[0]
     qv = b_qv.shape[0]
     owner = lax.axis_index(("fsdp", "seq"))
-    s = lax.axis_index("seq")
     width = b_ada.shape[0]
     bias_slot = lax.dynamic_update_slice(
         jnp.zeros((w_ada.shape[1],), F32), b_ada.astype(F32), (owner * width,)
@@ -1531,36 +1503,37 @@
     bias_pack = jnp.concatenate([b_qv, b_out, b_two, b_one]).astype(F32)[None]
     tokens = latents[0]
     two_rows = w_two.shape[0]
-    mixed, mod, silu_all, packs, g_qkv, g_one, g_two, g_out = front(
+    (
+        mixed_all,
+        heads,
+        log_sums,
+        merged,
+        branch_one,
+        mixed_two,
+        mod,
+        silu_all,
+        grad_all,
+        full_qkv,
+        full_out,
+        bias_one,
+        bias_two,
+        g_one,
+        g_two,
+    ) = forward(
         sizes,
         cond,
         w_ada,
         bias_slot,
         tokens,
+        cotangent[0],
         w_qkv,
         w_one,
+        bias_pack,
         w_two.reshape(2, two_rows // 2, D),
         w_out,
-        bias_pack,
     )
-    packs = packs[:, 0]
-    half = G // 2
-    own = F // 2
-    q_bias = lax.dynamic_slice_in_dim(packs[:half, :qv], s * own, own, 0).reshape(1, C)
-    v_bias = lax.dynamic_slice_in_dim(packs[half:, :qv], s * own, own, 0).reshape(1, C)
-    qkv_bias = jnp.concatenate([q_bias, jnp.zeros((1, C), F32), v_bias], axis=1)
-    bias_out = packs[:, qv : qv + rows].reshape(1, D)
-    bias_two = packs[:, qv + rows : qv + 2 * rows].reshape(1, D)
-    bias_one = lax.dynamic_index_in_dim(
-        packs[:, qv + 2 * rows :].reshape(F, S, -1), s, 1, False
-    ).reshape(1, hidden)
-    full_qkv = g_qkv.reshape(D, 3 * C)
     full_one = g_one.reshape(D, hidden)
     full_two = g_two.reshape(hidden, D)
-    full_out = g_out.reshape(D, D)
-    mixed_all, heads, log_sums, merged, branch_one, mixed_two = attend(
-        sizes, mixed, full_qkv, qkv_bias, mod, tokens, full_out, bias_out
-    )
     (
         block_out,
         grad_resid,
@@ -1575,6 +1548,7 @@
     ) = mlp(
         sizes,
         mixed_two,
+        grad_all,
         cotangent[0],
         mod,
         full_one,
@@ -1586,23 +1560,28 @@
         full_out,
         merged,
     )
-    grad_latents, qkv_g, grad_b_qkv, mod_sums = attend_back(
-        sizes, grad_heads, heads, log_sums, mixed_all, full_qkv, tokens, mod, grad_resid, mod_sums
-    )
-    o_qkv, o_one, o_two, o_out, o_ada, o_b_ada, o_small, o_cond = sums(
+    grad_latents, qkv_sum, one_sum, two_sum, out_sum, mod_all, o_small, o_cond = backward(
         sizes,
-        qkv_g.reshape(G, rows, 3 * C),
+        grad_heads,
+        heads,
+        log_sums,
+        mixed_all,
+        full_qkv,
+        tokens,
+        mod,
+        grad_resid,
+        mod_sums,
         one_g.reshape(G, rows, hidden),
         two_g.reshape(F, 2, two_rows // 2, D),
         out_g.reshape(F, S, rows, D),
-        mod_sums,
         grad_b_one,
         grad_b_two,
         grad_b_out,
-        grad_b_qkv,
-        silu_all,
         w_ada,
         cond,
+    )
+    o_qkv, o_one, o_two, o_out, o_ada, o_b_ada = assemble(
+        sizes, qkv_sum, one_sum, two_sum, out_sum, mod_all, silu_all
     )
     small = o_small[0]
     return (

time: 610 us -> 396 us (0.65)
  Pallas kernels: 569 us -> 375 us
  local copies, waits for them, and re-layouts: 31.1 us -> 13.4 us
    pallas_call x4 -> x3, Pallas kernels: 455 us -> 312 us  [the longest x1 167 us: forward(): pl.pallas_call(lambda *refs: forward_kernel(sizes, *refs), name='forward'...]
    pallas_call x1, Pallas kernels: 113 us -> 62.4 us  [mlp(): pl.pallas_call(lambda *refs: mlp_kernel(sizes, *refs), name='mlp', out_sh...]
    unnamed x56 -> x23, local copies, waits for them, and re-layouts: 23.2 us -> 8.14 us
where the time goes in v2:
time: 396 us; the launch traced here: 391 us
  Pallas kernels  375 us (95%)
  local copies, waits for them, and re-layouts  13.4 us (3%)
    pallas_call x1, Pallas kernels, forward(): pl.pallas_call(lambda *refs: forward_kernel(sizes, *refs), name='forward'...  167 us
    pallas_call x1, Pallas kernels, backward(): pl.pallas_call(lambda *refs: backward_kernel(sizes, *refs), name='backwar...  142 us
    pallas_call x1, Pallas kernels, mlp(): pl.pallas_call(lambda *refs: mlp_kernel(sizes, *refs), name='mlp', out_sh...  62.4 us
    unnamed x23, local copies, waits for them, and re-layouts  8.14 us

profile of v2, /device:TPU:0, one launch (start us, length us, event | category | flops | bytes accessed | tf_op | source)
XLA Modules:
  0.0 390.9 jit_solution(6725211834665964209)
XLA Ops:
  0.7 0.7 concatenate.18
  1.3 0.7 concatenate.21
  2.0 1.3 maximum_convert_fusion.refs_7_
  3.3 0.7 broadcast_in_dim.20
  4.0 0.2 dynamic_update_slice.4.refs_2_
  4.2 0.0 copy-start.8
  4.2 0.6 copy-done.8
  4.8 166.9 %forward.1 = (bf16[4,256,1152]{2,1,0:T(8,128)(2,1)}, bf16[12,1024,128]{2,1,0:T(8,128)(2,1)}, f32[4,4,1,256]{3,2,1,0:T(1,128)}, bf16[256,1152]{1,0:T(8,128)(2,1)}...) custom-call(bf16[1,1152]{1,0:T(2,128)(2,1)} %refs_16_.1, ...), custom_call_target="tpu_custom_call" | custom-call | tf_op jit(solution)/shard_map/forward/pallas_call | solution.py:635
  171.7 62.4 %mlp.1 = (bf16[256,1152]{1,0:T(8,128)(2,1)}, f32[256,1152]{1,0:T(8,128)}, bf16[4,256,288]{2,1,0:T(8,128)(2,1)}, bf16[1152,1152]{1,0:T(8,128)(2,1)}, bf16[1152,11...) custom-call(bf16[256,1152]{1,0:T(8,128)(2,1)} %get-tuple-element.52., ...), custom_call_target="tpu_custom_call" | custom-call | tf_op jit(solution)/shard_map/mlp/pallas_call | solution.py:835
  234.1 0.0 copy-start.5
  234.1 0.0 copy-start.7
  234.1 142.1 %backward.1 = (f32[256,1152]{1,0:T(8,128)}, bf16[4,72,864]{2,1,0:T(8,128)(2,1)}, bf16[4,72,1152]{2,1,0:T(8,128)(2,1)}, bf16[2,144,1152]{2,1,0:T(8,128)(2,1)}, bf...) custom-call(bf16[4,256,288]{2,1,0:T(8,128)(2,1)} %get-tuple-element.63.refs_0_, ...), custom_call_target="tpu_custom_call" | custom-call | tf_op jit(solution)/shard_map/backward/pallas_call | solution.py:1402
  376.2 1.2 slice.24
  377.4 1.3 slice_bitcast_fusion
  378.6 1.3 slice_reduce_fusion
  380.0 0.0 copy-done.5
  380.0 0.0 copy-start
  380.0 1.1 copy-done
  381.0 0.0 copy-start.1
  381.1 1.1 copy-done.1
  382.1 0.0 copy-start.2
  382.1 1.0 copy-done.2
  383.2 0.0 copy-start.3
  383.2 1.0 copy-done.3
  384.2 0.0 copy-start.4
  384.2 0.9 copy-done.4
  385.1 0.0 copy-start.6
  385.1 0.0 copy-start.9
  385.1 3.4 assemble.1
  388.5 0.0 copy-done.7
  388.5 0.8 copy.30
  389.3 0.0 copy-done.6
  389.3 1.0 copy.31
  390.3 0.0 copy-done.9
  390.3 0.6 copy.32
  (1 shorter events, 0.0 us)
Async XLA Ops:
  4.2 0.6 copy-start.8
  234.1 145.9 %copy-start.5 = (f32[8,1,72]{2,1,0:T(1,128)S(1)}, f32[8,1,72]{2,1,0:T(1,128)}, u32[]{:S(2)}) copy-start(f32[8,1,72]{2,1,0:T(1,128)} %get-tuple-element.83.refs_5_) | copy-start | bytes 6916
  234.1 154.4 %copy-start.7 = (bf16[256,1152]{1,0:T(8,128)(2,1)S(1)}, bf16[256,1152]{1,0:T(8,128)(2,1)}, u32[]{:S(2)}) copy-start(bf16[256,1152]{1,0:T(8,128)(2,1)} %get-tuple-element.62) | copy-start | bytes 1769476
  380.0 1.1 copy-start
  381.0 1.1 copy-start.1
  382.1 1.0 copy-start.2
  383.2 1.0 copy-start.3
  384.2 0.9 copy-start.4
  385.1 4.2 %copy-start.6 = (f32[256,1152]{1,0:T(8,128)S(1)}, f32[256,1152]{1,0:T(8,128)}, u32[]{:S(2)}) copy-start(f32[256,1152]{1,0:T(8,128)} %get-tuple-element.76) | copy-start | bytes 3538948
  385.1 5.2 %copy-start.9 = (f32[1,1152]{1,0:T(1,128)S(1)}, f32[1,1152]{1,0:T(1,128)}, u32[]{:S(2)}) copy-start(f32[1,1152]{1,0:T(1,128)} %get-tuple-element.108) | copy-start | bytes 13828

commit v3 on v2

--- a/solution.py
+++ b/solution.py
@@ -44,6 +44,19 @@
     pltpu.make_async_copy(like, like, sem).wait()
 
 
+class Moves:
+    def __init__(self, sem, *pairs):
+        self.copies = [local(pair[0], pair[1], sem.at[i]) for i, pair in enumerate(pairs)]
+
+    def start(self, *which):
+        for i in which or range(len(self.copies)):
+            self.copies[i].start()
+
+    def wait(self, *which):
+        for i in which or range(len(self.copies)):
+            self.copies[i].wait()
+
+
 def each(start, stop, body):
     def step(index, carry):
         body(index)
@@ -103,6 +116,7 @@
         self.s = lax.axis_index("seq")
         self.me = self.z * self.S + self.s
         self.mine = lax.rem(self.s, 2) == self.y
+        self.steps = (2, 1, 3) if self.F == 4 else tuple(range(1, self.F))
 
     def zs(self, i):
         return lax.rem(self.z + i, self.F)
@@ -233,182 +247,229 @@
         return value
 
 
-class ColumnGather:
-    sems = (6,)
-
-    def __init__(self, at, src, dst, sem):
-        self.at, self.src, self.dst, self.sem = at, src, dst, sem
+class FarGather:
+    relayed = True
+
+    def __init__(self, at, dst, sem):
+        self.at, self.dst, self.sem = at, dst, sem
+        self.line = self.relayed and at.F == 4
 
     @staticmethod
     def scratch(F):
         return DMA((7, F))
 
+    def send(self, z_from, z_to, kind):
+        pieces = self.half(z_from)
+        held = self.origin() if kind == 0 else pieces
+        for source, piece in zip(held, pieces):
+            remote(
+                source, piece, self.sem.at[kind, z_to], self.sem.at[2, z_from], {"fsdp": z_to}
+            ).start()
+
+    def origin(self):
+        return self.half(self.at.z)
+
+    def await_half(self, row, z):
+        await_bytes(self.like(), self.sem.at[row, z])
+
+    def around(self, step, body):
+        at = self.at
+
+        @pl.when(at.z >= step)
+        def _():
+            body(at.z - step)
+
+        @pl.when(at.z + step < at.F)
+        def _():
+            body(at.z + step)
+
+    def direct(self, step, body):
+        if self.line and step == 3:
+            return
+        self.around(step, body)
+
+    def start_far(self):
+        for step in self.at.steps:
+            self.direct(step, lambda z_to: self.send(self.at.z, z_to, 0))
+
+    def service(self, step):
+        at = self.at
+
+        def take(z_from):
+            self.await_half(2, z_from)
+            for piece in self.half(z_from):
+                remote(
+                    piece, piece, self.sem.at[3, z_from], self.sem.at[4, z_from], at.flip()
+                ).start()
+
+        self.around(step, take)
+        if self.line and step == 2:
+
+            @pl.when((at.z == 1) | (at.z == 2))
+            def _():
+                far = jnp.where(at.z == 1, 3, 0)
+                end = 3 - far
+                self.send(far, end, 1)
+
+    def finish_far(self):
+        at = self.at
+
+        def swapped(z_from):
+            self.await_half(3, z_from)
+            self.await_half(4, z_from)
+
+        for step in range(1, at.F):
+            self.around(step, swapped)
+            self.direct(step, lambda z_to: self.await_half(0, z_to))
+        if self.line:
+
+            @pl.when((at.z == 1) | (at.z == 2))
+            def _():
+                self.await_half(1, jnp.where(at.z == 1, 0, 3))
+
+
+class ColumnGather(FarGather):
+    def __init__(self, at, src, dst, sem):
+        super().__init__(at, dst, sem)
+        self.src = src
+
+    def half(self, z):
+        at = self.at
+        return [self.dst.at[z * at.S + 2 * k + at.y] for k in range(at.S // 2)]
+
+    def like(self):
+        return self.dst.at[pl.ds(0, self.at.S // 2)]
+
     def start(self):
         at, src, dst, sem = self.at, self.src, self.dst, self.sem
-        local(src.at[at.s], dst.at[at.me], sem.at[0, 0]).start()
 
         def near(j):
             t = at.ss(j)
-            remote(src.at[t], dst.at[at.me], sem.at[1, 0], sem.at[2, 0], {"seq": t}).start()
+            remote(src.at[t], dst.at[at.me], sem.at[5, 0], sem.at[6, 0], {"seq": t}).start()
 
         each(1, at.S, near)
+        local(src.at[at.s], dst.at[at.me], sem.at[5, 1]).start()
+
+    def near_done(self):
+        at, dst, sem = self.at, self.dst, self.sem
+        local(self.src.at[at.s], dst.at[at.me], sem.at[5, 1]).wait()
+        near = dst.at[pl.ds(0, at.S - 1)]
+        await_bytes(near, sem.at[5, 0])
+        await_bytes(near, sem.at[6, 0])
+
+
+class RowGather(FarGather):
+    def __init__(self, at, src, dst, sem):
+        super().__init__(at, dst, sem)
+        self.src = src
+
+    def half(self, z):
+        return [self.dst.at[z, self.at.y]]
+
+    def origin(self):
+        return [self.src.at[self.at.y]]
+
+    def like(self):
+        return self.dst.at[0, 0]
+
+    def start(self):
+        at = self.at
+        local(self.src, self.dst.at[at.z], self.sem.at[5, 0]).start()
+
+    def near_done(self):
+        at = self.at
+        local(self.src, self.dst.at[at.z], self.sem.at[5, 0]).wait()
+
+
+class OwnGather(FarGather):
+    relayed = False
+
+    def __init__(self, at, src, dst, sem):
+        super().__init__(at, dst, sem)
+        self.src = src
+
+    def half(self, z):
+        return [self.dst.at[self.at.s, z]]
+
+    def origin(self):
+        return [self.src]
+
+    def like(self):
+        return self.src
+
+    def start(self):
+        at = self.at
+        local(self.src, self.dst.at[at.s, at.z], self.sem.at[5, 0]).start()
+
+    def near_done(self):
+        at = self.at
+        local(self.src, self.dst.at[at.s, at.z], self.sem.at[5, 0]).wait()
+
+    def start_far(self):
+        pl.when(self.at.mine)(super().start_far)
+
+    def service(self, step):
+        take = super().service
+        pl.when(self.at.mine)(lambda: take(step))
+
+    def finish_far(self):
+        at = self.at
+
+        def sent(z_from):
+            self.await_half(3, z_from)
+
+        def swapped(z_from):
+            self.await_half(4, z_from)
 
         @pl.when(at.mine)
         def _():
-            def far(i):
-                def one(j):
-                    t = at.ss(j)
-                    remote(
-                        src.at[t],
-                        dst.at[at.me],
-                        sem.at[3, i],
-                        sem.at[4, i],
-                        {"fsdp": at.zs(i), "seq": t},
-                    ).start()
-
-                each(0, at.S, one)
-
-            each(1, at.F, far)
-
-    def half(self):
-        return self.dst.at[pl.ds(0, self.at.S // 2)]
-
-    def forward(self):
-        at, dst, sem = self.at, self.dst, self.sem
-
-        def far(i):
-            await_bytes(self.half(), sem.at[4, i])
-
-            def one(k):
-                slot = at.zs_back(i) * at.S + 2 * k + at.y
-                remote(
-                    dst.at[slot], dst.at[slot], sem.at[5, i], sem.at[6, i], at.flip()
-                ).start()
-
-            each(0, at.S // 2, one)
-
-        each(1, at.F, far)
-
-    def finish(self):
-        at, src, dst, sem = self.at, self.src, self.dst, self.sem
-        local(src.at[at.s], dst.at[at.me], sem.at[0, 0]).wait()
-        near = dst.at[pl.ds(0, at.S - 1)]
-        await_bytes(near, sem.at[1, 0])
-        await_bytes(near, sem.at[2, 0])
-
-        @pl.when(at.mine)
-        def _():
-            each(1, at.F, lambda i: await_bytes(src, sem.at[3, i]))
-
-        def far(i):
-            await_bytes(self.half(), sem.at[5, i])
-            await_bytes(self.half(), sem.at[6, i])
-
-        each(1, at.F, far)
-
-
-class RowGather:
-    def __init__(self, at, src, dst, sem):
-        self.at, self.src, self.dst, self.sem = at, src, dst, sem
-
-    @staticmethod
-    def scratch(F):
-        return DMA((5, F))
-
-    def start(self):
-        at, src, dst, sem = self.at, self.src, self.dst, self.sem
-        local(src, dst.at[at.z], sem.at[0, 0]).start()
-
-        def far(i):
-            remote(
-                src.at[at.y], dst.at[at.z, at.y], sem.at[1, i], sem.at[2, i], {"fsdp": at.zs(i)}
-            ).start()
-
-        each(1, at.F, far)
-
-    def forward(self):
-        at, dst, sem = self.at, self.dst, self.sem
-
-        def far(i):
-            block = dst.at[at.zs_back(i), at.y]
-            await_bytes(block, sem.at[2, i])
-            remote(block, block, sem.at[3, i], sem.at[4, i], at.flip()).start()
-
-        each(1, at.F, far)
-
-    def finish(self):
-        at, src, dst, sem = self.at, self.src, self.dst, self.sem
-        local(src, dst.at[at.z], sem.at[0, 0]).wait()
-
-        def far(i):
-            block = dst.at[0, 0]
-            await_bytes(block, sem.at[1, i])
-            await_bytes(block, sem.at[3, i])
-            await_bytes(block, sem.at[4, i])
-
-        each(1, at.F, far)
-
-
-class FullGather:
-    def __init__(self, at, src, dst, sem):
-        self.at, self.src, self.dst, self.sem = at, src, dst, sem
-
-    @staticmethod
-    def scratch(F):
-        return DMA((5, F))
-
-    def spread(self, i, block):
-        at, sem = self.at, self.sem
-
-        def one(j):
-            remote(block, block, sem.at[3, i], sem.at[4, i], {"seq": at.ss(j)}).start()
-
-        each(1, at.S, one)
-
-    def start(self):
-        at, src, dst, sem = self.at, self.src, self.dst, self.sem
-        mine = dst.at[at.z, at.s]
-        local(src, mine, sem.at[0, 0]).start()
-
-        def far(i):
-            remote(src, mine, sem.at[1, i], sem.at[2, i], {"fsdp": at.zs(i)}).start()
-
-        each(1, at.F, far)
-
-    def forward(self):
-        at, src, dst, sem = self.at, self.src, self.dst, self.sem
-        local(src, dst.at[at.z, at.s], sem.at[0, 0]).wait()
-        self.spread(0, dst.at[at.z, at.s])
-
-        def far(i):
-            block = dst.at[at.zs_back(i), at.s]
-            await_bytes(block, sem.at[2, i])
-            self.spread(i, block)
-
-        each(1, at.F, far)
-
-    def finish(self):
-        at, src, dst, sem = self.at, self.src, self.dst, self.sem
-        others = dst.at[0, pl.ds(0, at.S - 1)]
-
-        def far(i):
-            await_bytes(others, sem.at[3, i])
-            await_bytes(others, sem.at[4, i])
-
-        each(0, at.F, far)
-        each(1, at.F, lambda i: await_bytes(src, sem.at[1, i]))
+            for step in range(1, at.F):
+                self.around(step, sent)
+                self.direct(step, lambda z_to: self.await_half(0, z_to))
+            if self.line:
+
+                @pl.when((at.z == 1) | (at.z == 2))
+                def _():
+                    self.await_half(1, jnp.where(at.z == 1, 0, 3))
+
+        @pl.when(jnp.logical_not(at.mine))
+        def _():
+            for step in range(1, at.F):
+                self.around(step, swapped)
 
 
 def forward_kernel(sizes, *refs):
     at = Place(sizes)
     R, F, S, G = at.R, at.F, at.S, at.G
-    cond, w_ada, bias_slot, latents, cotangent, w_qkv, w_one, bias_pack, w_two, w_out = refs[:10]
-    mixed_all, heads, log_sums, merged, branch_one, mixed_two = refs[10:16]
-    mod, silu_all, grad_all, full_qkv, full_out, bias_one, bias_two, g_one, g_two = refs[16:25]
+    cond, bias_slot, bias_pack, i_latents, i_cotangent, i_ada, i_qkv, i_one, w_two, w_out = refs[:10]
+    o_mixed, o_heads, o_merged, o_branch, o_mix, o_grad, o_full_qkv, o_full_out = refs[10:18]
+    log_sums, mod, silu_all, bias_one, bias_two, g_one, g_two = refs[18:25]
     silu_src, part, parts_in, mod_src, mod_in, qkv_src, one_src, pack_all = refs[25:33]
     g_qkv, g_out, wide, bias_qkv, bias_out, val_flip, att, merged_in = refs[33:41]
     silu_sem, part_sem, mod_sem, pack_sem, qkv_sem, one_sem, two_sem, out_sem = refs[41:49]
-    mixed_sem, grad_sem, att_sem = refs[49:52]
+    mixed_sem, grad_sem, att_sem, mix_sem, spread_sem, load_sem, save_sem = refs[49:56]
+    latents, cotangent, w_ada, w_qkv, w_one = refs[56:61]
+    mixed_all, heads, merged, branch_one, mix_all, grad_all, full_qkv, full_out = refs[61:69]
+    loads = Moves(
+        load_sem,
+        (i_qkv, w_qkv),
+        (i_ada, w_ada),
+        (i_one, w_one),
+        (i_latents, latents),
+        (i_cotangent, cotangent),
+    )
+    loads.start()
+    saves = Moves(
+        save_sem,
+        (mixed_all, o_mixed),
+        (heads, o_heads),
+        (merged, o_merged),
+        (branch_one, o_branch),
+        (mix_all, o_mix),
+        (grad_all, o_grad),
+        (full_qkv, o_full_qkv),
+        (full_out, o_full_out),
+    )
     L, D = latents.shape
     C = D // S
     T = S * L
@@ -456,18 +517,19 @@
     qkv = ColumnGather(at, qkv_src, g_qkv, qkv_sem)
     one = ColumnGather(at, one_src, g_one, one_sem)
     two = RowGather(at, w_two, g_two, two_sem)
-    out = FullGather(at, w_out, g_out, out_sem)
+    out = OwnGather(at, w_out, g_out, out_sem)
+    loads.wait(0)
     for t in range(S):
         for j in range(3):
             qkv_src[t, :, j * C : (j + 1) * C] = w_qkv[:, j * D + t * C : j * D + (t + 1) * C]
+
     qkv.start()
-    for t in range(S):
-        for f in range(F):
-            col = (f * S + t) * block
-            one_src[t, :, f * block : (f + 1) * block] = w_one[:, col : col + block]
+    two.start()
+    out.start()
 
     each(1, 2 * F, lambda i: cond_copy(i).wait())
     left = jnp.concatenate([silu_all[at.y * F + f] for f in range(F)], axis=0).astype(BF)
+    loads.wait(1)
     sums = mm(left, w_ada[...]) + bias_slot[...]
     for f in range(F):
         for v in range(6):
@@ -487,6 +549,13 @@
 
     each(1, G, lambda i: part_copy(i).start())
     parts_in[at.me] = part[at.me]
+    loads.wait(2)
+    for t in range(S):
+        for f in range(F):
+            col = (f * S + t) * block
+            one_src[t, :, f * block : (f + 1) * block] = w_one[:, col : col + block]
+    qkv.near_done()
+    qkv.start_far()
     each(1, G, lambda i: part_copy(i).wait())
     total = parts_in[0]
     for g in range(1, G):
@@ -499,11 +568,14 @@
         )
 
     each(1, S, lambda i: mod_copy(i).start())
+    one.start()
     mod_in[at.s] = total
+    out.start_far()
     each(1, S, lambda i: mod_copy(i).wait())
     for t in range(S):
         mod[:, t * C : (t + 1) * C] = mod_in[t]
 
+    loads.wait(3)
     step = min(64, L)
 
     def norm(i):
@@ -514,7 +586,15 @@
     each(0, L // step, norm)
     gather = SeqGather(at, mixed_all, mixed_sem)
     gather.start()
-    out.start()
+    loads.wait(4)
+    grad_all[at.s] = (mod[5:6, :] * cotangent[...].astype(F32)).astype(BF)
+    grad_gather = SeqGather(at, grad_all, grad_sem)
+    grad_gather.start()
+    one.near_done()
+    qkv.service(at.steps[0])
+    one.start_far()
+    out.near_done()
+    two.near_done()
 
     others = pack_all.at[pl.ds(0, G - 1)]
     await_bytes(others, pack_sem.at[0, 0])
@@ -534,13 +614,11 @@
     for f in range(F):
         bias_one[:, f * block : (f + 1) * block] = pack_all[f * S + at.s][:, qv + 2 * rows_own :]
 
-    qkv.forward()
-    one.start()
-    two.start()
-    grad_all[at.s] = (mod[5:6, :] * cotangent[...].astype(F32)).astype(BF)
-    grad_gather = SeqGather(at, grad_all, grad_sem)
-    grad_gather.start()
-    qkv.finish()
+    for i in at.steps[1:]:
+        qkv.service(i)
+    for i in at.steps:
+        out.service(i)
+    qkv.finish_far()
 
     def join(slabs, whole):
         cols = whole.shape[1]
@@ -555,6 +633,7 @@
         each(0, D // tall, cast)
 
     join(lambda g: g_qkv[g], full_qkv)
+    saves.start(6)
 
     pad = jnp.zeros((L, LANES - size), BF)
 
@@ -569,7 +648,12 @@
             )
 
     each(0, S, project)
-    out.forward()
+    saves.start(0, 1)
+    out.finish_far()
+    spread = SeqGather(at, g_out, spread_sem)
+    spread.start()
+    each(1, S, grad_gather.arrive)
+    saves.start(5)
     for h in range(local_heads):
         val_flip[h] = heads[2 * local_heads + h].T
 
@@ -598,14 +682,21 @@
         def _():
             att_copy(j).start()
 
+        @pl.when(index == S // 2)
+        def _():
+            one.service(at.steps[0])
+            one.service(at.steps[1])
+            two.start_far()
+
     each(0, S, attention)
     merged_in[at.s] = att[at.s]
-    out.finish()
-    join(lambda g: g_out[g // S, g % S], full_out)
-    one.forward()
+    each(1, S, spread.arrive)
+    join(lambda g: g_out[g % S, g // S], full_out)
+    saves.start(7)
     each(1, S, lambda j: att_copy(j).wait())
     for t in range(S):
         merged[:, t * C : (t + 1) * C] = merged_in[t]
+    saves.start(2)
 
     def project_out(i):
         at_rows = pl.ds(pl.multiple_of(i * step, step), step)
@@ -613,16 +704,24 @@
         branch_one[at_rows, :] = branch
         residual = latents[at_rows, :].astype(F32) + mod[2:3, :] * branch
         normed, _ = norm_stats(residual)
-        mixed_two[at_rows, :] = (normed * (1.0 + mod[4:5, :]) + mod[3:4, :]).astype(BF)
+        mix_all[at.s, at_rows, :] = (normed * (1.0 + mod[4:5, :]) + mod[3:4, :]).astype(BF)
 
     each(0, L // step, project_out)
-    each(1, S, grad_gather.arrive)
-    two.forward()
-    one.finish()
-    two.finish()
-
-
-def forward(sizes, cond, w_ada, bias_slot, latents, cotangent, w_qkv, w_one, bias_pack, w_two, w_out):
+    saves.start(3)
+    mix_gather = SeqGather(at, mix_all, mix_sem)
+    mix_gather.start()
+    for i in at.steps[2:]:
+        one.service(i)
+    for i in at.steps:
+        two.service(i)
+    one.finish_far()
+    each(1, S, mix_gather.arrive)
+    saves.start(4)
+    two.finish_far()
+    saves.wait()
+
+
+def forward(sizes, cond, bias_slot, bias_pack, latents, cotangent, w_ada, w_qkv, w_one, w_two, w_out):
     R, F, S = sizes
     G = F * S
     rows, D = w_out.shape
@@ -632,28 +731,31 @@
     local_heads = H // S
     hidden = w_one.shape[1] // S
     shape = jax.ShapeDtypeStruct
+    kept = (
+        ((S, L, D), BF),
+        ((3 * local_heads, T, LANES), BF),
+        ((L, D), BF),
+        ((L, D), F32),
+        ((S, L, D), BF),
+        ((S, L, D), BF),
+        ((D, 3 * C), BF),
+        ((D, D), BF),
+    )
     return pl.pallas_call(
         lambda *refs: forward_kernel(sizes, *refs),
         name="forward",
-        out_shape=(
-            shape((S, L, D), BF),
-            shape((3 * local_heads, T, LANES), BF),
+        out_shape=tuple(shape(*item) for item in kept)
+        + (
             shape((local_heads, S, 1, L), F32),
-            shape((L, D), BF),
-            shape((L, D), F32),
-            shape((L, D), BF),
             shape((6, D), F32),
             shape((R * F, 1, rows), F32),
-            shape((S, L, D), BF),
-            shape((D, 3 * C), BF),
-            shape((D, D), BF),
             shape((1, hidden), F32),
             shape((1, D), F32),
             shape((G, rows, hidden), BF),
             shape((F,) + w_two.shape, BF),
         ),
-        in_specs=[VM] * 8 + [HB] * 2,
-        out_specs=(VM,) * 13 + (HB,) * 2,
+        in_specs=[VM] * 3 + [HB] * 7,
+        out_specs=(HB,) * 8 + (VM,) * 5 + (HB,) * 2,
         scratch_shapes=[
             pltpu.VMEM((G, 1, rows), F32),
             pltpu.VMEM((G, 6, C), F32),
@@ -664,7 +766,7 @@
             pltpu.VMEM((S, rows, hidden), BF),
             pltpu.VMEM((G,) + bias_pack.shape, F32),
             pltpu.VMEM((G, rows, 3 * C), BF),
-            pltpu.VMEM((F, S, rows, D), BF),
+            pltpu.VMEM((S, F, rows, D), BF),
             pltpu.VMEM((D, max(D, 3 * C)), F32),
             pltpu.VMEM((1, 3 * C), F32),
             pltpu.VMEM((1, D), F32),
@@ -678,117 +780,386 @@
             ColumnGather.scratch(F),
             ColumnGather.scratch(F),
             RowGather.scratch(F),
-            FullGather.scratch(F),
+            OwnGather.scratch(F),
             SeqGather.scratch(S),
             SeqGather.scratch(S),
             DMA((2, S)),
-        ],
+            SeqGather.scratch(S),
+            SeqGather.scratch(S),
+            DMA((5,)),
+            DMA((8,)),
+        ]
+        + [pltpu.VMEM(x.shape, x.dtype) for x in (latents, cotangent, w_ada, w_qkv, w_one)]
+        + [pltpu.VMEM(*item) for item in kept],
         compiler_params=params(1, 60),
-    )(cond, w_ada, bias_slot, latents, cotangent, w_qkv, w_one, bias_pack, w_two, w_out)
-
-
-def mlp_kernel(
-    sizes,
-    mixed_two,
-    grad_all,
-    cotangent,
-    mod,
-    w_one,
-    bias_one,
-    w_two,
-    bias_two,
-    branch_one,
-    latents,
-    w_out,
-    merged,
-    block_out,
-    grad_resid,
-    grad_heads,
-    grad_w_one,
-    grad_w_two,
-    grad_w_out,
-    grad_b_one,
-    grad_b_two,
-    grad_b_out,
-    mod_sums,
-    mix_all,
-    act_all,
-    pre_all,
-    grad_branch,
-    mixed_sem,
-    *rest,
-):
-    branch_refs, mix_refs = rest[:4], rest[4:]
+    )(cond, bias_slot, bias_pack, latents, cotangent, w_ada, w_qkv, w_one, w_two, w_out)
+
+
+class RowScatter:
+    def __init__(self, at, src, got, stage, sem):
+        self.at, self.src, self.got, self.stage, self.sem = at, src, got, stage, sem
+
+    def start(self):
+        at = self.at
+
+        def far(i):
+            z_to = at.zs(i)
+            remote(
+                self.src.at[z_to, 1 - at.y],
+                self.got.at[z_to],
+                self.sem.at[0, i],
+                self.sem.at[1, i],
+                at.flip(),
+            ).start()
+
+        each(0, at.F, far)
+
+    def reduce(self):
+        at = self.at
+
+        def far(i):
+            z_to = at.zs(i)
+            await_bytes(self.got.at[0], self.sem.at[0, i])
+            await_bytes(self.got.at[0], self.sem.at[1, i])
+            total = self.src[z_to, at.y].astype(F32) + self.got[z_to].astype(F32)
+            self.stage[z_to] = total.astype(BF)
+
+        each(0, at.F, far)
+
+
+class Line:
+    def line_up(self):
+        at = self.at
+        self.line = at.F == 4
+        self.inner = self.line & ((at.z == 1) | (at.z == 2))
+        self.end = self.line & ((at.z == 0) | (at.z == 3))
+        self.opposite = jnp.where(at.z < 2, 3, 0)
+        self.beside = jnp.where(at.z == 0, 1, 2)
+
+
+class RowOwner(Line):
+    def __init__(self, at, stage, inn, done, far, sem):
+        self.at, self.stage, self.inn, self.done, self.far, self.sem = at, stage, inn, done, far, sem
+        self.line_up()
+
+    @staticmethod
+    def scratch(F, shape):
+        return [pltpu.VMEM(shape, BF), pltpu.VMEM(shape[1:], BF), DMA((5, F))]
+
+    def out_copy(self, z_to):
+        at = self.at
+        return remote(
+            self.stage.at[z_to],
+            self.inn.at[at.z],
+            self.sem.at[0, z_to],
+            self.sem.at[1, at.z],
+            {"fsdp": z_to},
+        )
+
+    def far_copy(self):
+        return remote(
+            self.stage.at[self.opposite],
+            self.far,
+            self.sem.at[0, self.opposite],
+            self.sem.at[4, 0],
+            {"fsdp": self.beside},
+        )
+
+    def start(self):
+        at = self.at
+
+        @pl.when(self.end)
+        def _():
+            self.far_copy().start()
+            self.inn[self.opposite] = jnp.zeros_like(self.far)
+
+        def one(i):
+            z_to = at.zs(i)
+
+            @pl.when(jnp.logical_not(self.line & (z_to == self.opposite)))
+            def _():
+                self.out_copy(z_to).start()
+
+        each(1, at.F, one)
+        self.inn[at.z] = self.stage[at.z]
+
+    def relay(self):
+        @pl.when(self.inner)
+        def _():
+            await_bytes(self.far, self.sem.at[4, 0])
+            z_to = self.opposite
+            both = self.stage[z_to].astype(F32) + self.far[...].astype(F32)
+            self.stage[z_to] = both.astype(BF)
+            self.out_copy(z_to).start()
+
+    def total(self):
+        at = self.at
+
+        def arrived(i):
+            z = at.zs(i)
+            await_bytes(self.far, self.sem.at[0, z])
+
+            @pl.when(jnp.logical_not(self.end & (z == self.opposite)))
+            def _():
+                await_bytes(self.far, self.sem.at[1, z])
+
+        each(1, at.F, arrived)
+        total = self.inn[0].astype(F32)
+        for f in range(1, at.F):
+            total = total + self.inn[f].astype(F32)
+        self.done[at.y] = total.astype(BF)
+        half = self.done.at[at.y]
+        remote(half, half, self.sem.at[2, 0], self.sem.at[3, 0], at.flip()).start()
+
+    def finish(self):
+        await_bytes(self.done.at[0], self.sem.at[2, 0])
+        await_bytes(self.done.at[0], self.sem.at[3, 0])
+
+
+class FullScatter:
+    def __init__(self, at, src, near, got, stage, inn, other, done, sem):
+        self.at, self.src, self.near, self.got, self.stage = at, src, near, got, stage
+        self.inn, self.other, self.done, self.sem = inn, other, done, sem
+
+    @staticmethod
+    def scratch(sizes, rows, cols):
+        R, F, S = sizes
+        return [
+            pltpu.VMEM((S // 2, F, rows, cols), BF),
+            pltpu.VMEM((S // 2, F, rows, cols), BF),
+            pltpu.VMEM((F, rows, cols), BF),
+            pltpu.VMEM((F, rows, cols), BF),
+            pltpu.VMEM((F, rows, cols), BF),
+            DMA((10, max(F, S))),
+        ]
+
+    def sibling(self, j):
+        at = self.at
+        return remote(
+            self.src.at[at.peer(j)],
+            self.near.at[j // 2],
+            self.sem.at[0, j],
+            self.sem.at[1, j],
+            {"seq": at.peer(1)},
+        )
+
+    def direct(self, j):
+        at = self.at
+        return remote(
+            self.near.at[j // 2],
+            self.got.at[j // 2],
+            self.sem.at[2, j],
+            self.sem.at[3, j],
+            {"seq": at.peer(j)},
+        )
+
+    def start(self):
+        for j in range(3, self.at.S, 2):
+            self.sibling(j).start()
+        self.sibling(1).start()
+
+    def cross(self):
+        at = self.at
+        for j in range(2, at.S, 2):
+            self.sibling(j + 1).wait()
+            k = j // 2
+
+            def add(f):
+                both = self.near[k, f].astype(F32) + self.src[at.peer(j), f].astype(F32)
+                self.near[k, f] = both.astype(BF)
+
+            each(0, at.F, add)
+            self.direct(j).start()
+        self.sibling(1).wait()
+
+    def out_copy(self, i):
+        at = self.at
+        return remote(
+            self.stage.at[at.zs(i)],
+            self.inn.at[at.z],
+            self.sem.at[4, i],
+            self.sem.at[5, i],
+            {"fsdp": at.zs(i)},
+        )
+
+    def scatter(self):
+        at = self.at
+        for j in range(2, at.S, 2):
+            self.direct(j).wait()
+
+        def far(i):
+            z_to = at.zs(i)
+            total = self.src[at.s, z_to].astype(F32) + self.near[0, z_to].astype(F32)
+            for k in range(1, at.S // 2):
+                total = total + self.got[k, z_to].astype(F32)
+            self.stage[z_to] = total.astype(BF)
+
+        each(0, at.F, far)
+
+        @pl.when(jnp.logical_not(at.mine))
+        def _():
+            self.swap_copy().start()
+
+    def swap_copy(self):
+        return remote(self.stage, self.other, self.sem.at[6, 0], self.sem.at[7, 0], self.at.flip())
+
+    def along(self):
+        at = self.at
+
+        @pl.when(at.mine)
+        def _():
+            await_bytes(self.other, self.sem.at[7, 0])
+
+            def one(i):
+                z_to = at.zs(i)
+                both = self.stage[z_to].astype(F32) + self.other[z_to].astype(F32)
+                self.stage[z_to] = both.astype(BF)
+
+                @pl.when(i > 0)
+                def _():
+                    self.out_copy(i).start()
+
+            each(0, at.F, one)
+            self.inn[at.z] = self.stage[at.z]
+
+        @pl.when(jnp.logical_not(at.mine))
+        def _():
+            await_bytes(self.other, self.sem.at[6, 0])
+
+    def total(self):
+        at = self.at
+
+        @pl.when(at.mine)
+        def _():
+            each(1, at.F, lambda i: self.out_copy(i).wait())
+            total = self.inn[0].astype(F32)
+            for f in range(1, at.F):
+                total = total + self.inn[f].astype(F32)
+            self.done[...] = total.astype(BF)
+            remote(
+                self.done, self.done, self.sem.at[8, 0], self.sem.at[9, 0], at.flip()
+            ).start()
+
+    def finish(self):
+        at = self.at
+
+        @pl.when(at.mine)
+        def _():
+            await_bytes(self.done, self.sem.at[8, 0])
+
+        @pl.when(jnp.logical_not(at.mine))
+        def _():
+            await_bytes(self.done, self.sem.at[9, 0])
+
+
+def mlp_kernel(sizes, *refs):
     at = Place(sizes)
-    S = at.S
-    L, D = mixed_two.shape
+    R, F, S, G = at.R, at.F, at.S, at.G
+    mod, bias_one, bias_two = refs[:3]
+    given = refs[3:12]
+    block_out, o_resid, o_heads, o_w_one, o_two_sum, o_out_g = refs[12:18]
+    grad_b_one, grad_b_two, grad_b_out, mod_sums = refs[18:22]
+    act_all, pre_wide, pre_all, grad_branch, wide, two_g, two_got, two_sem = refs[22:30]
+    branch_refs, mix_refs = refs[30:34], refs[34:38]
+    load_sem, save_sem = refs[38:40]
+    held = refs[40:49]
+    w_one, mix_all, w_two, grad_all, latents, branch_one, cotangent, w_out, merged = held
+    grad_resid, grad_heads, grad_w_one, two_sum, out_g = refs[49:54]
+    loads = Moves(load_sem, *zip(given, held))
+    loads.start()
+    saves = Moves(
+        save_sem,
+        (grad_w_one, o_w_one),
+        (grad_resid, o_resid),
+        (grad_heads, o_heads),
+        (out_g, o_out_g),
+        (two_sum, o_two_sum),
+    )
+    _, L, D = mix_all.shape
     C = D // S
     hidden = w_one.shape[1]
-    greet_wait(greet(S, lambda i: {"seq": at.ss(i)}))
+    tokens = S * L
+    greet(S, lambda i: {"seq": at.ss(i)})
+    greet(2, lambda i: at.flip())
+    greet_wait(S)
     gate_one = mod[2:3, :]
     scale = mod[4:5, :]
     gate_two = mod[5:6, :]
-
-    mixed_gather = SeqGather(at, mix_all, mixed_sem)
     branch_sum = SeqSum(at, *branch_refs)
     mix_sum = SeqSum(at, *mix_refs)
     branch_src = branch_refs[0]
     mix_src = mix_refs[0]
-    mix_all[at.s] = mixed_two[...]
-    mixed_gather.start()
-
-    def block(index):
-        mixed_gather.arrive(index)
+    two = RowScatter(at, two_g, two_got, two_sum, two_sem)
+    step = min(128, L)
+
+    def ahead(order):
+        index = lax.rem(order + 2, S)
         t = at.peer(arrival(index))
-        step = min(128, L)
 
         def part(i):
             rows = pl.ds(pl.multiple_of(i * step, step), step)
             pre = mm(mix_all[t, rows, :], w_one[...]) + bias_one[...]
+            pre_wide[t, rows, :] = pre
+            inner = gelu_coef * (pre + 0.044715 * pre * pre * pre)
+            act = (0.5 * pre * (1.0 + jnp.tanh(inner))).astype(BF)
+            act_all[t, rows, :] = act
+            branch_src[t, rows, :] = mm(act, w_two[...]).astype(BF)
+
+        each(0, L // step, part)
+        branch_sum.send(index)
+
+    loads.wait(0, 1, 2)
+    each(0, S, ahead)
+    loads.wait(3)
+    column = 384 if hidden % 384 == 0 else hidden
+    for i in range(hidden // column):
+        cols = slice(i * column, (i + 1) * column)
+        wide[cols, :] = mm_tn(
+            act_all[:, :, cols].reshape(tokens, column), grad_all[...].reshape(tokens, D)
+        )
+    part_rows = two_g.shape[2]
+    for f in range(F):
+        for half in range(2):
+            first = (2 * f + half) * part_rows
+            two_g[f, half] = wide[first : first + part_rows, :].astype(BF)
+    two.start()
+
+    def behind(order):
+        index = lax.rem(order + 2, S)
+        t = at.peer(arrival(index))
+
+        def part(i):
+            rows = pl.ds(pl.multiple_of(i * step, step), step)
+            pre = pre_wide[t, rows, :]
             square = pre * pre
-            inner = gelu_coef * (pre + 0.044715 * square * pre)
-            tanh_val = jnp.tanh(inner)
-            half = 0.5 * (1.0 + tanh_val)
-            act = (pre * half).astype(BF)
-            act_all[t, rows, :] = act
-            slope = half + 0.5 * pre * (1.0 - tanh_val * tanh_val) * gelu_coef * (
-                1.0 + 3.0 * 0.044715 * square
-            )
+            tanh_val = jnp.tanh(gelu_coef * (pre + 0.044715 * square * pre))
+            slope = 0.5 * (1.0 + tanh_val) + 0.5 * pre * (
+                1.0 - tanh_val * tanh_val
+            ) * gelu_coef * (1.0 + 3.0 * 0.044715 * square)
             grad_pre = (mm_nt(grad_all[t, rows, :], w_two[...]) * slope).astype(BF)
             pre_all[t, rows, :] = grad_pre
             mix_src[t, rows, :] = mm_nt(grad_pre, w_one[...]).astype(BF)
-            branch_src[t, rows, :] = mm(act, w_two[...]).astype(BF)
 
         each(0, L // step, part)
-
         mix_sum.send(index)
-        branch_sum.send(index)
-
-    each(0, S, block)
-
-    step = 128 if hidden % 128 == 0 else hidden
-    for i in range(hidden // step):
-        cols = slice(i * step, (i + 1) * step)
-        grads = pre_all[:, :, cols].reshape(S * L, step)
+
+    each(0, S, behind)
+    for i in range(hidden // column):
+        cols = slice(i * column, (i + 1) * column)
+        grads = pre_all[:, :, cols].reshape(tokens, column)
+        grad_w_one[:, cols] = mm_tn(mix_all[...].reshape(tokens, D), grads).astype(BF)
         grad_b_one[:, cols] = jnp.sum(grads.astype(F32), axis=0, keepdims=True)
-    wide = 384 if hidden % 384 == 0 else hidden
-    for i in range(hidden // wide):
-        cols = slice(i * wide, (i + 1) * wide)
-        grad_w_one[:, cols] = mm_tn(
-            mix_all[...].reshape(S * L, D), pre_all[:, :, cols].reshape(S * L, wide)
-        ).astype(BF)
-        grad_w_two[cols, :] = mm_tn(
-            act_all[:, :, cols].reshape(S * L, wide), grad_all[...].reshape(S * L, D)
-        ).astype(BF)
     grad_b_two[...] = jnp.sum(grad_all[at.s].astype(F32), axis=0, keepdims=True)
+    saves.start(0)
+    loads.wait(4, 5, 6, 7, 8)
 
     mix_sum.wait()
-    step = min(32, L)
+    step_back = min(32, L)
     mod_sums[...] = jnp.zeros_like(mod_sums)
     grad_b_out[...] = jnp.zeros_like(grad_b_out)
 
     def back(i):
-        rows = pl.ds(pl.multiple_of(i * step, step), step)
+        rows = pl.ds(pl.multiple_of(i * step_back, step_back), step_back)
         grad_mixed = mix_sum.total(rows)
         branch = branch_one[rows, :]
         residual = latents[rows, :].astype(F32) + gate_one * branch
@@ -803,69 +1174,89 @@
         mod_sums[4:5, :] += jnp.sum(grad_mixed * normed, axis=0, keepdims=True)
         grad_b_out[...] += jnp.sum(low.astype(F32), axis=0, keepdims=True)
 
-    each(0, L // step, back)
+    each(0, L // step_back, back)
     grad_merged = mm_nt(grad_branch[...], w_out[...]).astype(BF)
     for t in range(S):
         grad_heads[t] = grad_merged[:, t * C : (t + 1) * C]
-    wide = 384
-    for i in range(D // wide):
-        cols = slice(i * wide, (i + 1) * wide)
-        grad_w_out[:, cols] = mm_tn(merged[...], grad_branch[:, cols]).astype(BF)
+    saves.start(1, 2)
+    for i in range(D // 384):
+        cols = slice(i * 384, (i + 1) * 384)
+        wide[:D, cols] = mm_tn(merged[...], grad_branch[:, cols])
+    rows_own = out_g.shape[2]
+    for f in range(F):
+        for t in range(S):
+            first = (f * S + t) * rows_own
+            out_g[t, f] = wide[first : first + rows_own, :].astype(BF)
+    saves.start(3)
 
     branch_sum.wait()
 
     def finish(i):
-        rows = pl.ds(pl.multiple_of(i * step, step), step)
+        rows = pl.ds(pl.multiple_of(i * step_back, step_back), step_back)
         branch_two = branch_sum.total(rows) + bias_two[...]
         residual = latents[rows, :].astype(F32) + gate_one * branch_one[rows, :]
         block_out[rows, :] = (residual + gate_two * branch_two).astype(BF)
         grad_out = cotangent[rows, :].astype(F32)
         mod_sums[5:6, :] += jnp.sum(grad_out * branch_two, axis=0, keepdims=True)
 
-    each(0, L // step, finish)
-
-
-def mlp(sizes, mixed_two, *args):
-    S = sizes[2]
-    L, D = mixed_two.shape
+    each(0, L // step_back, finish)
+    two.reduce()
+    saves.start(4)
+    saves.wait()
+
+
+def mlp(sizes, *args):
+    R, F, S = sizes
+    G = F * S
+    D, hidden = args[3].shape
+    L = args[7].shape[0]
     C = D // S
-    hidden = args[3].shape[1]
+    half = hidden // F // 2
     shape = jax.ShapeDtypeStruct
-    tokens = (S, L, D)
+    kept = (
+        ((L, D), F32),
+        ((S, L, C), BF),
+        ((D, hidden), BF),
+        ((F, half, D), BF),
+        ((S, F, D // G, D), BF),
+    )
     return pl.pallas_call(
         lambda *refs: mlp_kernel(sizes, *refs),
         name="mlp",
-        out_shape=(
-            shape((L, D), BF),
-            shape((L, D), F32),
-            shape((S, L, C), BF),
-            shape((D, hidden), BF),
-            shape((hidden, D), BF),
-            shape((D, D), BF),
+        out_shape=(shape((L, D), BF),)
+        + tuple(shape(*item) for item in kept)
+        + (
             shape((1, hidden), F32),
             shape((1, D), F32),
             shape((1, D), F32),
             shape((6, D), F32),
         ),
-        in_specs=[VM] * 12,
-        out_specs=(VM,) * 10,
+        in_specs=[VM] * 3 + [HB] * 9,
+        out_specs=(VM,) + (HB,) * 5 + (VM,) * 4,
         scratch_shapes=[
-            pltpu.VMEM(tokens, BF),
             pltpu.VMEM((S, L, hidden), BF),
+            pltpu.VMEM((S, L, hidden), F32),
             pltpu.VMEM((S, L, hidden), BF),
             pltpu.VMEM((L, D), BF),
-            SeqGather.scratch(S),
+            pltpu.VMEM((max(hidden, D), D), F32),
+            pltpu.VMEM((F, 2, half, D), BF),
+            pltpu.VMEM((F, half, D), BF),
+            DMA((2, F)),
         ]
         + SeqSum.scratch(S, L, D)
-        + SeqSum.scratch(S, L, D),
+        + SeqSum.scratch(S, L, D)
+        + [DMA((9,)), DMA((5,))]
+        + [pltpu.VMEM(x.shape, x.dtype) for x in args[3:]]
+        + [pltpu.VMEM(*item) for item in kept],
         compiler_params=params(3, 60),
-    )(mixed_two, *args)
-
-
-class ColumnScatter:
-    def __init__(self, at, src, got, stage, inn, done, sem):
+    )(*args)
+
+
+class ColumnScatter(Line):
+    def __init__(self, at, src, got, stage, inn, far, done, sem):
         self.at, self.src, self.got, self.stage = at, src, got, stage
-        self.inn, self.done, self.sem = inn, done, sem
+        self.inn, self.far, self.done, self.sem = inn, far, done, sem
+        self.line_up()
 
     @staticmethod
     def scratch(sizes, rows, cols):
@@ -874,7 +1265,8 @@
             pltpu.VMEM((F, S // 2, rows, cols), BF),
             pltpu.VMEM((F, S // 2, rows, cols), BF),
             pltpu.VMEM((F * S, rows, cols), BF),
-            DMA((7, F)),
+            pltpu.VMEM((S // 2, rows, cols), BF),
+            DMA((8, F)),
         ]
 
     def start(self):
@@ -889,8 +1281,8 @@
                 remote(
                     self.src.at[z_to * at.S + 2 * k + 1 - at.y],
                     self.got.at[z_to, k],
-                    self.sem.at[0, i],
-                    self.sem.at[1, i],
+                    self.sem.at[0, z_to],
+                    self.sem.at[1, z_to],
                     at.flip(),
                 ).start()
 
@@ -898,47 +1290,90 @@
 
         each(0, at.F, far)
 
+    def send(self, z_to, k):
+        at = self.at
+        s_to = 2 * k + at.y
+        home = (z_to == at.z) & (s_to == at.s)
+
+        @pl.when(home)
+        def _():
+            self.inn[at.me] = self.stage[z_to, k]
+
+        @pl.when(jnp.logical_not(home))
+        def _():
+            remote(
+                self.stage.at[z_to, k],
+                self.inn.at[at.me],
+                self.sem.at[2, z_to],
+                self.sem.at[3, 0],
+                {"fsdp": z_to, "seq": s_to},
+            ).start()
+
     def scatter(self):
         at = self.at
 
-        def far(index):
-            i = lax.rem(index + 1, at.F)
+        def step(index):
+            i = lax.rem(index + 2, at.F)
             z_to = at.zs(i)
-            await_bytes(self.got.at[0], self.sem.at[1, i])
+            await_bytes(self.got.at[0], self.sem.at[1, z_to])
             await_bytes(self.got.at[0], self.sem.at[6, i])
 
             def one(k):
-                s_to = 2 * k + at.y
                 total = self.stage[z_to, k].astype(F32) + self.got[z_to, k].astype(F32)
-                low = total.astype(BF)
-                home = (i == 0) & (s_to == at.s)
-                self.stage[z_to, k] = low
-
-                @pl.when(home)
+                self.stage[z_to, k] = total.astype(BF)
+
+                @pl.when(jnp.logical_not(self.line & (z_to == self.opposite)))
                 def _():
-                    self.inn[at.me] = low
-
-                @pl.when(jnp.logical_not(home))
-                def _():
-                    remote(
-                        self.stage.at[z_to, k],
-                        self.inn.at[at.me],
-                        self.sem.at[2, i],
-                        self.sem.at[3, 0],
-                        {"fsdp": z_to, "seq": s_to},
-                    ).start()
+                    self.send(z_to, k)
 
             each(0, at.S // 2, one)
 
-        each(0, at.F, far)
+            @pl.when(self.end & (z_to == self.opposite))
+            def _():
+                remote(
+                    self.stage.at[z_to],
+                    self.far,
+                    self.sem.at[2, z_to],
+                    self.sem.at[7, 0],
+                    {"fsdp": self.beside},
+                ).start()
+
+        each(0, at.F, step)
+
+    def relay(self):
+        at = self.at
+
+        @pl.when(self.inner)
+        def _():
+            await_bytes(self.far, self.sem.at[7, 0])
+            z_to = self.opposite
+
+            def one(k):
+                total = self.stage[z_to, k].astype(F32) + self.far[k].astype(F32)
+                self.stage[z_to, k] = total.astype(BF)
+                self.send(z_to, k)
+
+            each(0, at.S // 2, one)
 
     def total(self):
         at = self.at
 
+        @pl.when(at.mine & self.end)
+        def _():
+            await_bytes(self.inn.at[pl.ds(0, max(1, at.G - 1 - at.S))], self.sem.at[3, 0])
+
+            def clear(t):
+                slot = self.opposite * at.S + t
+                self.inn[slot] = jnp.zeros_like(self.done[0])
+
+            each(0, at.S, clear)
+
+        @pl.when(at.mine & jnp.logical_not(self.end))
+        def _():
+            await_bytes(self.inn.at[pl.ds(0, at.G - 1)], self.sem.at[3, 0])
+
         @pl.when(at.mine)
         def _():
-            await_bytes(self.inn.at[pl.ds(0, at.G - 1)], self.sem.at[3, 0])
-
             def one(t):
                 total = self.inn[t].astype(F32)
                 for f in range(1, at.F):
@@ -953,177 +1388,19 @@
     def finish(self):
         at = self.at
         half = self.got.at[0]
-        each(0, at.F, lambda i: await_bytes(half, self.sem.at[0, i]))
-        each(1, at.F, lambda i: await_bytes(half, self.sem.at[2, i]))
+        each(0, at.F, lambda z: await_bytes(half, self.sem.at[0, z]))
+        each(1, at.F, lambda i: await_bytes(half, self.sem.at[2, at.zs(i)]))
 
         @pl.when(at.mine)
         def _():
             if at.S > 2:
-                await_bytes(self.got.at[0, pl.ds(0, at.S // 2 - 1)], self.sem.at[2, 0])
+                await_bytes(self.got.at[0, pl.ds(0, at.S // 2 - 1)], self.sem.at[2, at.z])
             await_bytes(self.done, self.sem.at[4, 0])
 
         @pl.when(jnp.logical_not(at.mine))
         def _():
-            await_bytes(half, self.sem.at[2, 0])
+            await_bytes(half, self.sem.at[2, at.z])
             await_bytes(self.done, self.sem.at[5, 0])
-
-
-class RowScatter:
-    def __init__(self, at, src, got, stage, inn, done, sem):
-        self.at, self.src, self.got, self.stage = at, src, got, stage
-        self.inn, self.done, self.sem = inn, done, sem
-
-    @staticmethod
-    def scratch(sizes, rows, cols):
-        R, F, S = sizes
-        return [
-            pltpu.VMEM((F, rows, cols), BF),
-            pltpu.VMEM((F, rows, cols), BF),
-            pltpu.VMEM((F, rows, cols), BF),
-            DMA((7, F)),
-        ]
-
-    def start(self):
-        at = self.at
-
-        def far(i):
-            z_to = at.zs(i)
-            local(self.src.at[z_to, at.y], self.stage.at[z_to], self.sem.at[6, i]).start()
-            remote(
-                self.src.at[z_to, 1 - at.y],
-                self.got.at[z_to],
-                self.sem.at[0, i],
-                self.sem.at[1, i],
-                at.flip(),
-            ).start()
-
-        each(0, at.F, far)
-
-    def out_copy(self, i):
-        at = self.at
-        return remote(
-            self.stage.at[at.zs(i)],
-            self.inn.at[at.z],
-            self.sem.at[2, i],
-            self.sem.at[3, i],
-            {"fsdp": at.zs(i)},
-        )
-
-    def scatter(self):
-        at = self.at
-
-        def far(index):
-            i = lax.rem(index + 1, at.F)
-            z_to = at.zs(i)
-            await_bytes(self.got.at[0], self.sem.at[1, i])
-            await_bytes(self.got.at[0], self.sem.at[6, i])
-            total = self.stage[z_to].astype(F32) + self.got[z_to].astype(F32)
-            self.stage[z_to] = total.astype(BF)
-
-            @pl.when(i > 0)
-            def _():
-                self.out_copy(i).start()
-
-        each(0, at.F, far)
-
-    def total(self):
-        at = self.at
-        self.inn[at.z] = self.stage[at.z]
-        each(1, at.F, lambda i: self.out_copy(i).wait())
-        total = self.inn[0].astype(F32)
-        for f in range(1, at.F):
-            total = total + self.inn[f].astype(F32)
-        self.done[at.y] = total.astype(BF)
-        half = self.done.at[at.y]
-        remote(half, half, self.sem.at[4, 0], self.sem.at[5, 0], at.flip()).start()
-
-    def finish(self):
-        at = self.at
-        each(0, at.F, lambda i: await_bytes(self.got.at[0], self.sem.at[0, i]))
-        await_bytes(self.done.at[0], self.sem.at[4, 0])
-        await_bytes(self.done.at[0], self.sem.at[5, 0])
-
-
-class FullScatter:
-    def __init__(self, at, src, got, stage, inn, swap, sem):
-        self.at, self.src, self.got, self.stage = at, src, got, stage
-        self.inn, self.swap, self.sem = inn, swap, sem
-
-    @staticmethod
-    def scratch(sizes, rows, cols):
-        R, F, S = sizes
-        return [
-            pltpu.VMEM((S, F, rows, cols), BF),
-            pltpu.VMEM((F, rows, cols), BF),
-            pltpu.VMEM((F, rows, cols), BF),
-            DMA((6, max(F, S))),
-        ]
-
-    def start(self):
-        at = self.at
-
-        def near(j):
-            def one(f):
-                remote(
-                    self.src.at[f, at.ss(j)],
-                    self.got.at[j, f],
-                    self.sem.at[0, j],
-                    self.sem.at[1, j],
-                    {"seq": at.ss(j)},
-                ).start()
-
-            each(0, at.F, one)
-
-        each(1, at.S, near)
-        local(self.src.at[:, at.s], self.stage, self.sem.at[0, 0]).start()
-
-    def out_copy(self, i):
-        at = self.at
-        return remote(
-            self.stage.at[at.zs(i)],
-            self.inn.at[at.z],
-            self.sem.at[2, i],
-            self.sem.at[3, i],
-            {"fsdp": at.zs(i)},
-        )
-
-    def scatter(self):
-        at = self.at
-
-        def arrived(j):
-            await_bytes(self.got.at[0], self.sem.at[0, j])
-            await_bytes(self.got.at[0], self.sem.at[1, j])
-
-        each(1, at.S, arrived)
-        local(self.src.at[:, at.s], self.stage, self.sem.at[0, 0]).wait()
-
-        def far(i):
-            z_to = at.zs(i)
-            total = self.stage[z_to].astype(F32)
-            for j in range(1, at.S):
-                total = total + self.got[j, z_to].astype(F32)
-            self.stage[z_to] = total.astype(BF)
-
-            @pl.when(i > 0)
-            def _():
-                self.out_copy(i).start()
-
-        each(0, at.F, far)
-
-    def total(self):
-        at = self.at
-        self.inn[at.z] = self.stage[at.z]
-        each(1, at.F, lambda i: self.out_copy(i).wait())
-        total = self.inn[0].astype(F32)
-        for f in range(1, at.F):
-            total = total + self.inn[f].astype(F32)
-        self.swap[at.y] = total.astype(BF)
-        mine = self.swap.at[at.y]
-        remote(mine, mine, self.sem.at[4, 0], self.sem.at[5, 0], at.flip()).start()
-
-    def finish(self):
-        await_bytes(self.swap.at[0], self.sem.at[4, 0])
-        await_bytes(self.swap.at[0], self.sem.at[5, 0])
 
 
 class Tail:
@@ -1268,20 +1545,25 @@
 def backward_kernel(sizes, *refs):
     at = Place(sizes)
     R, F, S, G = at.R, at.F, at.S, at.G
-    grad_heads, heads, log_sums, mixed_all, w_qkv, latents, mod, grad_resid, sums_in = refs[:9]
-    one_g, two_g, out_g, b_one, b_two, b_out, w_ada, cond = refs[9:17]
+    grad_heads, heads, two_g, out_g, w_qkv, mixed_all, latents, grad_resid, w_ada = refs[-9:]
+    log_sums, mod, sums_in, b_one, b_two, b_out, cond, one_g = refs[:8]
+    given = refs[8:17]
     grad_latents, o_qkv, o_one, o_two, o_out, o_mod, o_small, o_cond = refs[17:25]
     grad_in, key_flip, key_grad, val_grad, grad_proj, qkv_wide, qkv_g, mod_sums, b_qkv, in_sem = refs[25:35]
     rest = list(refs[35:])
     mix_sum = SeqSum(at, *rest[0:4])
     mix_src = rest[0]
-    qkv = ColumnScatter(at, qkv_g, *rest[4:7], o_qkv, rest[7])
-    one = ColumnScatter(at, one_g, *rest[8:11], o_one, rest[11])
-    two = RowScatter(at, two_g, *rest[12:15], o_two, rest[15])
-    out = FullScatter(at, out_g, *rest[16:19], o_out, rest[19])
-    tail = Tail(at, o_mod, *rest[20:29])
+    qkv = ColumnScatter(at, qkv_g, *rest[4:8], o_qkv, rest[8])
+    one = ColumnScatter(at, one_g, *rest[9:13], o_one, rest[13])
+    two = RowOwner(at, two_g, rest[14], o_two, rest[15], rest[16])
+    out = FullScatter(at, out_g, *rest[17:22], o_out, rest[22])
+    tail = Tail(at, o_mod, *rest[23:32])
+    load_sem = rest[32]
+    held = rest[33:42]
+    loads = Moves(load_sem, *zip(given, held))
+    loads.start()
     _, L, C = grad_heads.shape
-    rows_own, D = o_out.shape[1:]
+    rows_own, D = o_out.shape
     hidden = one_g.shape[2]
     local_heads = H // S
     size = D // H
@@ -1298,10 +1580,12 @@
             {"seq": at.peer(j)},
         )
 
+    loads.wait(0)
     each(1, S, lambda j: in_copy(j).start())
+    one.start()
+    loads.wait(1, 2, 3)
     two.start()
     out.start()
-    one.start()
     grad_in[at.s] = grad_heads[at.s]
     for h in range(local_heads):
         key_flip[h] = heads[local_heads + h].T
@@ -1332,29 +1616,34 @@
             key_grad[h] += mm(grad_scores, query)
             val_grad[h] += mm(probs.astype(BF), grad)
 
-    each(0, S, block)
+    block(0)
+    out.cross()
+    each(1, S, block)
+    two.relay()
     for h in range(local_heads):
         low = (key_grad[h] * score_scale)[:, :size].astype(BF)
         grad_proj[:, :, C + h * size : C + (h + 1) * size] = low.reshape(S, L, size)
         low = val_grad[h][:, :size].astype(BF)
         grad_proj[:, :, 2 * C + h * size : 2 * C + (h + 1) * size] = low.reshape(S, L, size)
 
+    loads.wait(4, 5)
+
     def spread(index):
         t = at.peer(arrival(index))
         mix_src[t] = mm_nt(grad_proj[t], w_qkv[...]).astype(BF)
         mix_sum.send(index)
 
     each(0, S, lambda index: spread(lax.rem(index + 2, S)))
+    one.scatter()
+    out.scatter()
     grads = grad_proj[...].reshape(S * L, 3 * C)
     qkv_wide[...] = mm_tn(mixed_all[...].reshape(S * L, D), grads)
     for g in range(G):
         qkv_g[g] = qkv_wide[g * rows_own : (g + 1) * rows_own, :].astype(BF)
     qkv.start()
     b_qkv[...] = jnp.sum(grads.astype(F32), axis=0, keepdims=True)
-
-    two.scatter()
-    out.scatter()
     mix_sum.wait()
+    loads.wait(6, 7, 8)
     step = min(32, L)
     mod_sums[...] = sums_in[...]
     scale = mod[1:2, :]
@@ -1371,13 +1660,15 @@
 
     each(0, L // step, back)
     tail.start(mod_sums, b_one, b_two, b_out, b_qkv)
-    one.scatter()
+    out.along()
+    one.relay()
+    two.total()
     tail.middle(D, hidden, rows_own)
+    qkv.scatter()
     out.total()
-    two.total()
+    one.total()
+    qkv.relay()
     tail.owners(w_ada, o_small)
-    qkv.scatter()
-    one.total()
     tail.finish(cond, o_cond)
     qkv.total()
     out.finish()
@@ -1389,8 +1680,8 @@
 def backward(sizes, *args):
     R, F, S = sizes
     G = F * S
-    grad_heads, latents = args[0], args[5]
-    one_g, two_g, w_ada = args[9], args[10], args[15]
+    one_g, grad_heads, two_g = args[7], args[8], args[10]
+    latents, w_ada = args[14], args[16]
     _, L, C = grad_heads.shape
     D = latents.shape[1]
     T = S * L
@@ -1406,13 +1697,13 @@
             shape((L, D), F32),
             shape((S, rows, 3 * C), BF),
             shape((S, rows, hidden), BF),
-            shape(two_g.shape[1:], BF),
-            shape((2, rows, D), BF),
+            shape((2,) + two_g.shape[1:], BF),
+            shape((rows, D), BF),
             shape((R * F, 6, D), BF),
             shape((1, pack), F32),
             shape((1, D), F32),
         ),
-        in_specs=[VM] * 9 + [HB] * 3 + [VM] * 5,
+        in_specs=[VM] * 7 + [HB] * 10,
         out_specs=(VM,) * 8,
         scratch_shapes=[
             pltpu.VMEM((S, L, C), BF),
@@ -1429,9 +1720,11 @@
         + SeqSum.scratch(S, L, D)
         + ColumnScatter.scratch(sizes, rows, 3 * C)
         + ColumnScatter.scratch(sizes, rows, hidden)
-        + RowScatter.scratch(sizes, two_g.shape[2], D)
+        + RowOwner.scratch(F, two_g.shape)
         + FullScatter.scratch(sizes, rows, D)
-        + Tail.scratch(sizes, D, hidden, rows),
+        + Tail.scratch(sizes, D, hidden, rows)
+        + [DMA((9,))]
+        + [pltpu.VMEM(x.shape, x.dtype) for x in args[8:]],
         compiler_params=params(4, 60),
     )(*args)
 
@@ -1442,7 +1735,7 @@
     D = o_out.shape[1]
     C = D // S
     hidden = one.shape[2]
-    o_out[...] = out[0].astype(F32) + out[1].astype(F32)
+    o_out[...] = out[...].astype(F32)
     for p in range(2):
         o_two[p] = two[p].astype(F32)
     block = hidden // F
@@ -1466,7 +1759,7 @@
 def assemble(sizes, qkv, one, two, out, mod_all, silu_all):
     R, F, S = sizes
     G = F * S
-    rows, D = out.shape[1:]
+    rows, D = out.shape
     shape = jax.ShapeDtypeStruct
     return pl.pallas_call(
         lambda *refs: assemble_kernel(sizes, *refs),
@@ -1506,15 +1799,15 @@
     (
         mixed_all,
         heads,
-        log_sums,
         merged,
         branch_one,
-        mixed_two,
-        mod,
-        silu_all,
+        mix_all,
         grad_all,
         full_qkv,
         full_out,
+        log_sums,
+        mod,
+        silu_all,
         bias_one,
         bias_two,
         g_one,
@@ -1522,13 +1815,13 @@
     ) = forward(
         sizes,
         cond,
-        w_ada,
         bias_slot,
+        bias_pack,
         tokens,
         cotangent[0],
+        w_ada,
         w_qkv,
         w_one,
-        bias_pack,
         w_two.reshape(2, two_rows // 2, D),
         w_out,
     )
@@ -1547,38 +1840,38 @@
         mod_sums,
     ) = mlp(
         sizes,
-        mixed_two,
+        mod,
+        bias_one,
+        bias_two,
+        full_one,
+        mix_all,
+        full_two,
         grad_all,
+        tokens,
+        branch_one,
         cotangent[0],
-        mod,
-        full_one,
-        bias_one,
-        full_two,
-        bias_two,
-        branch_one,
-        tokens,
         full_out,
         merged,
     )
     grad_latents, qkv_sum, one_sum, two_sum, out_sum, mod_all, o_small, o_cond = backward(
         sizes,
-        grad_heads,
-        heads,
         log_sums,
-        mixed_all,
-        full_qkv,
-        tokens,
         mod,
-        grad_resid,
         mod_sums,
-        one_g.reshape(G, rows, hidden),
-        two_g.reshape(F, 2, two_rows // 2, D),
-        out_g.reshape(F, S, rows, D),
         grad_b_one,
         grad_b_two,
         grad_b_out,
+        cond,
+        one_g.reshape(G, rows, hidden),
+        grad_heads,
+        heads,
+        two_g,
+        out_g,
+        full_qkv,
+        mixed_all,
+        tokens,
+        grad_resid,
         w_ada,
-        cond,
     )
     o_qkv, o_one, o_two, o_out, o_ada, o_b_ada = assemble(
         sizes, qkv_sum, one_sum, two_sum, out_sum, mod_all, silu_all

time: 396 us -> 294 us (0.74)
  Pallas kernels: 375 us -> 276 us
    pallas_call x1, Pallas kernels: 167 us -> 116 us  [forward(): pl.pallas_call(lambda *refs: forward_kernel(sizes, *refs), name='forward'...]
    pallas_call x1, Pallas kernels: 142 us -> 107 us  [backward(): pl.pallas_call(lambda *refs: backward_kernel(sizes, *refs), name='backwar...]
    pallas_call x1, Pallas kernels: 62.4 us -> 50.1 us  [mlp(): pl.pallas_call(lambda *refs: mlp_kernel(sizes, *refs), name='mlp', out_sh...]
where the time goes in v3:
time: 294 us; the launch traced here: 293 us
  Pallas kernels  276 us (94%)
  local copies, waits for them, and re-layouts  13.5 us (5%)
    pallas_call x1, Pallas kernels, forward(): pl.pallas_call(lambda *refs: forward_kernel(sizes, *refs), name='forward'...  116 us
    pallas_call x1, Pallas kernels, backward(): pl.pallas_call(lambda *refs: backward_kernel(sizes, *refs), name='backwar...  107 us
    pallas_call x1, Pallas kernels, mlp(): pl.pallas_call(lambda *refs: mlp_kernel(sizes, *refs), name='mlp', out_sh...  50.1 us
    unnamed x23, local copies, waits for them, and re-layouts  8.08 us

profile of v3, /device:TPU:0, one launch (start us, length us, event | category | flops | bytes accessed | tf_op | source)
XLA Modules:
  0.0 292.6 jit_solution(9989827841523731572)
XLA Ops:
  0.7 0.7 concatenate.18
  1.3 0.7 concatenate.21
  2.0 1.3 maximum_convert_fusion.refs_2_
  3.3 0.7 broadcast_in_dim.20
  4.0 0.2 dynamic_update_slice.4.refs_1_
  4.2 0.0 copy-start.8
  4.2 0.6 copy-done.8
  4.8 116.1 %forward.1 = (bf16[4,256,1152]{2,1,0:T(8,128)(2,1)}, bf16[12,1024,128]{2,1,0:T(8,128)(2,1)}, bf16[256,1152]{1,0:T(8,128)(2,1)}, f32[256,1152]{1,0:T(8,128)}, bf1...) custom-call(bf16[1,1152]{1,0:T(2,128)(2,1)} %refs_6_.3, ...), custom_call_target="tpu_custom_call" | custom-call | tf_op jit(solution)/shard_map/forward/pallas_call | solution.py:744
  120.9 50.1 %mlp.1 = (bf16[256,1152]{1,0:T(8,128)(2,1)}, f32[256,1152]{1,0:T(8,128)}, bf16[4,256,288]{2,1,0:T(8,128)(2,1)}, bf16[1152,1152]{1,0:T(8,128)(2,1)}, bf16[4,144,1...) custom-call(f32[6,1152]{1,0:T(8,128)} %get-tuple-element.52.refs_0_., ...), custom_call_target="tpu_custom_call" | custom-call | tf_op jit(solution)/shard_map/mlp/pallas_call | solution.py:1223
  171.0 0.0 copy-start.5
  171.0 0.0 copy-start.7
  171.0 106.9 %backward.1 = (f32[256,1152]{1,0:T(8,128)}, bf16[4,72,864]{2,1,0:T(8,128)(2,1)}, bf16[4,72,1152]{2,1,0:T(8,128)(2,1)}, bf16[2,144,1152]{2,1,0:T(8,128)(2,1)}, bf...) custom-call(f32[4,4,1,256]{3,2,1,0:T(1,128)} %get-tuple-element.63.refs_0_, ...), custom_call_target="tpu_custom_call" | custom-call | tf_op jit(solution)/shard_map/backward/pallas_call | solution.py:1693
  277.9 1.2 slice.24
  279.1 1.3 slice_bitcast_fusion
  280.4 1.3 slice_reduce_fusion
  281.8 0.0 copy-done.5
  281.8 0.0 copy-start
  281.8 1.1 copy-done
  282.9 0.0 copy-start.1
  282.9 1.1 copy-done.1
  283.9 0.0 copy-start.2
  284.0 1.0 copy-done.2
  285.0 0.0 copy-start.3
  285.0 0.9 copy-done.3
  285.9 0.0 copy-start.4
  285.9 0.9 copy-done.4
  286.8 0.0 copy-start.6
  286.8 0.0 copy-start.9
  286.8 3.4 %assemble.1 = (f32[72,3456]{1,0:T(8,128)}, f32[72,4608]{1,0:T(8,128)}, f32[2,144,1152]{2,1,0:T(8,128)}, f32[72,1152]{1,0:T(8,128)}, f32[72,6912]{1,0:T(8,128)}, /*index=5*/f32[1,432]{1,0:T(1,128)}) custom-call(bf16[4,72,864]{2,1,0:T(8,128)(2,1)S(1)} %copy-done.2, bf16[4,72,1152]{2,1,0:T(8,128)(2,1)S(1)} %copy-done, bf16[2,144,1152]{2,1,0:T(8,128)(2,1)S(1)} %copy-done.1, ...), custom_call_target="tpu_custom_call" | custom-call | tf_op jit(solution)/shard_map/assemble/pallas_call | solution.py:1764
  290.2 0.0 copy-done.7
  290.2 0.8 copy.30
  291.0 0.0 copy-done.6
  291.0 1.0 copy.31
  292.0 0.0 copy-done.9
  292.0 0.6 copy.32
  (1 shorter events, 0.0 us)
Async XLA Ops:
  4.2 0.6 copy-start.8
  171.0 110.8 %copy-start.5 = (f32[8,1,72]{2,1,0:T(1,128)S(1)}, f32[8,1,72]{2,1,0:T(1,128)}, u32[]{:S(2)}) copy-start(f32[8,1,72]{2,1,0:T(1,128)} %get-tuple-element.83.refs_5_) | copy-start | bytes 6916
  171.0 119.2 %copy-start.7 = (bf16[256,1152]{1,0:T(8,128)(2,1)S(1)}, bf16[256,1152]{1,0:T(8,128)(2,1)}, u32[]{:S(2)}) copy-start(bf16[256,1152]{1,0:T(8,128)(2,1)} %get-tuple-element.62) | copy-start | bytes 1769476
  281.8 1.1 copy-start
  282.9 1.1 copy-start.1
  283.9 1.0 copy-start.2
  285.0 0.9 copy-start.3
  285.9 0.9 copy-start.4
  286.8 4.2 %copy-start.6 = (f32[256,1152]{1,0:T(8,128)S(1)}, f32[256,1152]{1,0:T(8,128)}, u32[]{:S(2)}) copy-start(f32[256,1152]{1,0:T(8,128)} %get-tuple-element.76) | copy-start | bytes 3538948
  286.8 5.2 %copy-start.9 = (f32[1,1152]{1,0:T(1,128)S(1)}, f32[1,1152]{1,0:T(1,128)}, u32[]{:S(2)}) copy-start(f32[1,1152]{1,0:T(1,128)} %get-tuple-element.108) | copy-start | bytes 13828
